TPU v7x, 512 devices: a whole 4x8x8 slice. The times are simulated.
512 devices in a mesh: sub: 16 (over z_lo, x), reg: 32 (over y, z_hi, core).
Axes of the slice: x: 4, y: 8, z: 8 (z_hi: 2, z_lo: 4; z = z_hi * 4 + z_lo), core: 2. Of those that a mesh axis runs over, the one named last changes fastest.
Arguments:
- port_loads: bfloat16 [32, 16, 384, 512], P('reg', 'sub'), may hold values from -6 to 6
- leaf_inverse: bfloat16 [32, 16, 384, 384], P('reg', 'sub'), may hold values from -3 to 3, as said below
- leaf_coupling: bfloat16 [32, 16, 896, 384], P('reg', 'sub'), may hold values from -0.3125 to 0.3125
- first_inverse: bfloat16 [32, 7168, 896], P('reg', 'sub'), may hold values from -3 to 3, as said below
- second_coupling: bfloat16 [32, 7168, 896], P('reg', 'sub'), may hold values from -0.1875 to 0.1875
- second_inverse: bfloat16 [32, 3584, 896], P('reg', 'sub'), may hold values from -3 to 3, as said below
- border_coupling: bfloat16 [32, 2048, 896], P('reg', 'sub'), may hold values from -0.1875 to 0.1875
- border_inverse: bfloat16 [512, 512], replicated, may hold values from -3 to 3, as said below
- border_rows: int32 [32], P('reg'), may hold values from 128 to 512, as said below
Outputs:
- solution: bfloat16 [32, 16, 384, 512], P('reg', 'sub')
Inputs may be any that keep to these rules, and one draw needn't show every extreme that they name: `leaf_inverse`: every 384 x 384 block is lower triangular. `first_inverse`: every 896 x 896 block is lower triangular. `second_inverse`: every 896 x 896 block is lower triangular. `border_inverse`: lower triangular. `border_rows`: some region touches all 512 rows.
All inputs are finite; a program needn't handle non-finite values.
Results may differ from a plain program's by a relative error of at most 0.013.
Values may be sent and summed in bfloat16 or wider, within the bound.
No kernel may reach another device: no remote copies, remote signals or barrier semaphores. Data moves between devices by JAX's collectives and lax.ppermute only.
A program may use at most 64 MiB of HBM per device.

v0:
```python
import jax
import jax.numpy as jnp
from jax import lax
from jax.sharding import PartitionSpec as P


def swapped(x, axis, bit):
    return lax.ppermute(x, axis, [(i, i ^ 1 << bit) for i in range(lax.axis_size(axis))])


def in_blocks(x, dim, count):
    before, after = (x.shape[:dim], x.shape[dim + 1 :])
    return jnp.moveaxis(x.reshape(*before, count, -1, *after), dim, 0)


def sent_and_summed(x, axis, dim):
    tiles = in_blocks(x, dim, lax.axis_size(axis))
    arrived = lax.all_to_all(tiles, axis, split_axis=0, concat_axis=0, tiled=True)
    return arrived.sum(axis=0)


def from_everyone(x, axis):
    copies = jnp.broadcast_to(x, (lax.axis_size(axis), *x.shape))
    return lax.all_to_all(copies, axis, split_axis=0, concat_axis=0, tiled=True)


def joined_along(tiles, dim):
    dims = list(tiles.shape[1:])
    dims[dim] *= tiles.shape[0]
    return jnp.moveaxis(tiles, 0, dim).reshape(dims)


def gathered_copies(x, axis, dim):
    tiles = from_everyone(x, axis)
    return joined_along(tiles, dim)


def attach(mine, other, mine_first, axis_pos):
    return jnp.where(
        mine_first,
        jnp.concatenate([mine, other], axis_pos),
        jnp.concatenate([other, mine], axis_pos),
    )


def apply_transpose(matrix, vector):
    return lax.dot_general(
        matrix, vector, (((0,), (0,)), ((), ())), preferred_element_type=jnp.float32
    )


def product(matrix, vector):
    return jnp.dot(matrix, vector, preferred_element_type=jnp.float32)


def per_device(
    port_loads,
    leaf_inverse,
    leaf_coupling,
    first_inverse,
    second_coupling,
    second_inverse,
    border_coupling,
    border_inverse,
    border_rows,
):
    sub_index = lax.axis_index("sub")
    first_low = sub_index % 2 == 0
    second_low = sub_index // 2 % 2 == 0
    sub_bits = lax.axis_size("sub").bit_length() - 1
    inv_one = first_inverse[0]
    coup_two = second_coupling[0]
    inv_two = second_inverse[0]
    coup_border = border_coupling[0]
    partner = swapped((inv_one, coup_two, inv_two, coup_border), "sub", 0)
    inv_one = attach(inv_one, partner[0], first_low, 0)
    coup_two = attach(coup_two, partner[1], first_low, 0)
    inv_two = attach(inv_two, partner[2], first_low, 0)
    coup_border = attach(coup_border, partner[3], first_low, 0)
    partner = swapped((inv_two, coup_border), "sub", 1)
    inv_two = attach(inv_two, partner[0], second_low, 0)
    coup_border = attach(coup_border, partner[1], second_low, 0)
    leaf_inv = leaf_inverse[0, 0]
    leaf_coup = leaf_coupling[0, 0]
    fwd_leaf = product(leaf_inv, port_loads[0, 0]).astype(jnp.bfloat16)
    part_one = product(leaf_coup, fwd_leaf)
    col_count = part_one.shape[1]
    half_cols = col_count // 2
    kept_one = jnp.where(first_low, part_one[:, :half_cols], part_one[:, half_cols:])
    sent_one = jnp.where(first_low, part_one[:, half_cols:], part_one[:, :half_cols])
    rhs_one = (-(kept_one + swapped(sent_one, "sub", 0))).astype(jnp.bfloat16)
    fwd_one = product(inv_one, rhs_one).astype(jnp.bfloat16)
    part_two = product(coup_two, fwd_one)
    quarter_cols = half_cols // 2
    kept_two = jnp.where(second_low, part_two[:, :quarter_cols], part_two[:, quarter_cols:])
    sent_two = jnp.where(second_low, part_two[:, quarter_cols:], part_two[:, :quarter_cols])
    rhs_two = (-(kept_two + swapped(sent_two, "sub", 1))).astype(jnp.bfloat16)
    fwd_two = product(inv_two, rhs_two).astype(jnp.bfloat16)
    border_count = coup_border.shape[0]
    row_mask = lax.broadcasted_iota(jnp.int32, (border_count, 1), 0) < border_rows[0]
    part_border = jnp.where(row_mask, product(coup_border, fwd_two), jnp.float32(0.0))
    share_sum = sent_and_summed(part_border, "reg", 0)
    for bit_pos in range(2, sub_bits):
        share_sum = share_sum + swapped(share_sum, "sub", bit_pos)
    rhs_border = gathered_copies((-share_sum).astype(jnp.bfloat16), "reg", 0)
    fwd_border = product(border_inverse, rhs_border).astype(jnp.bfloat16)
    back_border = apply_transpose(border_inverse, fwd_border).astype(jnp.bfloat16)
    masked = jnp.where(row_mask, back_border, jnp.zeros_like(back_border))
    diff_two = (fwd_two.astype(jnp.float32) - apply_transpose(coup_border, masked)).astype(
        jnp.bfloat16
    )
    back_two = apply_transpose(inv_two, diff_two).astype(jnp.bfloat16)
    back_two = attach(back_two, swapped(back_two, "sub", 1), second_low, 1)
    diff_one = (fwd_one.astype(jnp.float32) - apply_transpose(coup_two, back_two)).astype(
        jnp.bfloat16
    )
    back_one = apply_transpose(inv_one, diff_one).astype(jnp.bfloat16)
    back_one = attach(back_one, swapped(back_one, "sub", 0), first_low, 1)
    diff_leaf = (fwd_leaf.astype(jnp.float32) - apply_transpose(leaf_coup, back_one)).astype(
        jnp.bfloat16
    )
    solution = apply_transpose(leaf_inv, diff_leaf).astype(jnp.bfloat16)
    return solution[None, None]


def solution(mesh):
    return jax.shard_map(
        per_device,
        mesh=mesh,
        in_specs=(
            P("reg", "sub", None, None),
            P("reg", "sub", None, None),
            P("reg", "sub", None, None),
            P("reg", "sub", None),
            P("reg", "sub", None),
            P("reg", "sub", None),
            P("reg", "sub", None),
            P(),
            P("reg"),
        ),
        out_specs=P("reg", "sub", None, None),
        check_vma=False,
    )
```

profile of v0, /device:TPU:1, one launch (start us, length us, event | category | flops | bytes accessed | tf_op | source)
XLA Modules:
  0.0 211.2 jit_solution(17179806871546068828)
XLA Ops:
  0.0 1.5 convolution_convert_fusion.3
  1.5 0.0 copy-done
  1.5 0.7 convolution_bitcast_fusion
  2.2 0.0 copy-start.4
  2.3 0.0 copy-start.6
  2.3 1.0 slice_select_fusion
  3.3 3.9 %collective-permute-start.1 = (f32[896,256]{0,1:T(8,128)}, f32[896,256]{0,1:T(8,128)}, u32[]{:S(2)}, u32[]{:S(2)}) collective-permute-start(f32[896,256]{0,1:T(8,128)} %slice_select_fusion), channel_id=1, source_target_pairs={{0,32},{32,0},{64,96},{96,64},{128,160},{160,128},{192,224},{224,1... | collective-permute-start | bytes 2752520 | tf_op jit(solution)/shard_map/ppermute | solution.py:8
  7.2 1.9 collective-permute-start
  9.2 3.4 %collective-permute-start.3 = (bf16[224,896]{1,0:T(8,128)(2,1)S(1)}, bf16[224,896]{1,0:T(8,128)(2,1)}, u32[]{:S(2)}, u32[]{:S(2)}) collective-permute-start(bf16[224,896]{1,0:T(8,128)(2,1)S(1)} %bitcast.45), channel_id=1, source_target_pairs={{0,32},{32,0},{64,96},{96,64},{128,160},{160,128},{192,224},{224,1... | collective-permute-start | bytes 1204232 | tf_op jit(solution)/shard_map/ppermute | solution.py:8
  12.6 1.9 collective-permute-start.2
  14.5 3.4 %collective-permute-start.6 = (bf16[128,896]{1,0:T(8,128)(2,1)S(1)}, bf16[128,896]{1,0:T(8,128)(2,1)}, u32[]{:S(2)}, u32[]{:S(2)}) collective-permute-start(bf16[128,896]{1,0:T(8,128)(2,1)S(1)} %bitcast.48), channel_id=1, source_target_pairs={{0,32},{32,0},{64,96},{96,64},{128,160},{160,128},{192,224},{224,1... | collective-permute-start | bytes 688136 | tf_op jit(solution)/shard_map/ppermute | solution.py:8
  17.9 30.5 %collective-permute-done.3 = bf16[224,896]{1,0:T(8,128)(2,1)} collective-permute-done((bf16[224,896]{1,0:T(8,128)(2,1)S(1)}, bf16[224,896]{1,0:T(8,128)(2,1)}, u32[]{:S(2)}, u32[]{:S(2)}) %collective-permute-start.3) | collective-permute-done | bytes 401440 | tf_op jit(solution)/shard_map/ppermute | solution.py:8
  48.4 1.4 maximum_select_fusion.6
  49.8 9.6 %collective-permute-start.4 = (bf16[448,896]{1,0:T(8,128)(2,1)S(1)}, bf16[448,896]{1,0:T(8,128)(2,1)S(1)}, u32[]{:S(2)}, u32[]{:S(2)}) collective-permute-start(bf16[448,896]{1,0:T(8,128)(2,1)S(1)} %maximum_select_fusion.6), channel_id=1, source_target_pairs={{0,64},{32,96},{64,0},{96,32},{128,192},{160,224},{192,128},{224,1... | collective-permute-start | bytes 2408456 | tf_op jit(solution)/shard_map/ppermute | solution.py:8
  59.4 0.0 collective-permute-done
  59.4 0.0 collective-permute-done.1
  59.4 2.9 %convolution_convert_fusion.1 = bf16[896,256]{1,0:T(8,128)(2,1)S(1)} fusion(f32[896,256]{0,1:T(8,128)} %collective-permute-done.1, f32[896,512]{0,1:T(8,128)S(1)} %convolution_bitcast_fusion, pred[]{:T(512)S(6)} %eq.9, bf16[448,896]{1,0:T(8,128)(2,1)} %collective-permute-done, bf16[448,896]{1,0:T(8,128)(2,1)} %bitcast.2), kind=kOutput, calls=%fused_computation.7 | convolution fusion | flops 419414016 | bytes 4817920 | tf_op jit(solution)/shard_map/dot_general | solution.py:53
  62.3 0.0 copy-start.7
  62.3 3.4 %collective-permute-done.2 = bf16[448,896]{1,0:T(8,128)(2,1)} collective-permute-done((bf16[448,896]{1,0:T(8,128)(2,1)}, bf16[448,896]{1,0:T(8,128)(2,1)}, u32[]{:S(2)}, u32[]{:S(2)}) %collective-permute-start.2) | collective-permute-done | bytes 802848 | tf_op jit(solution)/shard_map/ppermute | solution.py:8
  65.7 2.6 %fusion.33 = f32[896,256]{1,0:T(8,128)S(1)} fusion(bf16[896,256]{1,0:T(8,128)(2,1)S(1)} %convolution_convert_fusion.1, bf16[448,896]{1,0:T(8,128)(2,1)} %collective-permute-done.2, bf16[448,896]{1,0:T(8,128)(2,1)} %bitcast.5, pred[]{:T(512)S(6)} %eq.9), kind=kOutput, calls=%fused_computation.49 | convolution fusion | flops 418267136 | bytes 2981889 | tf_op jit(solution)/shard_map/dot_general | solution.py:53
  68.4 9.5 %collective-permute-start.5 = (f32[896,128]{1,0:T(8,128)S(1)}, f32[896,128]{1,0:T(8,128)S(1)}, u32[]{:S(2)}, u32[]{:S(2)}) collective-permute-start(f32[896,128]{1,0:T(8,128)S(1)} %slice_select_fusion.1), channel_id=1, source_target_pairs={{0,64},{32,96},{64,0},{96,32},{128,192},{160,224},{192,128},{224,1... | collective-permute-start | bytes 1376264 | tf_op jit(solution)/shard_map/ppermute | solution.py:8
  77.9 0.0 collective-permute-done.6
  77.9 1.2 maximum_select_fusion.9
  79.1 2.2 %collective-permute-start.7 = (bf16[256,896]{1,0:T(8,128)(2,1)S(1)}, bf16[256,896]{1,0:T(8,128)(2,1)S(1)}, u32[]{:S(2)}, u32[]{:S(2)}) collective-permute-start(bf16[256,896]{1,0:T(8,128)(2,1)S(1)} %maximum_select_fusion.9), channel_id=1, source_target_pairs={{0,64},{32,96},{64,0},{96,32},{128,192},{160,224},{192,128},{224,1... | collective-permute-start | bytes 1376264 | tf_op jit(solution)/shard_map/ppermute | solution.py:8
  82.0 12.8 %collective-permute-done.4 = bf16[448,896]{1,0:T(8,128)(2,1)S(1)} collective-permute-done((bf16[448,896]{1,0:T(8,128)(2,1)S(1)}, bf16[448,896]{1,0:T(8,128)(2,1)S(1)}, u32[]{:S(2)}, u32[]{:S(2)}) %collective-permute-start.4) | collective-permute-done | bytes 802848 | tf_op jit(solution)/shard_map/ppermute | solution.py:8
  94.8 9.8 %collective-permute-done.5 = f32[896,128]{1,0:T(8,128)S(1)} collective-permute-done((f32[896,128]{1,0:T(8,128)S(1)}, f32[896,128]{1,0:T(8,128)S(1)}, u32[]{:S(2)}, u32[]{:S(2)}) %collective-permute-start.5) | collective-permute-done | bytes 458784 | tf_op jit(solution)/shard_map/ppermute | solution.py:8
  104.6 0.6 convolution_convert_fusion.5
  105.2 0.0 copy-start.9
  105.2 0.0 copy-start.3
  105.2 9.2 %collective-permute-done.7 = bf16[256,896]{1,0:T(8,128)(2,1)S(1)} collective-permute-done((bf16[256,896]{1,0:T(8,128)(2,1)S(1)}, bf16[256,896]{1,0:T(8,128)(2,1)S(1)}, u32[]{:S(2)}, u32[]{:S(2)}) %collective-permute-start.7) | collective-permute-done | bytes 458784 | tf_op jit(solution)/shard_map/ppermute | solution.py:8
  114.4 0.4 convolution_select_fusion
  114.9 32.4 %all_to_all.10 = f32[32,16,128]{2,1,0:T(8,128)S(1)} all-to-all(f32[32,16,128]{2,1,0:T(8,128)S(1)} %bitcast.47), channel_id=1, replica_groups=mesh['sub'=16,'reg'=32] {'reg'}, dimensions={0} | all-to-all | bytes 524288 | tf_op jit(solution)/shard_map/all_to_all | solution.py:18
  147.3 3.1 %collective-permute-start.8 = (f32[16,128]{1,0:T(8,128)S(1)}, f32[16,128]{1,0:T(8,128)S(1)}, u32[]{:S(2)}, u32[]{:S(2)}) collective-permute-start(f32[16,128]{1,0:T(8,128)S(1)} %reduce_sum.9), channel_id=1, source_target_pairs={{0,128},{32,160},{64,192},{96,224},{128,0},{160,32},{192,64},{224,... | collective-permute-start | bytes 24584 | tf_op jit(solution)/shard_map/ppermute | solution.py:8
  150.4 1.3 collective-permute-done.8
  151.7 4.0 %collective-permute-start.9 = (f32[16,128]{1,0:T(8,128)S(1)}, f32[16,128]{1,0:T(8,128)S(1)}, u32[]{:S(2)}, u32[]{:S(2)}) collective-permute-start(f32[16,128]{1,0:T(8,128)S(1)} %add.24), channel_id=1, source_target_pairs={{0,256},{32,288},{64,320},{96,352},{128,384},{160,416},{192,448},{... | collective-permute-start | bytes 24584 | tf_op jit(solution)/shard_map/ppermute | solution.py:8
  155.7 1.3 collective-permute-done.9
  157.0 19.4 %all_to_all.11 = bf16[32,16,128]{2,1,0:T(8,128)(2,1)S(1)} all-to-all(bf16[32,16,128]{2,1,0:T(8,128)(2,1)S(1)} %broadcast_in_dim.32), channel_id=1, replica_groups=mesh['sub'=16,'reg'=32] {'reg'}, dimensions={0} | all-to-all | bytes 262144 | tf_op jit(solution)/shard_map/all_to_all | solution.py:24
  176.4 0.3 convolution_convert_fusion.7
  176.7 1.4 fusion.4
  178.1 2.2 %convolution_convert_fusion.4 = bf16[896,128]{0,1:T(8,128)(2,1)S(1)} fusion(bf16[448,896]{1,0:T(8,128)(2,1)} %copy-done.8, bf16[448,896]{1,0:T(8,128)(2,1)S(1)} %copy-done.2, pred[]{:T(512)S(6)} %eq.10, f32[896,128]{1,0:T(8,128)} %fusion.4, bf16[896,128]{1,0:T(8,128)(2,1)} %copy-done.9), kind=kOutput, calls=%fused_computation.12 | convolution fusion | flops 213204992 | bytes 2523137 | tf_op jit(solution)/shard_map/dot_general | solution.py:47
  180.3 0.0 copy-start.5
  180.3 2.6 %collective-permute-start.10 = (bf16[896,128]{0,1:T(8,128)(2,1)S(1)}, bf16[896,128]{0,1:T(8,128)(2,1)S(1)}, u32[]{:S(2)}, u32[]{:S(2)}) collective-permute-start(bf16[896,128]{0,1:T(8,128)(2,1)S(1)} %convolution_convert_fusion.4), channel_id=1, source_target_pairs={{0,64},{32,96},{64,0},{96,32},{128,192},{160,224},{192,128},{224,1... | collective-permute-start | bytes 688136 | tf_op jit(solution)/shard_map/ppermute | solution.py:8
  182.9 7.9 %collective-permute-done.10 = bf16[896,128]{0,1:T(8,128)(2,1)S(1)} collective-permute-done((bf16[896,128]{0,1:T(8,128)(2,1)S(1)}, bf16[896,128]{0,1:T(8,128)(2,1)S(1)}, u32[]{:S(2)}, u32[]{:S(2)}) %collective-permute-start.10) | collective-permute-done | bytes 229408 | tf_op jit(solution)/shard_map/ppermute | solution.py:8
  190.9 5.4 %convolution_convert_fusion = bf16[896,256]{0,1:T(8,128)(2,1)S(1)} fusion(bf16[896,256]{1,0:T(8,128)(2,1)} %copy-done.10, bf16[896,128]{0,1:T(8,128)(2,1)S(1)} %collective-permute-done.10, bf16[896,128]{0,1:T(8,128)(2,1)S(1)} %convolution_convert_fusion.4, pred[]{:T(512)S(6)} %eq.10, bf16[448,896]{1,0:T(8,128)(2,1)} %collective-permute-done.2, ...), kind=kOutput, calls=%fused_computation.6 | convolution fusion | flops 839516160 | bytes 4587522 | tf_op jit(solution)/shard_map/dot_general | solution.py:47
  196.3 1.9 collective-permute-start.11
  198.2 11.0 %collective-permute-done.11 = bf16[896,256]{0,1:T(8,128)(2,1)S(1)} collective-permute-done((bf16[896,256]{0,1:T(8,128)(2,1)S(1)}, bf16[896,256]{0,1:T(8,128)(2,1)S(1)}, u32[]{:S(2)}, u32[]{:S(2)}) %collective-permute-start.11) | collective-permute-done | bytes 458784 | tf_op jit(solution)/shard_map/ppermute | solution.py:8
  209.2 1.1 fusion.2
  210.3 0.9 copy.10
  (21 shorter events, 0.2 us)
Async XLA Ops:
  0.0 1.5 copy-start
  2.2 6.9 %copy-start.4 = (bf16[1,224,896]{2,1,0:T(8,128)(2,1)S(1)}, bf16[1,224,896]{2,1,0:T(8,128)(2,1)}, u32[]{:S(2)}) copy-start(bf16[1,224,896]{2,1,0:T(8,128)(2,1)} %param.14) | copy-start | bytes 1204228
  2.3 12.2 %copy-start.6 = (bf16[1,128,896]{2,1,0:T(8,128)(2,1)S(1)}, bf16[1,128,896]{2,1,0:T(8,128)(2,1)}, u32[]{:S(2)}) copy-start(bf16[1,128,896]{2,1,0:T(8,128)(2,1)} %param.15) | copy-start | bytes 688132
  3.3 56.1 %collective-permute-start.1 = (f32[896,256]{0,1:T(8,128)}, f32[896,256]{0,1:T(8,128)}, u32[]{:S(2)}, u32[]{:S(2)}) collective-permute-start(f32[896,256]{0,1:T(8,128)} %slice_select_fusion), channel_id=1, source_target_pairs={{0,32},{32,0},{64,96},{96,64},{128,160},{160,128},{192,224},{224,1... | collective-permute-start | bytes 2752520 | tf_op jit(solution)/shard_map/ppermute | solution.py:8
  7.2 52.2 %collective-permute-start = (bf16[448,896]{1,0:T(8,128)(2,1)}, bf16[448,896]{1,0:T(8,128)(2,1)}, u32[]{:S(2)}, u32[]{:S(2)}) collective-permute-start(bf16[448,896]{1,0:T(8,128)(2,1)} %bitcast.2), channel_id=1, source_target_pairs={{0,32},{32,0},{64,96},{96,64},{128,160},{160,128},{192,224},{224,1... | collective-permute-start | bytes 2408456 | tf_op jit(solution)/shard_map/ppermute | solution.py:8
  9.2 39.2 %collective-permute-start.3 = (bf16[224,896]{1,0:T(8,128)(2,1)S(1)}, bf16[224,896]{1,0:T(8,128)(2,1)}, u32[]{:S(2)}, u32[]{:S(2)}) collective-permute-start(bf16[224,896]{1,0:T(8,128)(2,1)S(1)} %bitcast.45), channel_id=1, source_target_pairs={{0,32},{32,0},{64,96},{96,64},{128,160},{160,128},{192,224},{224,1... | collective-permute-start | bytes 1204232 | tf_op jit(solution)/shard_map/ppermute | solution.py:8
  12.6 53.2 %collective-permute-start.2 = (bf16[448,896]{1,0:T(8,128)(2,1)}, bf16[448,896]{1,0:T(8,128)(2,1)}, u32[]{:S(2)}, u32[]{:S(2)}) collective-permute-start(bf16[448,896]{1,0:T(8,128)(2,1)} %bitcast.5), channel_id=1, source_target_pairs={{0,32},{32,0},{64,96},{96,64},{128,160},{160,128},{192,224},{224,1... | collective-permute-start | bytes 2408456 | tf_op jit(solution)/shard_map/ppermute | solution.py:8
  14.5 63.4 %collective-permute-start.6 = (bf16[128,896]{1,0:T(8,128)(2,1)S(1)}, bf16[128,896]{1,0:T(8,128)(2,1)}, u32[]{:S(2)}, u32[]{:S(2)}) collective-permute-start(bf16[128,896]{1,0:T(8,128)(2,1)S(1)} %bitcast.48), channel_id=1, source_target_pairs={{0,32},{32,0},{64,96},{96,64},{128,160},{160,128},{192,224},{224,1... | collective-permute-start | bytes 688136 | tf_op jit(solution)/shard_map/ppermute | solution.py:8
  49.8 54.8 %copy-start.1 = (bf16[448,896]{1,0:T(8,128)(2,1)}, bf16[448,896]{1,0:T(8,128)(2,1)S(1)}, u32[]{:S(2)}) copy-start(bf16[448,896]{1,0:T(8,128)(2,1)S(1)} %maximum_select_fusion.6) | copy-start | bytes 2408452
  49.8 45.0 %collective-permute-start.4 = (bf16[448,896]{1,0:T(8,128)(2,1)S(1)}, bf16[448,896]{1,0:T(8,128)(2,1)S(1)}, u32[]{:S(2)}, u32[]{:S(2)}) collective-permute-start(bf16[448,896]{1,0:T(8,128)(2,1)S(1)} %maximum_select_fusion.6), channel_id=1, source_target_pairs={{0,64},{32,96},{64,0},{96,32},{128,192},{160,224},{192,128},{224,1... | collective-permute-start | bytes 2408456 | tf_op jit(solution)/shard_map/ppermute | solution.py:8
  62.3 6.0 %copy-start.10 = (bf16[896,256]{1,0:T(8,128)(2,1)}, bf16[896,256]{1,0:T(8,128)(2,1)S(1)}, u32[]{:S(2)}) copy-start(bf16[896,256]{1,0:T(8,128)(2,1)S(1)} %convolution_convert_fusion.1) | copy-start | bytes 1376260
  62.3 15.6 %copy-start.7 = (bf16[1,128,896]{2,1,0:T(8,128)(2,1)S(1)}, bf16[1,128,896]{2,1,0:T(8,128)(2,1)}, u32[]{:S(2)}) copy-start(bf16[1,128,896]{2,1,0:T(8,128)(2,1)} %param.15) | copy-start | bytes 688132
  68.4 36.2 %collective-permute-start.5 = (f32[896,128]{1,0:T(8,128)S(1)}, f32[896,128]{1,0:T(8,128)S(1)}, u32[]{:S(2)}, u32[]{:S(2)}) collective-permute-start(f32[896,128]{1,0:T(8,128)S(1)} %slice_select_fusion.1), channel_id=1, source_target_pairs={{0,64},{32,96},{64,0},{96,32},{128,192},{160,224},{192,128},{224,1... | collective-permute-start | bytes 1376264 | tf_op jit(solution)/shard_map/ppermute | solution.py:8
  79.1 35.3 %collective-permute-start.7 = (bf16[256,896]{1,0:T(8,128)(2,1)S(1)}, bf16[256,896]{1,0:T(8,128)(2,1)S(1)}, u32[]{:S(2)}, u32[]{:S(2)}) collective-permute-start(bf16[256,896]{1,0:T(8,128)(2,1)S(1)} %maximum_select_fusion.9), channel_id=1, source_target_pairs={{0,64},{32,96},{64,0},{96,32},{128,192},{160,224},{192,128},{224,1... | collective-permute-start | bytes 1376264 | tf_op jit(solution)/shard_map/ppermute | solution.py:8
  94.8 10.5 %copy-start.8 = (bf16[448,896]{1,0:T(8,128)(2,1)}, bf16[448,896]{1,0:T(8,128)(2,1)S(1)}, u32[]{:S(2)}) copy-start(bf16[448,896]{1,0:T(8,128)(2,1)S(1)} %collective-permute-done.4) | copy-start | bytes 2408452
  105.2 9.6 %copy-start.9 = (bf16[896,128]{1,0:T(8,128)(2,1)}, bf16[896,128]{1,0:T(8,128)(2,1)S(1)}, u32[]{:S(2)}) copy-start(bf16[896,128]{1,0:T(8,128)(2,1)S(1)} %convolution_convert_fusion.5) | copy-start | bytes 688132
  105.2 71.1 %copy-start.3 = (bf16[512,512]{1,0:T(8,128)(2,1)S(1)}, bf16[512,512]{1,0:T(8,128)(2,1)}, u32[]{:S(2)}) copy-start(bf16[512,512]{1,0:T(8,128)(2,1)} %param.16) | copy-start | bytes 1572868
  147.3 4.4 %collective-permute-start.8 = (f32[16,128]{1,0:T(8,128)S(1)}, f32[16,128]{1,0:T(8,128)S(1)}, u32[]{:S(2)}, u32[]{:S(2)}) collective-permute-start(f32[16,128]{1,0:T(8,128)S(1)} %reduce_sum.9), channel_id=1, source_target_pairs={{0,128},{32,160},{64,192},{96,224},{128,0},{160,32},{192,64},{224,... | collective-permute-start | bytes 24584 | tf_op jit(solution)/shard_map/ppermute | solution.py:8
  151.7 5.3 %collective-permute-start.9 = (f32[16,128]{1,0:T(8,128)S(1)}, f32[16,128]{1,0:T(8,128)S(1)}, u32[]{:S(2)}, u32[]{:S(2)}) collective-permute-start(f32[16,128]{1,0:T(8,128)S(1)} %add.24), channel_id=1, source_target_pairs={{0,256},{32,288},{64,320},{96,352},{128,384},{160,416},{192,448},{... | collective-permute-start | bytes 24584 | tf_op jit(solution)/shard_map/ppermute | solution.py:8
  176.7 1.4 copy-start.2
  180.3 28.8 %copy-start.5 = (bf16[1,1,384,384]{3,2,1,0:T(8,128)(2,1)S(1)}, bf16[1,1,384,384]{3,2,1,0:T(8,128)(2,1)}, u32[]{:S(2)}) copy-start(bf16[1,1,384,384]{3,2,1,0:T(8,128)(2,1)} %param.10) | copy-start | bytes 884740
  180.3 10.5 %collective-permute-start.10 = (bf16[896,128]{0,1:T(8,128)(2,1)S(1)}, bf16[896,128]{0,1:T(8,128)(2,1)S(1)}, u32[]{:S(2)}, u32[]{:S(2)}) collective-permute-start(bf16[896,128]{0,1:T(8,128)(2,1)S(1)} %convolution_convert_fusion.4), channel_id=1, source_target_pairs={{0,64},{32,96},{64,0},{96,32},{128,192},{160,224},{192,128},{224,1... | collective-permute-start | bytes 688136 | tf_op jit(solution)/shard_map/ppermute | solution.py:8
  196.3 12.9 %collective-permute-start.11 = (bf16[896,256]{0,1:T(8,128)(2,1)S(1)}, bf16[896,256]{0,1:T(8,128)(2,1)S(1)}, u32[]{:S(2)}, u32[]{:S(2)}) collective-permute-start(bf16[896,256]{0,1:T(8,128)(2,1)S(1)} %convolution_convert_fusion), channel_id=1, source_target_pairs={{0,32},{32,0},{64,96},{96,64},{128,160},{160,128},{192,224},{224,1... | collective-permute-start | bytes 1376264 | tf_op jit(solution)/shard_map/ppermute | solution.py:8
where the time goes:
time: 212 us; the launch traced here: 211 us
  waiting for transfers between devices  87.2 us (41%)
  blocking collectives  51.7 us (24%)
  starting transfers between devices  47.4 us (22%)
  matrix products  19.2 us (9%)
  other arithmetic  3.66 us (2%)
    ppermute x12, waiting for transfers between devices, swapped(): lax.ppermute(x, axis, [(i, i ^ 1 << bit) for i in range(lax.axis_size(axi...  87.2 us
    ppermute x12, starting transfers between devices, swapped(): lax.ppermute(x, axis, [(i, i ^ 1 << bit) for i in range(lax.axis_size(axi...  47.4 us
    all_to_all x1, blocking collectives, sent_and_summed(): lax.all_to_all(tiles, axis, split_axis=0, concat_axis=0, tiled=True)  32.4 us
    all_to_all x1, blocking collectives, from_everyone(): return lax.all_to_all(copies, axis, split_axis=0, concat_axis=0, tiled=True)  19.4 us
    dot_general x4, matrix products, apply_transpose(): lax.dot_general(matrix, vector, (((0,), (0,)), ((), ())), preferred_eleme...  10.1 us
    dot_general x7, matrix products, product(): return jnp.dot(matrix, vector, preferred_element_type=jnp.float32)  9.07 us
  transfers between devices with their start and end apart: 12, of which 9 were waited for; matrix products, arithmetic and copies ran while one was open for 4% of the time, Pallas kernels for 0%

commit v1 on v0

v1 whole, which is shorter than its diff:
```python
import jax
import jax.numpy as jnp
from jax import lax
from jax.sharding import PartitionSpec as P


from jax.sharding import Mesh

AXES = ("zl", "x", "y", "zh", "c")
GROUP = ("zl", "y", "zh", "c")
NEAR = [(0, 1), (1, 0), (2, 3), (3, 2)]
NEXT = [(0, 3), (3, 0), (1, 2), (2, 1)]
BF = jnp.bfloat16


def send(x, pairs):
    return lax.ppermute(x, "x", pairs)


def to_group(tiles):
    return lax.all_to_all(tiles, GROUP, split_axis=0, concat_axis=0, tiled=True)


def attach(mine, other, mine_first, axis_pos):
    return jnp.where(
        mine_first,
        jnp.concatenate([mine, other], axis_pos),
        jnp.concatenate([other, mine], axis_pos),
    )


def apply_transpose(matrix, vector):
    return lax.dot_general(
        matrix, vector, (((0,), (0,)), ((), ())), preferred_element_type=jnp.float32
    )


def product(matrix, vector):
    return jnp.dot(matrix, vector, preferred_element_type=jnp.float32)


def per_device(
    port_loads,
    leaf_inverse,
    leaf_coupling,
    first_inverse,
    second_coupling,
    second_inverse,
    border_coupling,
    border_inverse,
    border_rows,
):
    at = lax.axis_index("x")
    low = at % 2 == 0
    first_half = (at == 0) | (at == 3)
    lower = at < 2
    group = lax.axis_size(GROUP)
    leaf_inv = leaf_inverse[0, 0]
    leaf_coup = leaf_coupling[0, 0]
    fwd_leaf = product(leaf_inv, port_loads[0, 0]).astype(BF)
    half = fwd_leaf.shape[1] // 2
    left, right = fwd_leaf[:, :half], fwd_leaf[:, half:]
    sent_one = product(leaf_coup, jnp.where(first_half, right, left)).astype(BF)
    came_one = send(sent_one, NEAR)
    inv_one = first_inverse[0]
    coup_two = second_coupling[0]
    inv_two = second_inverse[0]
    coup_border = border_coupling[0]
    inv_one = attach(inv_one, send(inv_one, NEAR), low, 0)
    inv_two = attach(inv_two, send(inv_two, NEAR), low, 0)
    coup_border = attach(coup_border, send(coup_border, NEAR), low, 0)
    coup_two = attach(coup_two, send(coup_two, NEAR), low, 0)
    inv_two = attach(inv_two, send(inv_two, NEXT), lower, 0)
    coup_border = attach(coup_border, send(coup_border, NEXT), lower, 0)
    kept_one = product(leaf_coup, jnp.where(first_half, left, right))
    rhs_one = (-(kept_one + came_one.astype(jnp.float32))).astype(BF)
    fwd_one = product(inv_one, rhs_one).astype(BF)
    part_two = product(coup_two, fwd_one)
    quarter = half // 2
    kept_two = jnp.where(lower, part_two[:, :quarter], part_two[:, quarter:])
    sent_two = jnp.where(lower, part_two[:, quarter:], part_two[:, :quarter])
    came_two = send(sent_two.astype(BF), NEXT)
    rhs_two = (-(kept_two + came_two.astype(jnp.float32))).astype(BF)
    fwd_two = product(inv_two, rhs_two).astype(BF)
    border_count = coup_border.shape[0]
    row_mask = lax.broadcasted_iota(jnp.int32, (border_count, 1), 0) < border_rows[0]
    part_border = jnp.where(row_mask, product(coup_border, fwd_two), jnp.float32(0.0))
    tiles = part_border.astype(BF).reshape(group, border_count // group, quarter)
    share_sum = jnp.sum(to_group(tiles).astype(jnp.float32), axis=0)
    rhs_share = (-share_sum).astype(BF)
    rhs_border = to_group(jnp.broadcast_to(rhs_share, tiles.shape)).reshape(border_count, quarter)
    fwd_border = product(border_inverse, rhs_border).astype(BF)
    back_border = apply_transpose(border_inverse, fwd_border).astype(BF)
    masked = jnp.where(row_mask, back_border, jnp.zeros_like(back_border))
    diff_two = (fwd_two.astype(jnp.float32) - apply_transpose(coup_border, masked)).astype(BF)
    back_two = apply_transpose(inv_two, diff_two).astype(BF)
    back_two = attach(back_two, send(back_two, NEXT), lower, 1)
    diff_one = (fwd_one.astype(jnp.float32) - apply_transpose(coup_two, back_two)).astype(BF)
    back_one = apply_transpose(inv_one, diff_one).astype(BF)
    back_one = attach(back_one, send(back_one, NEAR), first_half, 1)
    diff_leaf = (fwd_leaf.astype(jnp.float32) - apply_transpose(leaf_coup, back_one)).astype(BF)
    solution = apply_transpose(leaf_inv, diff_leaf).astype(BF)
    return solution[None, None]


def solution(mesh):
    split = Mesh(mesh.devices.reshape(4, 4, 8, 2, 2), AXES)
    reg, sub = ("y", "zh", "c"), ("zl", "x")
    return jax.shard_map(
        per_device,
        mesh=split,
        in_specs=(P(reg, sub),) * 7 + (P(None, None), P(reg)),
        out_specs=P(reg, sub),
        check_vma=False,
    )
```

time: 212 us -> 163 us (0.77)
  waiting for transfers between devices: 87.2 us -> 50.6 us
  starting transfers between devices: 47.4 us -> 41 us
  blocking collectives: 51.7 us -> 48.1 us
  other arithmetic: 3.66 us -> 0.56 us
    ppermute x12 -> x10, waiting for transfers between devices: 87.2 us -> 50.6 us  [send(): return lax.ppermute(x, 'x', pairs)]
    ppermute x12 -> x10, starting transfers between devices: 47.4 us -> 41 us  [send(): return lax.ppermute(x, 'x', pairs)]
    all_to_all x2, blocking collectives: 51.7 us -> 48.1 us  [to_group(): return lax.all_to_all(tiles, GROUP, split_axis=0, concat_axis=0, tiled=True)]
    select_n x2, other arithmetic: 2.53 us -> 0.36 us  [attach(): jnp.where(mine_first, jnp.concatenate([mine, other], axis_pos), jnp.conca...]
  transfers between devices with their start and end apart: 12 -> 10, of which waited for: 9 -> 7; matrix products, arithmetic and copies ran while one was open for 4% -> 7% of each run, Pallas kernels for 0% -> 0%
where the time goes in v1:
time: 163 us
  waiting for transfers between devices  50.6 us (31%)
  blocking collectives  48.1 us (30%)
  starting transfers between devices  41 us (25%)
  matrix products  20.5 us (13%)
    ppermute x10, waiting for transfers between devices, send(): return lax.ppermute(x, 'x', pairs)  50.6 us
    all_to_all x2, blocking collectives, to_group(): return lax.all_to_all(tiles, GROUP, split_axis=0, concat_axis=0, tiled=True)  48.1 us
    ppermute x10, starting transfers between devices, send(): return lax.ppermute(x, 'x', pairs)  41 us
    dot_general x7, matrix products, product(): return jnp.dot(matrix, vector, preferred_element_type=jnp.float32)  11 us
    dot_general x4, matrix products, apply_transpose(): lax.dot_general(matrix, vector, (((0,), (0,)), ((), ())), preferred_eleme...  9.46 us
  transfers between devices with their start and end apart: 10, of which 7 were waited for; matrix products, arithmetic and copies ran while one was open for 7% of the time, Pallas kernels for 0%

profile of v1, /device:TPU:1, one launch (start us, length us, event | category | flops | bytes accessed | tf_op | source)
XLA Modules:
  0.0 162.6 jit_solution(15339199800607809909)
XLA Ops:
  0.0 0.0 copy-start
  0.0 4.1 %collective-permute-start = (bf16[448,896]{1,0:T(8,128)(2,1)}, bf16[448,896]{1,0:T(8,128)(2,1)}, u32[]{:S(2)}, u32[]{:S(2)}) collective-permute-start(bf16[448,896]{1,0:T(8,128)(2,1)} %bitcast.61), channel_id=1, source_target_pairs={{0,32},{32,0},{64,96},{96,64},{1,33},{33,1},{65,97},{97,65},{2,34}... | collective-permute-start | bytes 2408456 | tf_op jit(solution)/shard_map/ppermute | solution.py:17
  4.1 1.9 %collective-permute-start.3 = (bf16[224,896]{1,0:T(8,128)(2,1)}, bf16[224,896]{1,0:T(8,128)(2,1)S(1)}, u32[]{:S(2)}, u32[]{:S(2)}) collective-permute-start(bf16[224,896]{1,0:T(8,128)(2,1)} %bitcast.56), channel_id=1, source_target_pairs={{0,32},{32,0},{64,96},{96,64},{1,33},{33,1},{65,97},{97,65},{2,34}... | collective-permute-start | bytes 1204232 | tf_op jit(solution)/shard_map/ppermute | solution.py:17
  6.0 1.4 convolution_convert_fusion.4
  7.5 0.0 copy-start.4
  7.5 0.0 copy-start.2
  7.5 0.0 copy-done
  7.5 1.3 fusion.2
  8.8 3.4 %collective-permute-start.1 = (bf16[896,256]{0,1:T(8,128)(2,1)}, bf16[896,256]{0,1:T(8,128)(2,1)}, u32[]{:S(2)}, u32[]{:S(2)}) collective-permute-start(bf16[896,256]{0,1:T(8,128)(2,1)} %fusion.2), channel_id=1, source_target_pairs={{0,32},{32,0},{64,96},{96,64},{1,33},{33,1},{65,97},{97,65},{2,34}... | collective-permute-start | bytes 1376264 | tf_op jit(solution)/shard_map/ppermute | solution.py:17
  12.1 1.9 %collective-permute-start.2 = (bf16[448,896]{1,0:T(8,128)(2,1)}, bf16[448,896]{1,0:T(8,128)(2,1)}, u32[]{:S(2)}, u32[]{:S(2)}) collective-permute-start(bf16[448,896]{1,0:T(8,128)(2,1)} %bitcast.6), channel_id=1, source_target_pairs={{0,32},{32,0},{64,96},{96,64},{1,33},{33,1},{65,97},{97,65},{2,34}... | collective-permute-start | bytes 2408456 | tf_op jit(solution)/shard_map/ppermute | solution.py:17
  14.1 0.0 copy-done.4
  14.1 3.4 %collective-permute-start.6 = (bf16[128,896]{1,0:T(8,128)(2,1)S(1)}, bf16[128,896]{1,0:T(8,128)(2,1)S(1)}, u32[]{:S(2)}, u32[]{:S(2)}) collective-permute-start(bf16[128,896]{1,0:T(8,128)(2,1)S(1)} %bitcast.58), channel_id=1, source_target_pairs={{0,32},{32,0},{64,96},{96,64},{1,33},{33,1},{65,97},{97,65},{2,34}... | collective-permute-start | bytes 688136 | tf_op jit(solution)/shard_map/ppermute | solution.py:17
  17.4 8.2 %collective-permute-done.3 = bf16[224,896]{1,0:T(8,128)(2,1)S(1)} collective-permute-done((bf16[224,896]{1,0:T(8,128)(2,1)}, bf16[224,896]{1,0:T(8,128)(2,1)S(1)}, u32[]{:S(2)}, u32[]{:S(2)}) %collective-permute-start.3) | collective-permute-done | bytes 401440 | tf_op jit(solution)/shard_map/ppermute | solution.py:17
  25.7 0.0 copy-done.2
  25.7 0.3 maximum_select_fusion.6
  26.0 9.1 %collective-permute-start.4 = (bf16[448,896]{1,0:T(8,128)(2,1)S(1)}, bf16[448,896]{1,0:T(8,128)(2,1)}, u32[]{:S(2)}, u32[]{:S(2)}) collective-permute-start(bf16[448,896]{1,0:T(8,128)(2,1)S(1)} %maximum_select_fusion.6), channel_id=1, source_target_pairs={{0,96},{96,0},{32,64},{64,32},{1,97},{97,1},{33,65},{65,33},{2,98}... | collective-permute-start | bytes 2408456 | tf_op jit(solution)/shard_map/ppermute | solution.py:17
  35.1 0.4 collective-permute-done.1
  35.5 0.0 collective-permute-done
  35.5 3.1 %convolution_convert_fusion.2 = bf16[896,256]{1,0:T(8,128)(2,1)S(1)} fusion(bf16[896,256]{0,1:T(8,128)(2,1)} %collective-permute-done.1, bf16[1,1,896,384]{3,2,1,0:T(8,128)(2,1)S(1)} %copy-done, bf16[448,896]{1,0:T(8,128)(2,1)} %collective-permute-done, bf16[448,896]{1,0:T(8,128)(2,1)} %bitcast.62, pred[]{:T(512)S(6)} %eq.13, pred[]{:T(512)S(6)} %or.3, ...), kind=kOutput, calls=%fused_computation.8 | convolution fusion | flops 595673088 | bytes 3604482 | tf_op jit(solution)/shard_map/dot_general | solution.py:39
  38.6 0.0 copy-start.7
  38.6 14.1 %collective-permute-done.2 = bf16[448,896]{1,0:T(8,128)(2,1)} collective-permute-done((bf16[448,896]{1,0:T(8,128)(2,1)}, bf16[448,896]{1,0:T(8,128)(2,1)}, u32[]{:S(2)}, u32[]{:S(2)}) %collective-permute-start.2) | collective-permute-done | bytes 802848 | tf_op jit(solution)/shard_map/ppermute | solution.py:17
  52.7 2.5 %fusion.39 = f32[896,256]{1,0:T(8,128)S(1)} fusion(bf16[896,256]{1,0:T(8,128)(2,1)S(1)} %convolution_convert_fusion.2, bf16[448,896]{1,0:T(8,128)(2,1)} %collective-permute-done.2, bf16[448,896]{1,0:T(8,128)(2,1)} %bitcast.6, pred[]{:T(512)S(6)} %eq.13), kind=kOutput, calls=%fused_computation.51 | convolution fusion | flops 418267136 | bytes 2981889 | tf_op jit(solution)/shard_map/dot_general | solution.py:39
  55.2 0.0 copy-done.7
  55.3 9.2 %collective-permute-start.5 = (bf16[896,128]{1,0:T(8,128)(2,1)S(1)}, bf16[896,128]{1,0:T(8,128)(2,1)S(1)}, u32[]{:S(2)}, u32[]{:S(2)}) collective-permute-start(bf16[896,128]{1,0:T(8,128)(2,1)S(1)} %select_convert_fusion), channel_id=1, source_target_pairs={{0,96},{96,0},{32,64},{64,32},{1,97},{97,1},{33,65},{65,33},{2,98}... | collective-permute-start | bytes 688136 | tf_op jit(solution)/shard_map/ppermute | solution.py:17
  64.6 0.0 collective-permute-done.6
  64.6 0.1 maximum_select_fusion.9
  64.7 2.2 %collective-permute-start.7 = (bf16[256,896]{1,0:T(8,128)(2,1)S(1)}, bf16[256,896]{1,0:T(8,128)(2,1)S(1)}, u32[]{:S(2)}, u32[]{:S(2)}) collective-permute-start(bf16[256,896]{1,0:T(8,128)(2,1)S(1)} %maximum_select_fusion.9), channel_id=1, source_target_pairs={{0,96},{96,0},{32,64},{64,32},{1,97},{97,1},{33,65},{65,33},{2,98}... | collective-permute-start | bytes 1376264 | tf_op jit(solution)/shard_map/ppermute | solution.py:17
  67.5 0.4 collective-permute-done.5
  68.0 0.0 collective-permute-done.4
  68.0 2.0 %convolution_convert_fusion.6 = bf16[896,128]{1,0:T(8,128)(2,1)S(1)} fusion(bf16[448,896]{1,0:T(8,128)(2,1)} %collective-permute-done.4, bf16[448,896]{1,0:T(8,128)(2,1)S(1)} %maximum_select_fusion.6, pred[]{:T(512)S(6)} %lt.21, bf16[896,128]{1,0:T(8,128)(2,1)S(1)} %collective-permute-done.5, f32[896,256]{1,0:T(8,128)S(1)} %fusion.39), kind=kOutput, calls=%fused_computation.15 | convolution fusion | flops 213434368 | bytes 2982912 | tf_op jit(solution)/shard_map/dot_general | solution.py:39
  70.0 0.0 copy-start.6
  70.0 10.3 %collective-permute-done.7 = bf16[256,896]{1,0:T(8,128)(2,1)S(1)} collective-permute-done((bf16[256,896]{1,0:T(8,128)(2,1)S(1)}, bf16[256,896]{1,0:T(8,128)(2,1)S(1)}, u32[]{:S(2)}, u32[]{:S(2)}) %collective-permute-start.7) | collective-permute-done | bytes 458784 | tf_op jit(solution)/shard_map/ppermute | solution.py:17
  80.3 0.4 fusion.4
  80.8 0.0 copy-start.1
  80.8 30.6 %all_to_all.10 = bf16[128,4,128]{2,1,0:T(4,128)(2,1)S(1)} all-to-all(bf16[128,4,128]{2,1,0:T(4,128)(2,1)S(1)} %bitcast.60), channel_id=1, replica_groups=mesh['zl'=4,'x'=4,'y'=8,'zh'=2,'c'=2] {'zl','y','zh','c'}, dimensions={0} | all-to-all | bytes 262144 | tf_op jit(solution)/shard_map/all_to_all | solution.py:21
  111.4 0.1 convert_reduce_fusion
  111.6 17.5 %all_to_all.11 = bf16[128,4,128]{2,1,0:T(4,128)(2,1)S(1)} all-to-all(bf16[128,4,128]{2,1,0:T(4,128)(2,1)S(1)} %broadcast_in_dim.32), channel_id=1, replica_groups=mesh['zl'=4,'x'=4,'y'=8,'zh'=2,'c'=2] {'zl','y','zh','c'}, dimensions={0} | all-to-all | bytes 262144 | tf_op jit(solution)/shard_map/all_to_all | solution.py:21
  129.1 0.3 convolution_convert_fusion.8
  129.4 1.4 fusion.6
  130.8 2.3 %convolution_convert_fusion.5 = bf16[896,128]{0,1:T(8,128)(2,1)S(1)} fusion(bf16[448,896]{1,0:T(8,128)(2,1)} %collective-permute-done.4, bf16[448,896]{1,0:T(8,128)(2,1)S(1)} %maximum_select_fusion.6, pred[]{:T(512)S(6)} %lt.21, f32[896,128]{1,0:T(8,128)} %fusion.6, bf16[896,128]{1,0:T(8,128)(2,1)} %copy-done.6), kind=kOutput, calls=%fused_computation.14 | convolution fusion | flops 213204992 | bytes 2523137 | tf_op jit(solution)/shard_map/dot_general | solution.py:33
  133.1 0.0 copy-start.3
  133.1 3.9 %collective-permute-start.8 = (bf16[896,128]{0,1:T(8,128)(2,1)S(1)}, bf16[896,128]{0,1:T(8,128)(2,1)S(1)}, u32[]{:S(2)}, u32[]{:S(2)}) collective-permute-start(bf16[896,128]{0,1:T(8,128)(2,1)S(1)} %convolution_convert_fusion.5), channel_id=1, source_target_pairs={{0,96},{96,0},{32,64},{64,32},{1,97},{97,1},{33,65},{65,33},{2,98}... | collective-permute-start | bytes 688136 | tf_op jit(solution)/shard_map/ppermute | solution.py:17
  137.0 6.2 %collective-permute-done.8 = bf16[896,128]{0,1:T(8,128)(2,1)S(1)} collective-permute-done((bf16[896,128]{0,1:T(8,128)(2,1)S(1)}, bf16[896,128]{0,1:T(8,128)(2,1)S(1)}, u32[]{:S(2)}, u32[]{:S(2)}) %collective-permute-start.8) | collective-permute-done | bytes 229408 | tf_op jit(solution)/shard_map/ppermute | solution.py:17
  143.1 4.7 %convolution_convert_fusion.1 = bf16[896,256]{0,1:T(8,128)(2,1)S(1)} fusion(bf16[896,256]{1,0:T(8,128)(2,1)} %copy-done.7, bf16[896,128]{0,1:T(8,128)(2,1)S(1)} %collective-permute-done.8, bf16[896,128]{0,1:T(8,128)(2,1)S(1)} %convolution_convert_fusion.5, pred[]{:T(512)S(6)} %lt.21, bf16[448,896]{1,0:T(8,128)(2,1)} %collective-permute-done.2, ...), kind=kOutput, calls=%fused_computation.7 | convolution fusion | flops 839516160 | bytes 4587522 | tf_op jit(solution)/shard_map/dot_general | solution.py:33
  147.9 1.9 %collective-permute-start.9 = (bf16[896,256]{0,1:T(8,128)(2,1)S(1)}, bf16[896,256]{0,1:T(8,128)(2,1)S(1)}, u32[]{:S(2)}, u32[]{:S(2)}) collective-permute-start(bf16[896,256]{0,1:T(8,128)(2,1)S(1)} %convolution_convert_fusion.1), channel_id=1, source_target_pairs={{0,32},{32,0},{64,96},{96,64},{1,33},{33,1},{65,97},{97,65},{2,34}... | collective-permute-start | bytes 1376264 | tf_op jit(solution)/shard_map/ppermute | solution.py:17
  149.8 10.8 %collective-permute-done.9 = bf16[896,256]{0,1:T(8,128)(2,1)S(1)} collective-permute-done((bf16[896,256]{0,1:T(8,128)(2,1)S(1)}, bf16[896,256]{0,1:T(8,128)(2,1)S(1)}, u32[]{:S(2)}, u32[]{:S(2)}) %collective-permute-start.9) | collective-permute-done | bytes 458784 | tf_op jit(solution)/shard_map/ppermute | solution.py:17
  160.6 1.0 fusion.3
  161.7 0.9 copy.10
  (9 shorter events, 0.1 us)
Async XLA Ops:
  0.0 7.5 %copy-start = (bf16[1,1,896,384]{3,2,1,0:T(8,128)(2,1)S(1)}, bf16[1,1,896,384]{3,2,1,0:T(8,128)(2,1)}, u32[]{:S(2)}) copy-start(bf16[1,1,896,384]{3,2,1,0:T(8,128)(2,1)} %param.11) | copy-start | bytes 2064388
  0.0 35.5 %collective-permute-start = (bf16[448,896]{1,0:T(8,128)(2,1)}, bf16[448,896]{1,0:T(8,128)(2,1)}, u32[]{:S(2)}, u32[]{:S(2)}) collective-permute-start(bf16[448,896]{1,0:T(8,128)(2,1)} %bitcast.61), channel_id=1, source_target_pairs={{0,32},{32,0},{64,96},{96,64},{1,33},{33,1},{65,97},{97,65},{2,34}... | collective-permute-start | bytes 2408456 | tf_op jit(solution)/shard_map/ppermute | solution.py:17
  4.1 21.6 %collective-permute-start.3 = (bf16[224,896]{1,0:T(8,128)(2,1)}, bf16[224,896]{1,0:T(8,128)(2,1)S(1)}, u32[]{:S(2)}, u32[]{:S(2)}) collective-permute-start(bf16[224,896]{1,0:T(8,128)(2,1)} %bitcast.56), channel_id=1, source_target_pairs={{0,32},{32,0},{64,96},{96,64},{1,33},{33,1},{65,97},{97,65},{2,34}... | collective-permute-start | bytes 1204232 | tf_op jit(solution)/shard_map/ppermute | solution.py:17
  7.5 6.6 %copy-start.4 = (bf16[1,128,896]{2,1,0:T(8,128)(2,1)S(1)}, bf16[1,128,896]{2,1,0:T(8,128)(2,1)}, u32[]{:S(2)}) copy-start(bf16[1,128,896]{2,1,0:T(8,128)(2,1)} %param.15) | copy-start | bytes 688132
  7.5 18.2 %copy-start.2 = (bf16[1,224,896]{2,1,0:T(8,128)(2,1)S(1)}, bf16[1,224,896]{2,1,0:T(8,128)(2,1)}, u32[]{:S(2)}) copy-start(bf16[1,224,896]{2,1,0:T(8,128)(2,1)} %param.14) | copy-start | bytes 1204228
  8.8 26.7 %collective-permute-start.1 = (bf16[896,256]{0,1:T(8,128)(2,1)}, bf16[896,256]{0,1:T(8,128)(2,1)}, u32[]{:S(2)}, u32[]{:S(2)}) collective-permute-start(bf16[896,256]{0,1:T(8,128)(2,1)} %fusion.2), channel_id=1, source_target_pairs={{0,32},{32,0},{64,96},{96,64},{1,33},{33,1},{65,97},{97,65},{2,34}... | collective-permute-start | bytes 1376264 | tf_op jit(solution)/shard_map/ppermute | solution.py:17
  12.1 40.6 %collective-permute-start.2 = (bf16[448,896]{1,0:T(8,128)(2,1)}, bf16[448,896]{1,0:T(8,128)(2,1)}, u32[]{:S(2)}, u32[]{:S(2)}) collective-permute-start(bf16[448,896]{1,0:T(8,128)(2,1)} %bitcast.6), channel_id=1, source_target_pairs={{0,32},{32,0},{64,96},{96,64},{1,33},{33,1},{65,97},{97,65},{2,34}... | collective-permute-start | bytes 2408456 | tf_op jit(solution)/shard_map/ppermute | solution.py:17
  14.1 50.5 %collective-permute-start.6 = (bf16[128,896]{1,0:T(8,128)(2,1)S(1)}, bf16[128,896]{1,0:T(8,128)(2,1)S(1)}, u32[]{:S(2)}, u32[]{:S(2)}) collective-permute-start(bf16[128,896]{1,0:T(8,128)(2,1)S(1)} %bitcast.58), channel_id=1, source_target_pairs={{0,32},{32,0},{64,96},{96,64},{1,33},{33,1},{65,97},{97,65},{2,34}... | collective-permute-start | bytes 688136 | tf_op jit(solution)/shard_map/ppermute | solution.py:17
  26.0 42.0 %collective-permute-start.4 = (bf16[448,896]{1,0:T(8,128)(2,1)S(1)}, bf16[448,896]{1,0:T(8,128)(2,1)}, u32[]{:S(2)}, u32[]{:S(2)}) collective-permute-start(bf16[448,896]{1,0:T(8,128)(2,1)S(1)} %maximum_select_fusion.6), channel_id=1, source_target_pairs={{0,96},{96,0},{32,64},{64,32},{1,97},{97,1},{33,65},{65,33},{2,98}... | collective-permute-start | bytes 2408456 | tf_op jit(solution)/shard_map/ppermute | solution.py:17
  38.6 16.7 %copy-start.7 = (bf16[896,256]{1,0:T(8,128)(2,1)}, bf16[896,256]{1,0:T(8,128)(2,1)S(1)}, u32[]{:S(2)}) copy-start(bf16[896,256]{1,0:T(8,128)(2,1)S(1)} %convolution_convert_fusion.2) | copy-start | bytes 1376260
  55.3 12.6 %collective-permute-start.5 = (bf16[896,128]{1,0:T(8,128)(2,1)S(1)}, bf16[896,128]{1,0:T(8,128)(2,1)S(1)}, u32[]{:S(2)}, u32[]{:S(2)}) collective-permute-start(bf16[896,128]{1,0:T(8,128)(2,1)S(1)} %select_convert_fusion), channel_id=1, source_target_pairs={{0,96},{96,0},{32,64},{64,32},{1,97},{97,1},{33,65},{65,33},{2,98}... | collective-permute-start | bytes 688136 | tf_op jit(solution)/shard_map/ppermute | solution.py:17
  64.7 15.6 %collective-permute-start.7 = (bf16[256,896]{1,0:T(8,128)(2,1)S(1)}, bf16[256,896]{1,0:T(8,128)(2,1)S(1)}, u32[]{:S(2)}, u32[]{:S(2)}) collective-permute-start(bf16[256,896]{1,0:T(8,128)(2,1)S(1)} %maximum_select_fusion.9), channel_id=1, source_target_pairs={{0,96},{96,0},{32,64},{64,32},{1,97},{97,1},{33,65},{65,33},{2,98}... | collective-permute-start | bytes 1376264 | tf_op jit(solution)/shard_map/ppermute | solution.py:17
  70.0 59.1 %copy-start.6 = (bf16[896,128]{1,0:T(8,128)(2,1)}, bf16[896,128]{1,0:T(8,128)(2,1)S(1)}, u32[]{:S(2)}) copy-start(bf16[896,128]{1,0:T(8,128)(2,1)S(1)} %convolution_convert_fusion.6) | copy-start | bytes 688132
  80.8 48.3 %copy-start.1 = (bf16[512,512]{1,0:T(8,128)(2,1)S(1)}, bf16[512,512]{1,0:T(8,128)(2,1)}, u32[]{:S(2)}) copy-start(bf16[512,512]{1,0:T(8,128)(2,1)} %param.16) | copy-start | bytes 1572868
  130.8 12.3 %copy-start.5 = (bf16[1,448,896]{2,1,0:T(8,128)(2,1)S(1)}, bf16[1,448,896]{2,1,0:T(8,128)(2,1)}, u32[]{:S(2)}) copy-start(bf16[1,448,896]{2,1,0:T(8,128)(2,1)} %param.12) | copy-start | bytes 2408452
  133.1 27.6 %copy-start.3 = (bf16[1,1,384,384]{3,2,1,0:T(8,128)(2,1)S(1)}, bf16[1,1,384,384]{3,2,1,0:T(8,128)(2,1)}, u32[]{:S(2)}) copy-start(bf16[1,1,384,384]{3,2,1,0:T(8,128)(2,1)} %param.10) | copy-start | bytes 884740
  133.1 10.0 %collective-permute-start.8 = (bf16[896,128]{0,1:T(8,128)(2,1)S(1)}, bf16[896,128]{0,1:T(8,128)(2,1)S(1)}, u32[]{:S(2)}, u32[]{:S(2)}) collective-permute-start(bf16[896,128]{0,1:T(8,128)(2,1)S(1)} %convolution_convert_fusion.5), channel_id=1, source_target_pairs={{0,96},{96,0},{32,64},{64,32},{1,97},{97,1},{33,65},{65,33},{2,98}... | collective-permute-start | bytes 688136 | tf_op jit(solution)/shard_map/ppermute | solution.py:17
  147.9 12.8 %collective-permute-start.9 = (bf16[896,256]{0,1:T(8,128)(2,1)S(1)}, bf16[896,256]{0,1:T(8,128)(2,1)S(1)}, u32[]{:S(2)}, u32[]{:S(2)}) collective-permute-start(bf16[896,256]{0,1:T(8,128)(2,1)S(1)} %convolution_convert_fusion.1), channel_id=1, source_target_pairs={{0,32},{32,0},{64,96},{96,64},{1,33},{33,1},{65,97},{97,65},{2,34}... | collective-permute-start | bytes 1376264 | tf_op jit(solution)/shard_map/ppermute | solution.py:17

commit v2 on v1

v2 whole, which is shorter than its diff:
```python
import jax
import jax.numpy as jnp
from jax import lax
from jax.experimental import pallas as pl
from jax.experimental.pallas import tpu as pltpu
from jax.sharding import Mesh
from jax.sharding import PartitionSpec as P


AXES = ("zl", "x", "y", "zh", "c")
GROUP = ("zl", "y", "zh", "c")
NEAR = [(0, 1), (1, 0), (2, 3), (3, 2)]
NEXT = [(0, 3), (3, 0), (1, 2), (2, 1)]
ACROSS = [(0, 2), (2, 0), (1, 3), (3, 1)]
DOWN = [(0, 1), (2, 3)]
BF = jnp.bfloat16
F32 = jnp.float32

LANES = 128


def send(x, pairs):
    return lax.ppermute(x, "x", pairs)


def to_group(tiles):
    return lax.all_to_all(tiles, GROUP, split_axis=0, concat_axis=0, tiled=True)


def mul(a, b):
    return jnp.dot(a, b, preferred_element_type=F32)


def mul_t(a, b):
    return lax.dot_general(a, b, (((0,), (0,)), ((), ())), preferred_element_type=F32)


def call(kernel, outs, scratch, *args, flops=0):
    moved = sum(a.size * a.dtype.itemsize for a in args)
    space = pl.BlockSpec(memory_space=pltpu.VMEM)
    return pl.pallas_call(
        kernel,
        out_shape=[jax.ShapeDtypeStruct(s, d) for s, d in outs],
        in_specs=[
            pl.BlockSpec(memory_space=pltpu.SMEM) if a.dtype == jnp.int32 else space
            for a in args
        ],
        out_specs=[space] * len(outs),
        scratch_shapes=[pltpu.VMEM(s, d) for s, d in scratch],
        compiler_params=pltpu.CompilerParams(vmem_limit_bytes=24 << 20),
        cost_estimate=pl.CostEstimate(flops=flops, bytes_accessed=moved, transcendentals=0),
    )(*args)


def others(x):
    return x ^ 1, 3 - x, x ^ 2


def leaf_kernel(loads, inv, coup, fwd, top, bot):
    fwd[...] = mul(inv[...], loads[...]).astype(BF)
    half = top.shape[0]
    top[...] = mul(coup[:half], fwd[...]).astype(BF)
    bot[...] = mul(coup[half:], fwd[...]).astype(BF)


def first_kernel(at, inv, top, bot, came_top, came_bot, coup, came_coup, pack, own, near, nxt, far, rhs, held):
    x = at[0]
    high = x % 2
    half, sep = inv.shape
    ports = top.shape[1]
    width = held.shape[0]
    rhs[:half] = (-(top[...].astype(F32) + came_top[...].astype(F32))).astype(BF)
    rhs[half:] = (-(bot[...].astype(F32) + came_bot[...].astype(F32))).astype(BF)
    fwd = mul(inv[...], rhs[...]).astype(BF)
    pack[:, :sep] = inv[...]
    pack[:, sep + sep - width :] = fwd
    pad = width - half
    held[:pad] = jnp.zeros((pad, ports), BF)
    held[half:] = jnp.zeros((pad, ports), BF)
    start = pl.multiple_of(high * pad, pad)
    held[pl.ds(start, half)] = fwd
    lane = pl.multiple_of(high * (sep - width), LANES)
    rest = pl.multiple_of(high * width, LANES)
    pack[:, sep : sep + sep - width] = coup[:, pl.ds(rest, sep - width)]
    mine = coup[:, pl.ds(lane, width)]
    mine_at = pl.multiple_of(high * half, half)
    other_at = pl.multiple_of((1 - high) * half, half)
    share = own.shape[1]
    for ref, who in zip((far, nxt, near, own), others(x)[::-1] + (x,)):
        cols = held[:, pl.ds(pl.multiple_of(who * share, LANES), share)]
        ref[pl.ds(mine_at, half)] = mul(mine, cols).astype(BF)
        ref[pl.ds(other_at, half)] = mul(came_coup[...], cols).astype(BF)


def pieces(x, refs):
    return zip((x,) + others(x), refs)


def second_kernel(at, rows, own, near, nxt, far, w0, w1, w2, w3, fwd, tiles, rhs):
    x = at[0]
    total = own[...].astype(F32) + near[...].astype(F32)
    total = total + (nxt[...].astype(F32) + far[...].astype(F32))
    rhs[...] = (-total).astype(BF)
    each = rhs.shape[0] // 4
    for who, ref in pieces(x, (w0, w1, w2, w3)):
        fwd[pl.ds(pl.multiple_of(who * each, each), each)] = mul(ref[:each], rhs[...]).astype(BF)
    for who, ref in pieces(x, (w0, w1, w2, w3)):
        count = ref.shape[0] - each
        first = pl.multiple_of(who * count, count)
        part = mul(ref[each:], fwd[...])
        live = lax.broadcasted_iota(jnp.int32, part.shape, 0) + first < rows[0]
        tiles[pl.ds(first, count)] = jnp.where(live, part, 0.0).astype(BF)


def border_kernel(at, rows, rhs, inv, fwd, w0, w1, w2, w3, back, sol):
    x = at[0]
    mid = mul(inv[...], rhs[...]).astype(BF)
    end = mul_t(inv[...], mid)
    live = lax.broadcasted_iota(jnp.int32, end.shape, 0) < rows[0]
    sol[...] = jnp.where(live, end, 0.0).astype(BF)
    each = fwd.shape[0] // 4
    diff = fwd[...].astype(F32)
    for who, ref in pieces(x, (w0, w1, w2, w3)):
        count = ref.shape[0] - each
        diff = diff - mul_t(ref[each:], sol[pl.ds(pl.multiple_of(who * count, count), count)])
    fwd_ref = back
    fwd_ref[...] = diff.astype(BF)
    total = None
    for who, ref in pieces(x, (w0, w1, w2, w3)):
        term = mul_t(ref[:each], fwd_ref[pl.ds(pl.multiple_of(who * each, each), each)])
        total = term if total is None else total + term
    back[...] = total.astype(BF)


def fold_kernel(at, pack, came, coup, came_coup, leaf_coup, fwd_leaf, fold, rest, full):
    high = at[0] % 2
    half, sep = coup.shape
    width = came_coup.shape[1]
    mine_at = pl.multiple_of(high * half, half)
    other_at = pl.multiple_of((1 - high) * half, half)
    mine = mul(pack[:, :sep], leaf_coup[...]).astype(BF)
    other = mul(came[:, :sep], leaf_coup[...]).astype(BF)
    full[pl.ds(mine_at, half)] = mine
    full[pl.ds(other_at, half)] = other
    rest[...] = (
        fwd_leaf[...].astype(F32)
        - mul_t(mine, pack[:, sep + sep - width :])
        - mul_t(other, came[:, sep + sep - width :])
    )
    fold[pl.ds(mine_at, half)] = mul(coup[...], full[...]).astype(BF)
    win = pl.multiple_of(high * (sep - width), LANES)
    out = pl.multiple_of((1 - high) * width, LANES)
    fold[pl.ds(other_at, half)] = (
        mul(came_coup[...], full[pl.ds(win, width)])
        + mul(came[:, sep : sep + sep - width], full[pl.ds(out, sep - width)])
    ).astype(BF)


def last_kernel(at, fold, rest, own, near, nxt, far, inv, out, diff):
    share = own.shape[1]
    for who, ref in pieces(at[0], (own, near, nxt, far)):
        cols = pl.ds(pl.multiple_of(who * share, LANES), share)
        diff[:, cols] = (rest[:, cols] + mul_t(fold[...], ref[...])).astype(BF)
    out[...] = mul_t(inv[...], diff[...]).astype(BF)


def per_device(
    port_loads,
    leaf_inverse,
    leaf_coupling,
    first_inverse,
    second_coupling,
    second_inverse,
    border_coupling,
    border_inverse,
    border_rows,
):
    x = lax.axis_index("x")
    at = x.astype(jnp.int32)[None]
    low = x % 2 == 0
    group = lax.axis_size(GROUP)
    loads, leaf_inv, leaf_coup = port_loads[0, 0], leaf_inverse[0, 0], leaf_coupling[0, 0]
    inv_one, coup_two = first_inverse[0], second_coupling[0]
    half, sep = inv_one.shape
    leaf, ports = loads.shape
    share = ports // 4
    width = -(-half // LANES) * LANES
    border = border_inverse.shape[0]

    window = jnp.where(low, coup_two[:, sep - width :], coup_two[:, :width])
    came_coup = send(window, NEAR)
    block = jnp.concatenate([second_inverse[0], border_coupling[0]], 0)
    w_next = send(block, NEXT)
    fwd_leaf, top, bot = call(
        leaf_kernel,
        [((leaf, ports), BF), ((half, ports), BF), ((half, ports), BF)],
        [],
        loads,
        leaf_inv,
        leaf_coup,
        flops=2 * leaf * ports * (leaf + sep),
    )
    came_top = send(top, NEAR)
    came_bot = send(bot, DOWN)
    late_block, came_top = lax.optimization_barrier((block, came_top))
    w_near = send(late_block, NEAR)
    w_far = send(w_near, NEXT)
    quarter = ((sep, share), BF)
    pack, own, near, nxt, far = call(
        first_kernel,
        [((half, 2 * sep - width + ports), BF)] + [quarter] * 4,
        [((sep, ports), BF), ((width, ports), BF)],
        at,
        inv_one,
        top,
        bot,
        came_top,
        came_bot,
        coup_two,
        came_coup,
        flops=2 * half * ports * sep + 2 * sep * ports * width,
    )
    far = send(far, ACROSS)
    nxt = send(nxt, NEXT)
    near = send(near, NEAR)
    late_pack, near = lax.optimization_barrier((pack, near))
    came_pack = send(late_pack, NEAR)
    blocks = (block, w_near, w_next, w_far)
    fwd_two, tiles = call(
        second_kernel,
        [quarter, ((border, share), BF)],
        [quarter],
        at,
        border_rows,
        own,
        near,
        nxt,
        far,
        *blocks,
        flops=2 * sep * share * (sep + border),
    )
    tiles = tiles.reshape(group, border // group, share)
    share_sum = jnp.sum(to_group(tiles).astype(F32), axis=0)
    rhs_share = (-share_sum).astype(BF)
    rhs_border = to_group(jnp.broadcast_to(rhs_share, tiles.shape)).reshape(border, share)
    (back_two,) = call(
        border_kernel,
        [quarter],
        [((border, share), BF)],
        at,
        border_rows,
        rhs_border,
        border_inverse,
        fwd_two,
        *blocks,
        flops=2 * share * (2 * border * border + border * sep + sep * sep),
    )
    back_far = send(back_two, ACROSS)
    back_next = send(back_two, NEXT)
    back_near = send(back_two, NEAR)
    pack, came_pack, back_two = lax.optimization_barrier((pack, came_pack, back_two))
    fold, rest = call(
        fold_kernel,
        [((sep, leaf), BF), ((leaf, ports), F32)],
        [((sep, leaf), BF)],
        at,
        pack,
        came_pack,
        coup_two,
        came_coup,
        leaf_coup,
        fwd_leaf,
        flops=2 * sep * leaf * (2 * sep + ports),
    )
    (out,) = call(
        last_kernel,
        [((leaf, ports), BF)],
        [((leaf, ports), BF)],
        at,
        fold,
        rest,
        back_two,
        back_near,
        back_next,
        back_far,
        leaf_inv,
        flops=2 * leaf * ports * (sep + leaf),
    )
    return out[None, None]


def solution(mesh):
    split = Mesh(mesh.devices.reshape(4, 4, 8, 2, 2), AXES)
    reg, sub = ("y", "zh", "c"), ("zl", "x")
    return jax.shard_map(
        per_device,
        mesh=split,
        in_specs=(P(reg, sub),) * 7 + (P(None, None), P(reg)),
        out_specs=P(reg, sub),
        check_vma=False,
    )
```

time: 163 us -> 172 us (1.055)
  matrix products: 20.5 us -> 0 us
  starting transfers between devices: 41 us -> 52.2 us
  Pallas kernels: 0 us -> 10.1 us
  waiting for transfers between devices: 50.6 us -> 55.7 us
  local copies, waits for them, and re-layouts: 1.02 us -> 3.2 us
    dot_general x11 -> x0, matrix products: 20.5 us -> none  [the longest x7 11 us: product(): return jnp.dot(matrix, vector, preferred_element_type=jnp.float32)]
    ppermute x10 -> x13, starting transfers between devices: 41 us -> 52.2 us  [send(): return lax.ppermute(x, 'x', pairs)]
    pallas_call x0 -> x6, Pallas kernels: none -> 10.1 us  [call(): pl.pallas_call(kernel, out_shape=[jax.ShapeDtypeStruct(s, d) for s, d in...]
    ppermute x10 -> x13, waiting for transfers between devices: 50.6 us -> 55.7 us  [send(): return lax.ppermute(x, 'x', pairs)]
    unnamed x16 -> x20, local copies, waits for them, and re-layouts: 0.04 us -> 3.16 us
  transfers between devices with their start and end apart: 10 -> 13, of which waited for: 7 -> 7; matrix products, arithmetic and copies ran while one was open for 7% -> 0% of each run, Pallas kernels for 0% -> 4%
where the time goes in v2:
time: 172 us; the launch traced here: 171 us
  waiting for transfers between devices  55.7 us (32%)
  starting transfers between devices  52.2 us (30%)
  blocking collectives  48.9 us (28%)
  Pallas kernels  10.1 us (6%)
  local copies, waits for them, and re-layouts  3.2 us (2%)
    ppermute x13, waiting for transfers between devices, send(): return lax.ppermute(x, 'x', pairs)  55.7 us
    ppermute x13, starting transfers between devices, send(): return lax.ppermute(x, 'x', pairs)  52.2 us
    all_to_all x2, blocking collectives, to_group(): return lax.all_to_all(tiles, GROUP, split_axis=0, concat_axis=0, tiled=True)  48.9 us
    pallas_call x6, Pallas kernels, call(): pl.pallas_call(kernel, out_shape=[jax.ShapeDtypeStruct(s, d) for s, d in...  10.1 us
  transfers between devices with their start and end apart: 13, of which 7 were waited for; matrix products, arithmetic and copies ran while one was open for 0% of the time, Pallas kernels for 4%

profile of v2, /device:TPU:1, one launch (start us, length us, event | category | flops | bytes accessed | tf_op | source)
XLA Modules:
  0.0 171.2 jit_solution(18412949659959665948)
XLA Ops:
  0.0 1.0 copy-done.3
  1.0 1.1 copy-done.5
  2.1 1.0 copy-done.7
  3.1 0.9 shard_map.91
  4.1 3.9 %collective-permute-start = (bf16[448,512]{1,0:T(8,128)(2,1)S(1)}, bf16[448,512]{1,0:T(8,128)(2,1)S(1)}, u32[]{:S(2)}, u32[]{:S(2)}) collective-permute-start(bf16[448,512]{1,0:T(8,128)(2,1)S(1)} %get-tuple-element.24.top), channel_id=1, source_target_pairs={{0,32},{32,0},{64,96},{96,64},{1,33},{33,1},{65,97},{97,65},{2,34}... | collective-permute-start | bytes 1376264 | tf_op jit(solution)/shard_map/ppermute | solution.py:23
  8.0 0.0 copy-done
  8.1 0.0 copy-start.1
  8.1 0.1 slice_select_fusion
  8.1 2.1 %collective-permute-start.2 = (bf16[448,512]{1,0:T(8,128)(2,1)S(1)}, bf16[448,512]{1,0:T(8,128)(2,1)S(1)}, u32[]{:S(2)}, u32[]{:S(2)}) collective-permute-start(bf16[448,512]{1,0:T(8,128)(2,1)S(1)} %slice_select_fusion), channel_id=1, source_target_pairs={{0,32},{32,0},{64,96},{96,64},{1,33},{33,1},{65,97},{97,65},{2,34}... | collective-permute-start | bytes 1376264 | tf_op jit(solution)/shard_map/ppermute | solution.py:23
  10.2 3.4 %collective-permute-start.1 = (bf16[448,512]{1,0:T(8,128)(2,1)S(1)}, bf16[448,512]{1,0:T(8,128)(2,1)S(1)}, u32[]{:S(2)}, u32[]{:S(2)}) collective-permute-start(bf16[448,512]{1,0:T(8,128)(2,1)S(1)} %get-tuple-element.25.bot), channel_id=1, source_target_pairs={{0,32},{64,96},{1,33},{65,97},{2,34},{66,98},{3,35},{67,99},{4,36}... | collective-permute-start | bytes 1376264 | tf_op jit(solution)/shard_map/ppermute | solution.py:23
  13.6 0.0 copy-done.8
  13.6 0.0 copy-done.9
  13.6 0.1 pad_maximum_fusion.w0
  13.7 0.2 collective-permute-done.came_top
  13.9 3.4 %collective-permute-start.7 = (bf16[352,896]{1,0:T(8,128)(2,1)S(1)}, bf16[352,896]{1,0:T(8,128)(2,1)S(1)}, u32[]{:S(2)}, u32[]{:S(2)}) collective-permute-start(bf16[352,896]{1,0:T(8,128)(2,1)S(1)} %pad_maximum_fusion.w0), channel_id=1, source_target_pairs={{0,32},{32,0},{64,96},{96,64},{1,33},{33,1},{65,97},{97,65},{2,34}... | collective-permute-start | bytes 1892360 | tf_op jit(solution)/shard_map/ppermute | solution.py:23
  17.2 5.9 %collective-permute-done.2.came_coup = bf16[448,512]{1,0:T(8,128)(2,1)S(1)} collective-permute-done((bf16[448,512]{1,0:T(8,128)(2,1)S(1)}, bf16[448,512]{1,0:T(8,128)(2,1)S(1)}, u32[]{:S(2)}, u32[]{:S(2)}) %collective-permute-start.2) | collective-permute-done | bytes 458784 | tf_op jit(solution)/shard_map/ppermute | solution.py:23
  23.2 9.8 %collective-permute-done.1.came_bot = bf16[448,512]{1,0:T(8,128)(2,1)S(1)} collective-permute-done((bf16[448,512]{1,0:T(8,128)(2,1)S(1)}, bf16[448,512]{1,0:T(8,128)(2,1)S(1)}, u32[]{:S(2)}, u32[]{:S(2)}) %collective-permute-start.1) | collective-permute-done | bytes 458784 | tf_op jit(solution)/shard_map/ppermute | solution.py:23
  33.0 0.0 copy-done.1
  33.0 1.8 %shard_map.92 = (bf16[448,1792]{1,0:T(8,128)(2,1)S(1)}, bf16[896,128]{1,0:T(8,128)(2,1)S(1)}, bf16[896,128]{1,0:T(8,128)(2,1)S(1)}, bf16[896,128]{1,0:T(8,128)(2,1)S(1)}, bf16[896,128]{1,0:T(8,128)(2,1)S(1)}) custom-call(s32[1]{0:T(128)} %bitcast.at, bf16[448,896]{1,0:T(8,128)(2,1)S(1)} %bitcast.14, bf16[448,512]{1,0:T(8,128)(2,1)S(1)} %get-tuple-element.24.top, ...), custom_call_target="tpu_custom_call" | custom-call | flops 880803840 | bytes 3899396 | tf_op jit(solution)/shard_map/pallas_call | solution.py:41
  34.9 4.1 %collective-permute-start.3 = (bf16[896,128]{1,0:T(8,128)(2,1)S(1)}, bf16[896,128]{1,0:T(8,128)(2,1)S(1)}, u32[]{:S(2)}, u32[]{:S(2)}) collective-permute-start(bf16[896,128]{1,0:T(8,128)(2,1)S(1)} %get-tuple-element.28), channel_id=1, source_target_pairs={{0,32},{32,0},{64,96},{96,64},{1,33},{33,1},{65,97},{97,65},{2,34}... | collective-permute-start | bytes 688136 | tf_op jit(solution)/shard_map/ppermute | solution.py:23
  39.0 7.0 %collective-permute-start.8 = (bf16[352,896]{1,0:T(8,128)(2,1)S(1)}, bf16[352,896]{1,0:T(8,128)(2,1)S(1)}, u32[]{:S(2)}, u32[]{:S(2)}) collective-permute-start(bf16[352,896]{1,0:T(8,128)(2,1)S(1)} %pad_maximum_fusion.w0), channel_id=1, source_target_pairs={{0,96},{96,0},{32,64},{64,32},{1,97},{97,1},{33,65},{65,33},{2,98}... | collective-permute-start | bytes 1892360 | tf_op jit(solution)/shard_map/ppermute | solution.py:23
  46.0 0.5 collective-permute-done.7.w1
  46.5 9.2 %collective-permute-start.9 = (bf16[352,896]{1,0:T(8,128)(2,1)S(1)}, bf16[352,896]{1,0:T(8,128)(2,1)S(1)}, u32[]{:S(2)}, u32[]{:S(2)}) collective-permute-start(bf16[352,896]{1,0:T(8,128)(2,1)S(1)} %collective-permute-done.7.w1), channel_id=1, source_target_pairs={{0,96},{96,0},{32,64},{64,32},{1,97},{97,1},{33,65},{65,33},{2,98}... | collective-permute-start | bytes 1892360 | tf_op jit(solution)/shard_map/ppermute | solution.py:23
  55.8 0.0 collective-permute-done.3.near
  55.8 1.9 %collective-permute-start.4 = (bf16[448,1792]{1,0:T(8,128)(2,1)S(1)}, bf16[448,1792]{1,0:T(8,128)(2,1)S(1)}, u32[]{:S(2)}, u32[]{:S(2)}) collective-permute-start(bf16[448,1792]{1,0:T(8,128)(2,1)S(1)} %get-tuple-element.37.pack), channel_id=1, source_target_pairs={{0,32},{32,0},{64,96},{96,64},{1,33},{33,1},{65,97},{97,65},{2,34}... | collective-permute-start | bytes 4816904 | tf_op jit(solution)/shard_map/ppermute | solution.py:23
  57.7 4.9 %collective-permute-start.5 = (bf16[896,128]{1,0:T(8,128)(2,1)S(1)}, bf16[896,128]{1,0:T(8,128)(2,1)S(1)}, u32[]{:S(2)}, u32[]{:S(2)}) collective-permute-start(bf16[896,128]{1,0:T(8,128)(2,1)S(1)} %get-tuple-element.32), channel_id=1, source_target_pairs={{0,96},{96,0},{32,64},{64,32},{1,97},{97,1},{33,65},{65,33},{2,98}... | collective-permute-start | bytes 688136 | tf_op jit(solution)/shard_map/ppermute | solution.py:23
  62.6 3.1 %collective-permute-start.6 = (bf16[896,128]{1,0:T(8,128)(2,1)S(1)}, bf16[896,128]{1,0:T(8,128)(2,1)S(1)}, u32[]{:S(2)}, u32[]{:S(2)}) collective-permute-start(bf16[896,128]{1,0:T(8,128)(2,1)S(1)} %get-tuple-element.33), channel_id=1, source_target_pairs={{0,64},{64,0},{32,96},{96,32},{1,65},{65,1},{33,97},{97,33},{2,66}... | collective-permute-start | bytes 688136 | tf_op jit(solution)/shard_map/ppermute | solution.py:23
  66.3 0.0 collective-permute-done.8.w2
  66.4 9.1 %collective-permute-done.5.nxt = bf16[896,128]{1,0:T(8,128)(2,1)S(1)} collective-permute-done((bf16[896,128]{1,0:T(8,128)(2,1)S(1)}, bf16[896,128]{1,0:T(8,128)(2,1)S(1)}, u32[]{:S(2)}, u32[]{:S(2)}) %collective-permute-start.5) | collective-permute-done | bytes 229408 | tf_op jit(solution)/shard_map/ppermute | solution.py:23
  75.4 25.0 %collective-permute-done.6.far = bf16[896,128]{1,0:T(8,128)(2,1)S(1)} collective-permute-done((bf16[896,128]{1,0:T(8,128)(2,1)S(1)}, bf16[896,128]{1,0:T(8,128)(2,1)S(1)}, u32[]{:S(2)}, u32[]{:S(2)}) %collective-permute-start.6) | collective-permute-done | bytes 229408 | tf_op jit(solution)/shard_map/ppermute | solution.py:23
  100.4 0.0 collective-permute-done.9.w3
  100.4 1.1 shard_map.93
  101.5 31.4 %all_to_all.10 = bf16[128,4,128]{2,1,0:T(4,128)(2,1)S(1)} all-to-all(bf16[128,4,128]{2,1,0:T(4,128)(2,1)S(1)} %bitcast.18), channel_id=1, replica_groups=mesh['zl'=4,'x'=4,'y'=8,'zh'=2,'c'=2] {'zl','y','zh','c'}, dimensions={0} | all-to-all | bytes 262144 | tf_op jit(solution)/shard_map/all_to_all | solution.py:27
  132.9 0.1 convert_reduce_fusion
  133.1 17.5 %all_to_all.11 = bf16[128,4,128]{2,1,0:T(4,128)(2,1)S(1)} all-to-all(bf16[128,4,128]{2,1,0:T(4,128)(2,1)S(1)} %broadcast_in_dim.10), channel_id=1, replica_groups=mesh['zl'=4,'x'=4,'y'=8,'zh'=2,'c'=2] {'zl','y','zh','c'}, dimensions={0} | all-to-all | bytes 262144 | tf_op jit(solution)/shard_map/all_to_all | solution.py:27
  150.6 0.0 copy-done.2
  150.6 1.8 %shard_map.94.own = bf16[896,128]{1,0:T(8,128)(2,1)S(1)} custom-call(s32[1]{0:T(128)} %bitcast.at, s32[1]{0:T(128)S(6)} %copy.10.rows, bf16[512,128]{1,0:T(8,128)(2,1)S(1)} %bitcast.15, bf16[512,512]{1,0:T(8,128)(2,1)S(1)} %copy-done.2, bf16[896,128]{1,0:T(8,128)(2,1)S(1)} %get-tuple-element.36.fwd, bf16[352,896]{1,0:T(8,128)(2,1)S(1)} %pad_maximum_fusion.w0, ...), custom_call_target="tpu_custom_call" | custom-call | flops 457179136 | bytes 3407880 | tf_op jit(solution)/shard_map/pallas_call | solution.py:41
  152.4 1.9 %collective-permute-start.10 = (bf16[896,128]{1,0:T(8,128)(2,1)S(1)}, bf16[896,128]{1,0:T(8,128)(2,1)S(1)}, u32[]{:S(2)}, u32[]{:S(2)}) collective-permute-start(bf16[896,128]{1,0:T(8,128)(2,1)S(1)} %shard_map.94.own), channel_id=1, source_target_pairs={{0,32},{32,0},{64,96},{96,64},{1,33},{33,1},{65,97},{97,65},{2,34}... | collective-permute-start | bytes 688136 | tf_op jit(solution)/shard_map/ppermute | solution.py:23
  154.3 2.7 %collective-permute-start.11 = (bf16[896,128]{1,0:T(8,128)(2,1)S(1)}, bf16[896,128]{1,0:T(8,128)(2,1)S(1)}, u32[]{:S(2)}, u32[]{:S(2)}) collective-permute-start(bf16[896,128]{1,0:T(8,128)(2,1)S(1)} %shard_map.94.own), channel_id=1, source_target_pairs={{0,96},{96,0},{32,64},{64,32},{1,97},{97,1},{33,65},{65,33},{2,98}... | collective-permute-start | bytes 688136 | tf_op jit(solution)/shard_map/ppermute | solution.py:23
  157.0 4.5 %collective-permute-start.12 = (bf16[896,128]{1,0:T(8,128)(2,1)S(1)}, bf16[896,128]{1,0:T(8,128)(2,1)S(1)}, u32[]{:S(2)}, u32[]{:S(2)}) collective-permute-start(bf16[896,128]{1,0:T(8,128)(2,1)S(1)} %shard_map.94.own), channel_id=1, source_target_pairs={{0,64},{64,0},{32,96},{96,32},{1,65},{65,1},{33,97},{97,33},{2,66}... | collective-permute-start | bytes 688136 | tf_op jit(solution)/shard_map/ppermute | solution.py:23
  161.6 0.0 collective-permute-done.4.came
  161.6 0.0 copy-done.6
  161.6 0.0 copy-start.4
  161.6 2.4 %shard_map.95 = (bf16[896,384]{1,0:T(8,128)(2,1)S(1)}, f32[384,512]{1,0:T(8,128)S(1)}) custom-call(s32[1]{0:T(128)} %bitcast.at, bf16[448,1792]{1,0:T(8,128)(2,1)S(1)} %get-tuple-element.37.pack, bf16[448,1792]{1,0:T(8,128)(2,1)S(1)} %collective-permute-done.4.came, bf16[448,896]{1,0:T(8,128)(2,1)S(1)} %bitcast.13, ...), custom_call_target="tpu_custom_call" | custom-call | flops 1585446912 | bytes 5554180 | tf_op jit(solution)/shard_map/pallas_call | solution.py:41
  164.0 0.0 collective-permute-done.10.near
  164.0 5.1 %collective-permute-done.11.nxt = bf16[896,128]{1,0:T(8,128)(2,1)S(1)} collective-permute-done((bf16[896,128]{1,0:T(8,128)(2,1)S(1)}, bf16[896,128]{1,0:T(8,128)(2,1)S(1)}, u32[]{:S(2)}, u32[]{:S(2)}) %collective-permute-start.11) | collective-permute-done | bytes 229408 | tf_op jit(solution)/shard_map/ppermute | solution.py:23
  169.2 0.0 collective-permute-done.12.far
  169.2 2.1 %shard_map.96 = bf16[384,512]{1,0:T(8,128)(2,1)} custom-call(s32[1]{0:T(128)} %bitcast.at, bf16[896,384]{1,0:T(8,128)(2,1)S(1)} %get-tuple-element.40.fold, f32[384,512]{1,0:T(8,128)S(1)} %get-tuple-element.41.rest, bf16[896,128]{1,0:T(8,128)(2,1)S(1)} %shard_map.94.own, bf16[896,128]{1,0:T(8,128)(2,1)S(1)} %collective-permute-done.10.near, ...), custom_call_target="tpu_custom_call" | custom-call | flops 503316480 | bytes 2686980 | tf_op jit(solution)/shard_map/pallas_call | solution.py:41
  (11 shorter events, 0.1 us)
Async XLA Ops:
  0.0 8.0 %copy-start = (bf16[1,448,896]{2,1,0:T(8,128)(2,1)S(1)}, bf16[1,448,896]{2,1,0:T(8,128)(2,1)}, u32[]{:S(2)}) copy-start(bf16[1,448,896]{2,1,0:T(8,128)(2,1)} %param.13) | copy-start | bytes 2408452
  0.0 1.0 copy-start.3
  1.0 1.1 copy-start.5
  2.1 1.0 copy-start.7
  3.1 10.5 %copy-start.8 = (bf16[1,224,896]{2,1,0:T(8,128)(2,1)S(1)}, bf16[1,224,896]{2,1,0:T(8,128)(2,1)}, u32[]{:S(2)}) copy-start(bf16[1,224,896]{2,1,0:T(8,128)(2,1)} %param.14) | copy-start | bytes 1204228
  3.1 10.5 %copy-start.9 = (bf16[1,128,896]{2,1,0:T(8,128)(2,1)S(1)}, bf16[1,128,896]{2,1,0:T(8,128)(2,1)}, u32[]{:S(2)}) copy-start(bf16[1,128,896]{2,1,0:T(8,128)(2,1)} %param.15) | copy-start | bytes 688132
  4.1 9.8 %collective-permute-start = (bf16[448,512]{1,0:T(8,128)(2,1)S(1)}, bf16[448,512]{1,0:T(8,128)(2,1)S(1)}, u32[]{:S(2)}, u32[]{:S(2)}) collective-permute-start(bf16[448,512]{1,0:T(8,128)(2,1)S(1)} %get-tuple-element.24.top), channel_id=1, source_target_pairs={{0,32},{32,0},{64,96},{96,64},{1,33},{33,1},{65,97},{97,65},{2,34}... | collective-permute-start | bytes 1376264 | tf_op jit(solution)/shard_map/ppermute | solution.py:23
  8.1 24.9 %copy-start.1 = (bf16[1,448,896]{2,1,0:T(8,128)(2,1)S(1)}, bf16[1,448,896]{2,1,0:T(8,128)(2,1)}, u32[]{:S(2)}) copy-start(bf16[1,448,896]{2,1,0:T(8,128)(2,1)} %param.12) | copy-start | bytes 2408452
  8.1 15.0 %collective-permute-start.2 = (bf16[448,512]{1,0:T(8,128)(2,1)S(1)}, bf16[448,512]{1,0:T(8,128)(2,1)S(1)}, u32[]{:S(2)}, u32[]{:S(2)}) collective-permute-start(bf16[448,512]{1,0:T(8,128)(2,1)S(1)} %slice_select_fusion), channel_id=1, source_target_pairs={{0,32},{32,0},{64,96},{96,64},{1,33},{33,1},{65,97},{97,65},{2,34}... | collective-permute-start | bytes 1376264 | tf_op jit(solution)/shard_map/ppermute | solution.py:23
  10.2 22.8 %collective-permute-start.1 = (bf16[448,512]{1,0:T(8,128)(2,1)S(1)}, bf16[448,512]{1,0:T(8,128)(2,1)S(1)}, u32[]{:S(2)}, u32[]{:S(2)}) collective-permute-start(bf16[448,512]{1,0:T(8,128)(2,1)S(1)} %get-tuple-element.25.bot), channel_id=1, source_target_pairs={{0,32},{64,96},{1,33},{65,97},{2,34},{66,98},{3,35},{67,99},{4,36}... | collective-permute-start | bytes 1376264 | tf_op jit(solution)/shard_map/ppermute | solution.py:23
  13.9 32.6 %collective-permute-start.7 = (bf16[352,896]{1,0:T(8,128)(2,1)S(1)}, bf16[352,896]{1,0:T(8,128)(2,1)S(1)}, u32[]{:S(2)}, u32[]{:S(2)}) collective-permute-start(bf16[352,896]{1,0:T(8,128)(2,1)S(1)} %pad_maximum_fusion.w0), channel_id=1, source_target_pairs={{0,32},{32,0},{64,96},{96,64},{1,33},{33,1},{65,97},{97,65},{2,34}... | collective-permute-start | bytes 1892360 | tf_op jit(solution)/shard_map/ppermute | solution.py:23
  34.9 20.9 %collective-permute-start.3 = (bf16[896,128]{1,0:T(8,128)(2,1)S(1)}, bf16[896,128]{1,0:T(8,128)(2,1)S(1)}, u32[]{:S(2)}, u32[]{:S(2)}) collective-permute-start(bf16[896,128]{1,0:T(8,128)(2,1)S(1)} %get-tuple-element.28), channel_id=1, source_target_pairs={{0,32},{32,0},{64,96},{96,64},{1,33},{33,1},{65,97},{97,65},{2,34}... | collective-permute-start | bytes 688136 | tf_op jit(solution)/shard_map/ppermute | solution.py:23
  39.0 27.4 %collective-permute-start.8 = (bf16[352,896]{1,0:T(8,128)(2,1)S(1)}, bf16[352,896]{1,0:T(8,128)(2,1)S(1)}, u32[]{:S(2)}, u32[]{:S(2)}) collective-permute-start(bf16[352,896]{1,0:T(8,128)(2,1)S(1)} %pad_maximum_fusion.w0), channel_id=1, source_target_pairs={{0,96},{96,0},{32,64},{64,32},{1,97},{97,1},{33,65},{65,33},{2,98}... | collective-permute-start | bytes 1892360 | tf_op jit(solution)/shard_map/ppermute | solution.py:23
  46.5 53.9 %collective-permute-start.9 = (bf16[352,896]{1,0:T(8,128)(2,1)S(1)}, bf16[352,896]{1,0:T(8,128)(2,1)S(1)}, u32[]{:S(2)}, u32[]{:S(2)}) collective-permute-start(bf16[352,896]{1,0:T(8,128)(2,1)S(1)} %collective-permute-done.7.w1), channel_id=1, source_target_pairs={{0,96},{96,0},{32,64},{64,32},{1,97},{97,1},{33,65},{65,33},{2,98}... | collective-permute-start | bytes 1892360 | tf_op jit(solution)/shard_map/ppermute | solution.py:23
  55.8 105.8 %collective-permute-start.4 = (bf16[448,1792]{1,0:T(8,128)(2,1)S(1)}, bf16[448,1792]{1,0:T(8,128)(2,1)S(1)}, u32[]{:S(2)}, u32[]{:S(2)}) collective-permute-start(bf16[448,1792]{1,0:T(8,128)(2,1)S(1)} %get-tuple-element.37.pack), channel_id=1, source_target_pairs={{0,32},{32,0},{64,96},{96,64},{1,33},{33,1},{65,97},{97,65},{2,34}... | collective-permute-start | bytes 4816904 | tf_op jit(solution)/shard_map/ppermute | solution.py:23
  57.7 17.7 %collective-permute-start.5 = (bf16[896,128]{1,0:T(8,128)(2,1)S(1)}, bf16[896,128]{1,0:T(8,128)(2,1)S(1)}, u32[]{:S(2)}, u32[]{:S(2)}) collective-permute-start(bf16[896,128]{1,0:T(8,128)(2,1)S(1)} %get-tuple-element.32), channel_id=1, source_target_pairs={{0,96},{96,0},{32,64},{64,32},{1,97},{97,1},{33,65},{65,33},{2,98}... | collective-permute-start | bytes 688136 | tf_op jit(solution)/shard_map/ppermute | solution.py:23
  62.6 37.8 %collective-permute-start.6 = (bf16[896,128]{1,0:T(8,128)(2,1)S(1)}, bf16[896,128]{1,0:T(8,128)(2,1)S(1)}, u32[]{:S(2)}, u32[]{:S(2)}) collective-permute-start(bf16[896,128]{1,0:T(8,128)(2,1)S(1)} %get-tuple-element.33), channel_id=1, source_target_pairs={{0,64},{64,0},{32,96},{96,32},{1,65},{65,1},{33,97},{97,33},{2,66}... | collective-permute-start | bytes 688136 | tf_op jit(solution)/shard_map/ppermute | solution.py:23
  100.4 50.2 %copy-start.2 = (bf16[512,512]{1,0:T(8,128)(2,1)S(1)}, bf16[512,512]{1,0:T(8,128)(2,1)}, u32[]{:S(2)}) copy-start(bf16[512,512]{1,0:T(8,128)(2,1)} %inv.1) | copy-start | bytes 1572868
  150.6 11.0 %copy-start.6 = (bf16[1,1,896,384]{3,2,1,0:T(8,128)(2,1)S(1)}, bf16[1,1,896,384]{3,2,1,0:T(8,128)(2,1)}, u32[]{:S(2)}) copy-start(bf16[1,1,896,384]{3,2,1,0:T(8,128)(2,1)} %param.11) | copy-start | bytes 2064388
  152.4 11.6 %collective-permute-start.10 = (bf16[896,128]{1,0:T(8,128)(2,1)S(1)}, bf16[896,128]{1,0:T(8,128)(2,1)S(1)}, u32[]{:S(2)}, u32[]{:S(2)}) collective-permute-start(bf16[896,128]{1,0:T(8,128)(2,1)S(1)} %shard_map.94.own), channel_id=1, source_target_pairs={{0,32},{32,0},{64,96},{96,64},{1,33},{33,1},{65,97},{97,65},{2,34}... | collective-permute-start | bytes 688136 | tf_op jit(solution)/shard_map/ppermute | solution.py:23
  154.3 14.8 %collective-permute-start.11 = (bf16[896,128]{1,0:T(8,128)(2,1)S(1)}, bf16[896,128]{1,0:T(8,128)(2,1)S(1)}, u32[]{:S(2)}, u32[]{:S(2)}) collective-permute-start(bf16[896,128]{1,0:T(8,128)(2,1)S(1)} %shard_map.94.own), channel_id=1, source_target_pairs={{0,96},{96,0},{32,64},{64,32},{1,97},{97,1},{33,65},{65,33},{2,98}... | collective-permute-start | bytes 688136 | tf_op jit(solution)/shard_map/ppermute | solution.py:23
  157.0 12.1 %collective-permute-start.12 = (bf16[896,128]{1,0:T(8,128)(2,1)S(1)}, bf16[896,128]{1,0:T(8,128)(2,1)S(1)}, u32[]{:S(2)}, u32[]{:S(2)}) collective-permute-start(bf16[896,128]{1,0:T(8,128)(2,1)S(1)} %shard_map.94.own), channel_id=1, source_target_pairs={{0,64},{64,0},{32,96},{96,32},{1,65},{65,1},{33,97},{97,33},{2,66}... | collective-permute-start | bytes 688136 | tf_op jit(solution)/shard_map/ppermute | solution.py:23
  161.6 7.6 %copy-start.4 = (bf16[1,1,384,384]{3,2,1,0:T(8,128)(2,1)S(1)}, bf16[1,1,384,384]{3,2,1,0:T(8,128)(2,1)}, u32[]{:S(2)}) copy-start(bf16[1,1,384,384]{3,2,1,0:T(8,128)(2,1)} %param.10) | copy-start | bytes 884740

commit v3 on v2

--- a/solution.py
+++ b/solution.py
@@ -63,7 +63,7 @@
     bot[...] = mul(coup[half:], fwd[...]).astype(BF)
 
 
-def first_kernel(at, inv, top, bot, came_top, came_bot, coup, came_coup, pack, own, near, nxt, far, rhs, held):
+def first_kernel(at, inv, top, bot, came_top, came_bot, coup, came_coup, pack, own, near, nxt, far, rhs, held, turned):
     x = at[0]
     high = x % 2
     half, sep = inv.shape
@@ -86,10 +86,13 @@
     mine_at = pl.multiple_of(high * half, half)
     other_at = pl.multiple_of((1 - high) * half, half)
     share = own.shape[1]
-    for ref, who in zip((far, nxt, near, own), others(x)[::-1] + (x,)):
-        cols = held[:, pl.ds(pl.multiple_of(who * share, LANES), share)]
-        ref[pl.ds(mine_at, half)] = mul(mine, cols).astype(BF)
-        ref[pl.ds(other_at, half)] = mul(came_coup[...], cols).astype(BF)
+    for at_col, who in enumerate((x,) + others(x)):
+        cols = pl.ds(pl.multiple_of(who * share, LANES), share)
+        turned[:, at_col * share : (at_col + 1) * share] = held[:, cols]
+    for weights, row in ((mine, mine_at), (came_coup[...], other_at)):
+        part = mul(weights, turned[...]).astype(BF)
+        for at_col, ref in enumerate((own, near, nxt, far)):
+            ref[pl.ds(row, half)] = part[:, at_col * share : (at_col + 1) * share]
 
 
 def pieces(x, refs):
@@ -132,7 +135,7 @@
     back[...] = total.astype(BF)
 
 
-def fold_kernel(at, pack, came, coup, came_coup, leaf_coup, fwd_leaf, fold, rest, full):
+def fold_kernel(at, pack, came, coup, came_coup, leaf_coup, fwd_leaf, leaf_inv, fold_t, inv_t, rest, full, fold):
     high = at[0] % 2
     half, sep = coup.shape
     width = came_coup.shape[1]
@@ -154,14 +157,16 @@
         mul(came_coup[...], full[pl.ds(win, width)])
         + mul(came[:, sep : sep + sep - width], full[pl.ds(out, sep - width)])
     ).astype(BF)
-
-
-def last_kernel(at, fold, rest, own, near, nxt, far, inv, out, diff):
+    fold_t[...] = fold[...].T
+    inv_t[...] = leaf_inv[...].T
+
+
+def last_kernel(at, fold_t, inv_t, rest, own, near, nxt, far, out, back):
     share = own.shape[1]
     for who, ref in pieces(at[0], (own, near, nxt, far)):
-        cols = pl.ds(pl.multiple_of(who * share, LANES), share)
-        diff[:, cols] = (rest[:, cols] + mul_t(fold[...], ref[...])).astype(BF)
-    out[...] = mul_t(inv[...], diff[...]).astype(BF)
+        back[:, pl.ds(pl.multiple_of(who * share, LANES), share)] = ref[...]
+    diff = (rest[...] + mul(fold_t[...], back[...])).astype(BF)
+    out[...] = mul(inv_t[...], diff).astype(BF)
 
 
 def per_device(
@@ -188,8 +193,9 @@
     border = border_inverse.shape[0]
 
     window = jnp.where(low, coup_two[:, sep - width :], coup_two[:, :width])
+    block = jnp.concatenate([second_inverse[0], border_coupling[0]], 0)
+    w_near = send(block, NEAR)
     came_coup = send(window, NEAR)
-    block = jnp.concatenate([second_inverse[0], border_coupling[0]], 0)
     w_next = send(block, NEXT)
     fwd_leaf, top, bot = call(
         leaf_kernel,
@@ -202,14 +208,12 @@
     )
     came_top = send(top, NEAR)
     came_bot = send(bot, DOWN)
-    late_block, came_top = lax.optimization_barrier((block, came_top))
-    w_near = send(late_block, NEAR)
     w_far = send(w_near, NEXT)
     quarter = ((sep, share), BF)
     pack, own, near, nxt, far = call(
         first_kernel,
         [((half, 2 * sep - width + ports), BF)] + [quarter] * 4,
-        [((sep, ports), BF), ((width, ports), BF)],
+        [((sep, ports), BF), ((width, ports), BF), ((width, ports), BF)],
         at,
         inv_one,
         top,
@@ -259,10 +263,10 @@
     back_next = send(back_two, NEXT)
     back_near = send(back_two, NEAR)
     pack, came_pack, back_two = lax.optimization_barrier((pack, came_pack, back_two))
-    fold, rest = call(
+    fold_t, inv_t, rest = call(
         fold_kernel,
-        [((sep, leaf), BF), ((leaf, ports), F32)],
-        [((sep, leaf), BF)],
+        [((leaf, sep), BF), ((leaf, leaf), BF), ((leaf, ports), F32)],
+        [((sep, leaf), BF), ((sep, leaf), BF)],
         at,
         pack,
         came_pack,
@@ -270,20 +274,21 @@
         came_coup,
         leaf_coup,
         fwd_leaf,
+        leaf_inv,
         flops=2 * sep * leaf * (2 * sep + ports),
     )
     (out,) = call(
         last_kernel,
         [((leaf, ports), BF)],
-        [((leaf, ports), BF)],
-        at,
-        fold,
+        [((sep, ports), BF)],
+        at,
+        fold_t,
+        inv_t,
         rest,
         back_two,
         back_near,
         back_next,
         back_far,
-        leaf_inv,
         flops=2 * leaf * ports * (sep + leaf),
     )
     return out[None, None]

time: 172 us -> 169 us (0.983)
  local copies, waits for them, and re-layouts: 3.2 us -> 0.08 us
    unnamed x20 -> x16, local copies, waits for them, and re-layouts: 3.16 us -> 0.04 us
  transfers between devices with their start and end apart: 13 -> 13, of which waited for: 7 -> 6; matrix products, arithmetic and copies ran while one was open for 0% -> 0% of each run, Pallas kernels for 4% -> 5%
where the time goes in v3:
time: 169 us; the launch traced here: 168 us
  waiting for transfers between devices  56.5 us (33%)
  starting transfers between devices  50.7 us (30%)
  blocking collectives  48.9 us (29%)
  Pallas kernels  9.76 us (6%)
    ppermute x13, waiting for transfers between devices, send(): return lax.ppermute(x, 'x', pairs)  56.5 us
    ppermute x13, starting transfers between devices, send(): return lax.ppermute(x, 'x', pairs)  50.7 us
    all_to_all x2, blocking collectives, to_group(): return lax.all_to_all(tiles, GROUP, split_axis=0, concat_axis=0, tiled=True)  48.9 us
    pallas_call x6, Pallas kernels, call(): pl.pallas_call(kernel, out_shape=[jax.ShapeDtypeStruct(s, d) for s, d in...  9.76 us
  transfers between devices with their start and end apart: 13, of which 6 were waited for; matrix products, arithmetic and copies ran while one was open for 0% of the time, Pallas kernels for 5%

profile of v3, /device:TPU:1, one launch (start us, length us, event | category | flops | bytes accessed | tf_op | source)
XLA Modules:
  0.0 168.4 jit_solution(1660255975721802722)
XLA Ops:
  0.0 1.3 slice_select_fusion
  1.3 0.0 copy-start.6
  1.4 0.0 copy-start.7
  1.4 4.1 %collective-permute-start.2 = (bf16[448,512]{1,0:T(8,128)(2,1)S(1)}, bf16[448,512]{1,0:T(8,128)(2,1)S(1)}, u32[]{:S(2)}, u32[]{:S(2)}) collective-permute-start(bf16[448,512]{1,0:T(8,128)(2,1)S(1)} %slice_select_fusion), channel_id=1, source_target_pairs={{0,32},{32,0},{64,96},{96,64},{1,33},{33,1},{65,97},{97,65},{2,34}... | collective-permute-start | bytes 1376264 | tf_op jit(solution)/shard_map/ppermute | solution.py:23
  5.4 0.0 copy-done.5
  5.5 0.0 copy-done.3
  5.5 0.0 copy-done.4
  5.5 0.0 copy-start
  5.5 0.0 copy-start.1
  5.5 0.9 shard_map.91
  6.4 1.9 %collective-permute-start = (bf16[448,512]{1,0:T(8,128)(2,1)S(1)}, bf16[448,512]{1,0:T(8,128)(2,1)S(1)}, u32[]{:S(2)}, u32[]{:S(2)}) collective-permute-start(bf16[448,512]{1,0:T(8,128)(2,1)S(1)} %get-tuple-element.23.top), channel_id=1, source_target_pairs={{0,32},{32,0},{64,96},{96,64},{1,33},{33,1},{65,97},{97,65},{2,34}... | collective-permute-start | bytes 1376264 | tf_op jit(solution)/shard_map/ppermute | solution.py:23
  8.4 3.4 %collective-permute-start.1 = (bf16[448,512]{1,0:T(8,128)(2,1)S(1)}, bf16[448,512]{1,0:T(8,128)(2,1)S(1)}, u32[]{:S(2)}, u32[]{:S(2)}) collective-permute-start(bf16[448,512]{1,0:T(8,128)(2,1)S(1)} %get-tuple-element.24.bot), channel_id=1, source_target_pairs={{0,32},{64,96},{1,33},{65,97},{2,34},{66,98},{3,35},{67,99},{4,36}... | collective-permute-start | bytes 1376264 | tf_op jit(solution)/shard_map/ppermute | solution.py:23
  11.8 0.0 copy-done.6
  11.8 0.0 copy-done.7
  11.8 0.1 pad_maximum_fusion.w0
  11.8 1.9 %collective-permute-start.7 = (bf16[352,896]{1,0:T(8,128)(2,1)S(1)}, bf16[352,896]{1,0:T(8,128)(2,1)S(1)}, u32[]{:S(2)}, u32[]{:S(2)}) collective-permute-start(bf16[352,896]{1,0:T(8,128)(2,1)S(1)} %pad_maximum_fusion.w0), channel_id=1, source_target_pairs={{0,32},{32,0},{64,96},{96,64},{1,33},{33,1},{65,97},{97,65},{2,34}... | collective-permute-start | bytes 1892360 | tf_op jit(solution)/shard_map/ppermute | solution.py:23
  13.8 0.0 collective-permute-done.2.came_coup
  13.8 6.8 %collective-permute-done.came_top = bf16[448,512]{1,0:T(8,128)(2,1)S(1)} collective-permute-done((bf16[448,512]{1,0:T(8,128)(2,1)S(1)}, bf16[448,512]{1,0:T(8,128)(2,1)S(1)}, u32[]{:S(2)}, u32[]{:S(2)}) %collective-permute-start) | collective-permute-done | bytes 458784 | tf_op jit(solution)/shard_map/ppermute | solution.py:23
  20.6 9.8 %collective-permute-done.1.came_bot = bf16[448,512]{1,0:T(8,128)(2,1)S(1)} collective-permute-done((bf16[448,512]{1,0:T(8,128)(2,1)S(1)}, bf16[448,512]{1,0:T(8,128)(2,1)S(1)}, u32[]{:S(2)}, u32[]{:S(2)}) %collective-permute-start.1) | collective-permute-done | bytes 458784 | tf_op jit(solution)/shard_map/ppermute | solution.py:23
  30.4 0.0 copy-done
  30.4 0.0 copy-done.1
  30.4 1.4 shard_map.92
  31.9 4.1 %collective-permute-start.3 = (bf16[896,128]{1,0:T(8,128)(2,1)S(1)}, bf16[896,128]{1,0:T(8,128)(2,1)S(1)}, u32[]{:S(2)}, u32[]{:S(2)}) collective-permute-start(bf16[896,128]{1,0:T(8,128)(2,1)S(1)} %get-tuple-element.26), channel_id=1, source_target_pairs={{0,32},{32,0},{64,96},{96,64},{1,33},{33,1},{65,97},{97,65},{2,34}... | collective-permute-start | bytes 688136 | tf_op jit(solution)/shard_map/ppermute | solution.py:23
  36.0 7.0 %collective-permute-start.8 = (bf16[352,896]{1,0:T(8,128)(2,1)S(1)}, bf16[352,896]{1,0:T(8,128)(2,1)S(1)}, u32[]{:S(2)}, u32[]{:S(2)}) collective-permute-start(bf16[352,896]{1,0:T(8,128)(2,1)S(1)} %pad_maximum_fusion.w0), channel_id=1, source_target_pairs={{0,96},{96,0},{32,64},{64,32},{1,97},{97,1},{33,65},{65,33},{2,98}... | collective-permute-start | bytes 1892360 | tf_op jit(solution)/shard_map/ppermute | solution.py:23
  43.0 0.9 collective-permute-done.7.w1
  44.0 9.2 %collective-permute-start.9 = (bf16[352,896]{1,0:T(8,128)(2,1)S(1)}, bf16[352,896]{1,0:T(8,128)(2,1)S(1)}, u32[]{:S(2)}, u32[]{:S(2)}) collective-permute-start(bf16[352,896]{1,0:T(8,128)(2,1)S(1)} %collective-permute-done.7.w1), channel_id=1, source_target_pairs={{0,96},{96,0},{32,64},{64,32},{1,97},{97,1},{33,65},{65,33},{2,98}... | collective-permute-start | bytes 1892360 | tf_op jit(solution)/shard_map/ppermute | solution.py:23
  53.2 0.0 collective-permute-done.3.near
  53.2 1.9 %collective-permute-start.4 = (bf16[448,1792]{1,0:T(8,128)(2,1)S(1)}, bf16[448,1792]{1,0:T(8,128)(2,1)S(1)}, u32[]{:S(2)}, u32[]{:S(2)}) collective-permute-start(bf16[448,1792]{1,0:T(8,128)(2,1)S(1)} %get-tuple-element.34.pack), channel_id=1, source_target_pairs={{0,32},{32,0},{64,96},{96,64},{1,33},{33,1},{65,97},{97,65},{2,34}... | collective-permute-start | bytes 4816904 | tf_op jit(solution)/shard_map/ppermute | solution.py:23
  55.1 4.9 %collective-permute-start.5 = (bf16[896,128]{1,0:T(8,128)(2,1)S(1)}, bf16[896,128]{1,0:T(8,128)(2,1)S(1)}, u32[]{:S(2)}, u32[]{:S(2)}) collective-permute-start(bf16[896,128]{1,0:T(8,128)(2,1)S(1)} %get-tuple-element.30), channel_id=1, source_target_pairs={{0,96},{96,0},{32,64},{64,32},{1,97},{97,1},{33,65},{65,33},{2,98}... | collective-permute-start | bytes 688136 | tf_op jit(solution)/shard_map/ppermute | solution.py:23
  60.0 3.1 %collective-permute-start.6 = (bf16[896,128]{1,0:T(8,128)(2,1)S(1)}, bf16[896,128]{1,0:T(8,128)(2,1)S(1)}, u32[]{:S(2)}, u32[]{:S(2)}) collective-permute-start(bf16[896,128]{1,0:T(8,128)(2,1)S(1)} %get-tuple-element.31), channel_id=1, source_target_pairs={{0,64},{64,0},{32,96},{96,32},{1,65},{65,1},{33,97},{97,33},{2,66}... | collective-permute-start | bytes 688136 | tf_op jit(solution)/shard_map/ppermute | solution.py:23
  63.8 0.0 collective-permute-done.8.w2
  63.8 9.1 %collective-permute-done.5.nxt = bf16[896,128]{1,0:T(8,128)(2,1)S(1)} collective-permute-done((bf16[896,128]{1,0:T(8,128)(2,1)S(1)}, bf16[896,128]{1,0:T(8,128)(2,1)S(1)}, u32[]{:S(2)}, u32[]{:S(2)}) %collective-permute-start.5) | collective-permute-done | bytes 229408 | tf_op jit(solution)/shard_map/ppermute | solution.py:23
  72.8 25.0 %collective-permute-done.6.far = bf16[896,128]{1,0:T(8,128)(2,1)S(1)} collective-permute-done((bf16[896,128]{1,0:T(8,128)(2,1)S(1)}, bf16[896,128]{1,0:T(8,128)(2,1)S(1)}, u32[]{:S(2)}, u32[]{:S(2)}) %collective-permute-start.6) | collective-permute-done | bytes 229408 | tf_op jit(solution)/shard_map/ppermute | solution.py:23
  97.8 0.0 collective-permute-done.9.w3
  97.8 1.1 shard_map.93
  98.9 31.4 %all_to_all.10 = bf16[128,4,128]{2,1,0:T(4,128)(2,1)S(1)} all-to-all(bf16[128,4,128]{2,1,0:T(4,128)(2,1)S(1)} %bitcast.16), channel_id=1, replica_groups=mesh['zl'=4,'x'=4,'y'=8,'zh'=2,'c'=2] {'zl','y','zh','c'}, dimensions={0} | all-to-all | bytes 262144 | tf_op jit(solution)/shard_map/all_to_all | solution.py:27
  130.3 0.1 convert_reduce_fusion
  130.5 17.5 %all_to_all.11 = bf16[128,4,128]{2,1,0:T(4,128)(2,1)S(1)} all-to-all(bf16[128,4,128]{2,1,0:T(4,128)(2,1)S(1)} %broadcast_in_dim.10), channel_id=1, replica_groups=mesh['zl'=4,'x'=4,'y'=8,'zh'=2,'c'=2] {'zl','y','zh','c'}, dimensions={0} | all-to-all | bytes 262144 | tf_op jit(solution)/shard_map/all_to_all | solution.py:27
  148.0 1.8 %shard_map.94.own = bf16[896,128]{1,0:T(8,128)(2,1)S(1)} custom-call(s32[1]{0:T(128)} %bitcast.at, s32[1]{0:T(128)S(6)} %copy.10.rows, bf16[512,128]{1,0:T(8,128)(2,1)S(1)} %bitcast.15, bf16[512,512]{1,0:T(8,128)(2,1)S(1)} %copy-done.2, bf16[896,128]{1,0:T(8,128)(2,1)S(1)} %get-tuple-element.33.fwd, bf16[352,896]{1,0:T(8,128)(2,1)S(1)} %pad_maximum_fusion.w0, ...), custom_call_target="tpu_custom_call" | custom-call | flops 457179136 | bytes 3407880 | tf_op jit(solution)/shard_map/pallas_call | solution.py:41
  149.8 1.9 %collective-permute-start.10 = (bf16[896,128]{1,0:T(8,128)(2,1)S(1)}, bf16[896,128]{1,0:T(8,128)(2,1)S(1)}, u32[]{:S(2)}, u32[]{:S(2)}) collective-permute-start(bf16[896,128]{1,0:T(8,128)(2,1)S(1)} %shard_map.94.own), channel_id=1, source_target_pairs={{0,32},{32,0},{64,96},{96,64},{1,33},{33,1},{65,97},{97,65},{2,34}... | collective-permute-start | bytes 688136 | tf_op jit(solution)/shard_map/ppermute | solution.py:23
  151.7 2.7 %collective-permute-start.11 = (bf16[896,128]{1,0:T(8,128)(2,1)S(1)}, bf16[896,128]{1,0:T(8,128)(2,1)S(1)}, u32[]{:S(2)}, u32[]{:S(2)}) collective-permute-start(bf16[896,128]{1,0:T(8,128)(2,1)S(1)} %shard_map.94.own), channel_id=1, source_target_pairs={{0,96},{96,0},{32,64},{64,32},{1,97},{97,1},{33,65},{65,33},{2,98}... | collective-permute-start | bytes 688136 | tf_op jit(solution)/shard_map/ppermute | solution.py:23
  154.5 4.5 %collective-permute-start.12 = (bf16[896,128]{1,0:T(8,128)(2,1)S(1)}, bf16[896,128]{1,0:T(8,128)(2,1)S(1)}, u32[]{:S(2)}, u32[]{:S(2)}) collective-permute-start(bf16[896,128]{1,0:T(8,128)(2,1)S(1)} %shard_map.94.own), channel_id=1, source_target_pairs={{0,64},{64,0},{32,96},{96,32},{1,65},{65,1},{33,97},{97,33},{2,66}... | collective-permute-start | bytes 688136 | tf_op jit(solution)/shard_map/ppermute | solution.py:23
  159.0 0.0 collective-permute-done.4.came
  159.0 2.6 %shard_map.95 = (bf16[384,896]{1,0:T(8,128)(2,1)S(1)}, bf16[384,384]{1,0:T(8,128)(2,1)S(1)}, f32[384,512]{1,0:T(8,128)S(1)}) custom-call(s32[1]{0:T(128)} %bitcast.at, bf16[448,1792]{1,0:T(8,128)(2,1)S(1)} %get-tuple-element.34.pack, bf16[448,1792]{1,0:T(8,128)(2,1)S(1)} %collective-permute-done.4.came, bf16[448,896]{1,0:T(8,128)(2,1)S(1)} %bitcast.13, ...), custom_call_target="tpu_custom_call" | custom-call | flops 1585446912 | bytes 5849092 | tf_op jit(solution)/shard_map/pallas_call | solution.py:41
  161.7 0.0 collective-permute-done.10.near
  161.7 4.9 %collective-permute-done.11.nxt = bf16[896,128]{1,0:T(8,128)(2,1)S(1)} collective-permute-done((bf16[896,128]{1,0:T(8,128)(2,1)S(1)}, bf16[896,128]{1,0:T(8,128)(2,1)S(1)}, u32[]{:S(2)}, u32[]{:S(2)}) %collective-permute-start.11) | collective-permute-done | bytes 229408 | tf_op jit(solution)/shard_map/ppermute | solution.py:23
  166.6 0.0 collective-permute-done.12.far
  166.6 1.8 %shard_map.96 = bf16[384,512]{1,0:T(8,128)(2,1)} custom-call(s32[1]{0:T(128)} %bitcast.at, bf16[384,896]{1,0:T(8,128)(2,1)S(1)} %get-tuple-element.37.fold_t, bf16[384,384]{1,0:T(8,128)(2,1)S(1)} %get-tuple-element.38.inv_t, f32[384,512]{1,0:T(8,128)S(1)} %get-tuple-element.39.rest, bf16[896,128]{1,0:T(8,128)(2,1)S(1)} %shard_map.94.own, ...), custom_call_target="tpu_custom_call" | custom-call | flops 503316480 | bytes 2686980 | tf_op jit(solution)/shard_map/pallas_call | solution.py:41
  (7 shorter events, 0.1 us)
Async XLA Ops:
  0.0 5.4 %copy-start.5 = (bf16[1,1,384,384]{3,2,1,0:T(8,128)(2,1)S(1)}, bf16[1,1,384,384]{3,2,1,0:T(8,128)(2,1)}, u32[]{:S(2)}) copy-start(bf16[1,1,384,384]{3,2,1,0:T(8,128)(2,1)} %param.10) | copy-start | bytes 884740
  0.0 5.4 %copy-start.3 = (bf16[1,1,896,384]{3,2,1,0:T(8,128)(2,1)S(1)}, bf16[1,1,896,384]{3,2,1,0:T(8,128)(2,1)}, u32[]{:S(2)}) copy-start(bf16[1,1,896,384]{3,2,1,0:T(8,128)(2,1)} %param.11) | copy-start | bytes 2064388
  0.0 5.5 %copy-start.4 = (bf16[1,1,384,512]{3,2,1,0:T(8,128)(2,1)S(1)}, bf16[1,1,384,512]{3,2,1,0:T(8,128)(2,1)}, u32[]{:S(2)}) copy-start(bf16[1,1,384,512]{3,2,1,0:T(8,128)(2,1)} %param.9) | copy-start | bytes 1179652
  1.3 10.4 %copy-start.6 = (bf16[1,224,896]{2,1,0:T(8,128)(2,1)S(1)}, bf16[1,224,896]{2,1,0:T(8,128)(2,1)}, u32[]{:S(2)}) copy-start(bf16[1,224,896]{2,1,0:T(8,128)(2,1)} %param.14) | copy-start | bytes 1204228
  1.4 10.4 %copy-start.7 = (bf16[1,128,896]{2,1,0:T(8,128)(2,1)S(1)}, bf16[1,128,896]{2,1,0:T(8,128)(2,1)}, u32[]{:S(2)}) copy-start(bf16[1,128,896]{2,1,0:T(8,128)(2,1)} %param.15) | copy-start | bytes 688132
  1.4 12.4 %collective-permute-start.2 = (bf16[448,512]{1,0:T(8,128)(2,1)S(1)}, bf16[448,512]{1,0:T(8,128)(2,1)S(1)}, u32[]{:S(2)}, u32[]{:S(2)}) collective-permute-start(bf16[448,512]{1,0:T(8,128)(2,1)S(1)} %slice_select_fusion), channel_id=1, source_target_pairs={{0,32},{32,0},{64,96},{96,64},{1,33},{33,1},{65,97},{97,65},{2,34}... | collective-permute-start | bytes 1376264 | tf_op jit(solution)/shard_map/ppermute | solution.py:23
  5.5 25.0 %copy-start = (bf16[1,448,896]{2,1,0:T(8,128)(2,1)S(1)}, bf16[1,448,896]{2,1,0:T(8,128)(2,1)}, u32[]{:S(2)}) copy-start(bf16[1,448,896]{2,1,0:T(8,128)(2,1)} %param.13) | copy-start | bytes 2408452
  5.5 25.0 %copy-start.1 = (bf16[1,448,896]{2,1,0:T(8,128)(2,1)S(1)}, bf16[1,448,896]{2,1,0:T(8,128)(2,1)}, u32[]{:S(2)}) copy-start(bf16[1,448,896]{2,1,0:T(8,128)(2,1)} %param.12) | copy-start | bytes 2408452
  6.4 14.2 %collective-permute-start = (bf16[448,512]{1,0:T(8,128)(2,1)S(1)}, bf16[448,512]{1,0:T(8,128)(2,1)S(1)}, u32[]{:S(2)}, u32[]{:S(2)}) collective-permute-start(bf16[448,512]{1,0:T(8,128)(2,1)S(1)} %get-tuple-element.23.top), channel_id=1, source_target_pairs={{0,32},{32,0},{64,96},{96,64},{1,33},{33,1},{65,97},{97,65},{2,34}... | collective-permute-start | bytes 1376264 | tf_op jit(solution)/shard_map/ppermute | solution.py:23
  8.4 22.1 %collective-permute-start.1 = (bf16[448,512]{1,0:T(8,128)(2,1)S(1)}, bf16[448,512]{1,0:T(8,128)(2,1)S(1)}, u32[]{:S(2)}, u32[]{:S(2)}) collective-permute-start(bf16[448,512]{1,0:T(8,128)(2,1)S(1)} %get-tuple-element.24.bot), channel_id=1, source_target_pairs={{0,32},{64,96},{1,33},{65,97},{2,34},{66,98},{3,35},{67,99},{4,36}... | collective-permute-start | bytes 1376264 | tf_op jit(solution)/shard_map/ppermute | solution.py:23
  11.8 32.1 %collective-permute-start.7 = (bf16[352,896]{1,0:T(8,128)(2,1)S(1)}, bf16[352,896]{1,0:T(8,128)(2,1)S(1)}, u32[]{:S(2)}, u32[]{:S(2)}) collective-permute-start(bf16[352,896]{1,0:T(8,128)(2,1)S(1)} %pad_maximum_fusion.w0), channel_id=1, source_target_pairs={{0,32},{32,0},{64,96},{96,64},{1,33},{33,1},{65,97},{97,65},{2,34}... | collective-permute-start | bytes 1892360 | tf_op jit(solution)/shard_map/ppermute | solution.py:23
  31.9 21.3 %collective-permute-start.3 = (bf16[896,128]{1,0:T(8,128)(2,1)S(1)}, bf16[896,128]{1,0:T(8,128)(2,1)S(1)}, u32[]{:S(2)}, u32[]{:S(2)}) collective-permute-start(bf16[896,128]{1,0:T(8,128)(2,1)S(1)} %get-tuple-element.26), channel_id=1, source_target_pairs={{0,32},{32,0},{64,96},{96,64},{1,33},{33,1},{65,97},{97,65},{2,34}... | collective-permute-start | bytes 688136 | tf_op jit(solution)/shard_map/ppermute | solution.py:23
  36.0 27.8 %collective-permute-start.8 = (bf16[352,896]{1,0:T(8,128)(2,1)S(1)}, bf16[352,896]{1,0:T(8,128)(2,1)S(1)}, u32[]{:S(2)}, u32[]{:S(2)}) collective-permute-start(bf16[352,896]{1,0:T(8,128)(2,1)S(1)} %pad_maximum_fusion.w0), channel_id=1, source_target_pairs={{0,96},{96,0},{32,64},{64,32},{1,97},{97,1},{33,65},{65,33},{2,98}... | collective-permute-start | bytes 1892360 | tf_op jit(solution)/shard_map/ppermute | solution.py:23
  44.0 53.9 %collective-permute-start.9 = (bf16[352,896]{1,0:T(8,128)(2,1)S(1)}, bf16[352,896]{1,0:T(8,128)(2,1)S(1)}, u32[]{:S(2)}, u32[]{:S(2)}) collective-permute-start(bf16[352,896]{1,0:T(8,128)(2,1)S(1)} %collective-permute-done.7.w1), channel_id=1, source_target_pairs={{0,96},{96,0},{32,64},{64,32},{1,97},{97,1},{33,65},{65,33},{2,98}... | collective-permute-start | bytes 1892360 | tf_op jit(solution)/shard_map/ppermute | solution.py:23
  53.2 105.8 %collective-permute-start.4 = (bf16[448,1792]{1,0:T(8,128)(2,1)S(1)}, bf16[448,1792]{1,0:T(8,128)(2,1)S(1)}, u32[]{:S(2)}, u32[]{:S(2)}) collective-permute-start(bf16[448,1792]{1,0:T(8,128)(2,1)S(1)} %get-tuple-element.34.pack), channel_id=1, source_target_pairs={{0,32},{32,0},{64,96},{96,64},{1,33},{33,1},{65,97},{97,65},{2,34}... | collective-permute-start | bytes 4816904 | tf_op jit(solution)/shard_map/ppermute | solution.py:23
  55.1 17.7 %collective-permute-start.5 = (bf16[896,128]{1,0:T(8,128)(2,1)S(1)}, bf16[896,128]{1,0:T(8,128)(2,1)S(1)}, u32[]{:S(2)}, u32[]{:S(2)}) collective-permute-start(bf16[896,128]{1,0:T(8,128)(2,1)S(1)} %get-tuple-element.30), channel_id=1, source_target_pairs={{0,96},{96,0},{32,64},{64,32},{1,97},{97,1},{33,65},{65,33},{2,98}... | collective-permute-start | bytes 688136 | tf_op jit(solution)/shard_map/ppermute | solution.py:23
  60.0 37.8 %collective-permute-start.6 = (bf16[896,128]{1,0:T(8,128)(2,1)S(1)}, bf16[896,128]{1,0:T(8,128)(2,1)S(1)}, u32[]{:S(2)}, u32[]{:S(2)}) collective-permute-start(bf16[896,128]{1,0:T(8,128)(2,1)S(1)} %get-tuple-element.31), channel_id=1, source_target_pairs={{0,64},{64,0},{32,96},{96,32},{1,65},{65,1},{33,97},{97,33},{2,66}... | collective-permute-start | bytes 688136 | tf_op jit(solution)/shard_map/ppermute | solution.py:23
  97.8 50.2 %copy-start.2 = (bf16[512,512]{1,0:T(8,128)(2,1)S(1)}, bf16[512,512]{1,0:T(8,128)(2,1)}, u32[]{:S(2)}) copy-start(bf16[512,512]{1,0:T(8,128)(2,1)} %inv.1) | copy-start | bytes 1572868
  149.8 11.8 %collective-permute-start.10 = (bf16[896,128]{1,0:T(8,128)(2,1)S(1)}, bf16[896,128]{1,0:T(8,128)(2,1)S(1)}, u32[]{:S(2)}, u32[]{:S(2)}) collective-permute-start(bf16[896,128]{1,0:T(8,128)(2,1)S(1)} %shard_map.94.own), channel_id=1, source_target_pairs={{0,32},{32,0},{64,96},{96,64},{1,33},{33,1},{65,97},{97,65},{2,34}... | collective-permute-start | bytes 688136 | tf_op jit(solution)/shard_map/ppermute | solution.py:23
  151.7 14.8 %collective-permute-start.11 = (bf16[896,128]{1,0:T(8,128)(2,1)S(1)}, bf16[896,128]{1,0:T(8,128)(2,1)S(1)}, u32[]{:S(2)}, u32[]{:S(2)}) collective-permute-start(bf16[896,128]{1,0:T(8,128)(2,1)S(1)} %shard_map.94.own), channel_id=1, source_target_pairs={{0,96},{96,0},{32,64},{64,32},{1,97},{97,1},{33,65},{65,33},{2,98}... | collective-permute-start | bytes 688136 | tf_op jit(solution)/shard_map/ppermute | solution.py:23
  154.5 12.1 %collective-permute-start.12 = (bf16[896,128]{1,0:T(8,128)(2,1)S(1)}, bf16[896,128]{1,0:T(8,128)(2,1)S(1)}, u32[]{:S(2)}, u32[]{:S(2)}) collective-permute-start(bf16[896,128]{1,0:T(8,128)(2,1)S(1)} %shard_map.94.own), channel_id=1, source_target_pairs={{0,64},{64,0},{32,96},{96,32},{1,65},{65,1},{33,97},{97,33},{2,66}... | collective-permute-start | bytes 688136 | tf_op jit(solution)/shard_map/ppermute | solution.py:23

commit v4 on v3

--- a/solution.py
+++ b/solution.py
@@ -13,6 +13,8 @@
 NEXT = [(0, 3), (3, 0), (1, 2), (2, 1)]
 ACROSS = [(0, 2), (2, 0), (1, 3), (3, 1)]
 DOWN = [(0, 1), (2, 3)]
+UP = [(1, 0), (3, 2)]
+BACK = [(0, 3), (2, 1)]
 BF = jnp.bfloat16
 F32 = jnp.float32
 
@@ -99,40 +101,37 @@
     return zip((x,) + others(x), refs)
 
 
-def second_kernel(at, rows, own, near, nxt, far, w0, w1, w2, w3, fwd, tiles, rhs):
+def join_kernel(at, i0, i1, i2, i3, b0, up, nxt, down, border_inv, inv, inv_t, coup, coup_t, border_t):
     x = at[0]
+    each = i0.shape[0]
+    for who, ref in pieces(x, (i0, i1, i2, i3)):
+        inv[pl.ds(pl.multiple_of(who * each, each), each)] = ref[...]
+    count = b0.shape[0]
+    near = up[:count] + down[count:]
+    far = up[count:] + down[:count]
+    for who, block in pieces(x, (b0[...], near, nxt[...], far)):
+        coup[pl.ds(pl.multiple_of(who * count, count), count)] = block
+    inv_t[...] = inv[...].T
+    coup_t[...] = coup[...].T
+    border_t[...] = border_inv[...].T
+
+
+def second_kernel(rows, own, near, nxt, far, inv, coup, fwd, tiles):
     total = own[...].astype(F32) + near[...].astype(F32)
     total = total + (nxt[...].astype(F32) + far[...].astype(F32))
-    rhs[...] = (-total).astype(BF)
-    each = rhs.shape[0] // 4
-    for who, ref in pieces(x, (w0, w1, w2, w3)):
-        fwd[pl.ds(pl.multiple_of(who * each, each), each)] = mul(ref[:each], rhs[...]).astype(BF)
-    for who, ref in pieces(x, (w0, w1, w2, w3)):
-        count = ref.shape[0] - each
-        first = pl.multiple_of(who * count, count)
-        part = mul(ref[each:], fwd[...])
-        live = lax.broadcasted_iota(jnp.int32, part.shape, 0) + first < rows[0]
-        tiles[pl.ds(first, count)] = jnp.where(live, part, 0.0).astype(BF)
-
-
-def border_kernel(at, rows, rhs, inv, fwd, w0, w1, w2, w3, back, sol):
-    x = at[0]
+    fwd[...] = mul(inv[...], (-total).astype(BF)).astype(BF)
+    part = mul(coup[...], fwd[...])
+    live = lax.broadcasted_iota(jnp.int32, part.shape, 0) < rows[0]
+    tiles[...] = jnp.where(live, part, 0.0).astype(BF)
+
+
+def border_kernel(rows, rhs, inv, inv_t, fwd, second_t, coup_t, back):
     mid = mul(inv[...], rhs[...]).astype(BF)
-    end = mul_t(inv[...], mid)
+    end = mul(inv_t[...], mid)
     live = lax.broadcasted_iota(jnp.int32, end.shape, 0) < rows[0]
-    sol[...] = jnp.where(live, end, 0.0).astype(BF)
-    each = fwd.shape[0] // 4
-    diff = fwd[...].astype(F32)
-    for who, ref in pieces(x, (w0, w1, w2, w3)):
-        count = ref.shape[0] - each
-        diff = diff - mul_t(ref[each:], sol[pl.ds(pl.multiple_of(who * count, count), count)])
-    fwd_ref = back
-    fwd_ref[...] = diff.astype(BF)
-    total = None
-    for who, ref in pieces(x, (w0, w1, w2, w3)):
-        term = mul_t(ref[:each], fwd_ref[pl.ds(pl.multiple_of(who * each, each), each)])
-        total = term if total is None else total + term
-    back[...] = total.astype(BF)
+    sol = jnp.where(live, end, 0.0).astype(BF)
+    diff = (fwd[...].astype(F32) - mul(coup_t[...], sol)).astype(BF)
+    back[...] = mul(second_t[...], diff).astype(BF)
 
 
 def fold_kernel(at, pack, came, coup, came_coup, leaf_coup, fwd_leaf, leaf_inv, fold_t, inv_t, rest, full, fold):
@@ -192,11 +191,9 @@
     width = -(-half // LANES) * LANES
     border = border_inverse.shape[0]
 
-    window = jnp.where(low, coup_two[:, sep - width :], coup_two[:, :width])
-    block = jnp.concatenate([second_inverse[0], border_coupling[0]], 0)
-    w_near = send(block, NEAR)
-    came_coup = send(window, NEAR)
-    w_next = send(block, NEXT)
+    inv_two, coup_border = second_inverse[0], border_coupling[0]
+    i_near = send(inv_two, NEAR)
+    b_next = send(coup_border, NEXT)
     fwd_leaf, top, bot = call(
         leaf_kernel,
         [((leaf, ports), BF), ((half, ports), BF), ((half, ports), BF)],
@@ -206,9 +203,14 @@
         leaf_coup,
         flops=2 * leaf * ports * (leaf + sep),
     )
+    came_bot = send(bot, DOWN)
+    b_up = send(jnp.concatenate([coup_border, b_next], 0), UP)
+    window = jnp.where(low, coup_two[:, sep - width :], coup_two[:, :width])
+    came_coup = send(window, NEAR)
     came_top = send(top, NEAR)
-    came_bot = send(bot, DOWN)
-    w_far = send(w_near, NEXT)
+    i_next = send(inv_two, NEXT)
+    i_far = send(i_near, NEXT)
+    b_down = send(b_up, BACK)
     quarter = ((sep, share), BF)
     pack, own, near, nxt, far = call(
         first_kernel,
@@ -224,23 +226,43 @@
         came_coup,
         flops=2 * half * ports * sep + 2 * sep * ports * width,
     )
+    near = send(near, NEAR)
     far = send(far, ACROSS)
     nxt = send(nxt, NEXT)
-    near = send(near, NEAR)
     late_pack, near = lax.optimization_barrier((pack, near))
     came_pack = send(late_pack, NEAR)
-    blocks = (block, w_near, w_next, w_far)
+    inv_full, inv_full_t, coup_full, coup_full_t, border_t = call(
+        join_kernel,
+        [
+            ((sep, sep), BF),
+            ((sep, sep), BF),
+            ((border, sep), BF),
+            ((sep, border), BF),
+            ((border, border), BF),
+        ],
+        [],
+        at,
+        inv_two,
+        i_near,
+        i_next,
+        i_far,
+        coup_border,
+        b_up,
+        b_next,
+        b_down,
+        border_inverse,
+    )
     fwd_two, tiles = call(
         second_kernel,
         [quarter, ((border, share), BF)],
-        [quarter],
-        at,
+        [],
         border_rows,
         own,
         near,
         nxt,
         far,
-        *blocks,
+        inv_full,
+        coup_full,
         flops=2 * sep * share * (sep + border),
     )
     tiles = tiles.reshape(group, border // group, share)
@@ -250,13 +272,14 @@
     (back_two,) = call(
         border_kernel,
         [quarter],
-        [((border, share), BF)],
-        at,
+        [],
         border_rows,
         rhs_border,
         border_inverse,
+        border_t,
         fwd_two,
-        *blocks,
+        inv_full_t,
+        coup_full_t,
         flops=2 * share * (2 * border * border + border * sep + sep * sep),
     )
     back_far = send(back_two, ACROSS)

time: 169 us -> 166 us (0.982)
  waiting for transfers between devices: 56.5 us -> 47.6 us
  local copies, waits for them, and re-layouts: 0.08 us -> 3.12 us
    ppermute x13 -> x16, waiting for transfers between devices: 56.5 us -> 47.6 us  [send(): return lax.ppermute(x, 'x', pairs)]
    unnamed x16 -> x20, local copies, waits for them, and re-layouts: 0.04 us -> 3.08 us
    pallas_call x6 -> x7, Pallas kernels: 9.76 us -> 11.1 us  [call(): pl.pallas_call(kernel, out_shape=[jax.ShapeDtypeStruct(s, d) for s, d in...]
    ppermute x13 -> x16, starting transfers between devices: 50.7 us -> 52 us  [send(): return lax.ppermute(x, 'x', pairs)]
  transfers between devices with their start and end apart: 13 -> 16, of which waited for: 6 -> 6; matrix products, arithmetic and copies ran while one was open for 0% -> 0% of each run, Pallas kernels for 5% -> 6%
where the time goes in v4:
time: 166 us; the launch traced here: 165 us
  starting transfers between devices  52 us (31%)
  blocking collectives  48.9 us (29%)
  waiting for transfers between devices  47.6 us (29%)
  Pallas kernels  11.1 us (7%)
  local copies, waits for them, and re-layouts  3.12 us (2%)
    ppermute x16, starting transfers between devices, send(): return lax.ppermute(x, 'x', pairs)  52 us
    all_to_all x2, blocking collectives, to_group(): return lax.all_to_all(tiles, GROUP, split_axis=0, concat_axis=0, tiled=True)  48.9 us
    ppermute x16, waiting for transfers between devices, send(): return lax.ppermute(x, 'x', pairs)  47.6 us
    pallas_call x7, Pallas kernels, call(): pl.pallas_call(kernel, out_shape=[jax.ShapeDtypeStruct(s, d) for s, d in...  11.1 us
  transfers between devices with their start and end apart: 16, of which 6 were waited for; matrix products, arithmetic and copies ran while one was open for 0% of the time, Pallas kernels for 6%

profile of v4, /device:TPU:1, one launch (start us, length us, event | category | flops | bytes accessed | tf_op | source)
XLA Modules:
  0.0 165.2 jit_solution(16325571128945477795)
XLA Ops:
  0.0 1.3 slice_select_fusion
  1.3 0.0 copy-start
  1.3 0.0 copy-start.3
  1.3 4.1 %collective-permute-start.2 = (bf16[448,512]{1,0:T(8,128)(2,1)S(1)}, bf16[448,512]{1,0:T(8,128)(2,1)S(1)}, u32[]{:S(2)}, u32[]{:S(2)}) collective-permute-start(bf16[448,512]{1,0:T(8,128)(2,1)S(1)} %slice_select_fusion), channel_id=1, source_target_pairs={{0,32},{32,0},{64,96},{96,64},{1,33},{33,1},{65,97},{97,65},{2,34}... | collective-permute-start | bytes 1376264 | tf_op jit(solution)/shard_map/ppermute | solution.py:25
  5.4 0.0 copy-start.5
  5.4 1.1 copy-done.5
  6.5 1.0 copy-done.7
  7.5 1.0 copy-done.8
  8.5 0.9 shard_map.91
  9.4 1.9 %collective-permute-start = (bf16[448,512]{1,0:T(8,128)(2,1)S(1)}, bf16[448,512]{1,0:T(8,128)(2,1)S(1)}, u32[]{:S(2)}, u32[]{:S(2)}) collective-permute-start(bf16[448,512]{1,0:T(8,128)(2,1)S(1)} %get-tuple-element.28.top), channel_id=1, source_target_pairs={{0,32},{32,0},{64,96},{96,64},{1,33},{33,1},{65,97},{97,65},{2,34}... | collective-permute-start | bytes 1376264 | tf_op jit(solution)/shard_map/ppermute | solution.py:25
  11.3 3.4 %collective-permute-start.1 = (bf16[448,512]{1,0:T(8,128)(2,1)S(1)}, bf16[448,512]{1,0:T(8,128)(2,1)S(1)}, u32[]{:S(2)}, u32[]{:S(2)}) collective-permute-start(bf16[448,512]{1,0:T(8,128)(2,1)S(1)} %get-tuple-element.29.bot), channel_id=1, source_target_pairs={{0,32},{64,96},{1,33},{65,97},{2,34},{66,98},{3,35},{67,99},{4,36}... | collective-permute-start | bytes 1376264 | tf_op jit(solution)/shard_map/ppermute | solution.py:25
  14.7 2.5 %collective-permute-start.10 = (bf16[128,896]{1,0:T(8,128)(2,1)S(1)}, bf16[128,896]{1,0:T(8,128)(2,1)S(1)}, u32[]{:S(2)}, u32[]{:S(2)}) collective-permute-start(bf16[128,896]{1,0:T(8,128)(2,1)S(1)} %bitcast.14), channel_id=1, source_target_pairs={{0,96},{96,0},{32,64},{64,32},{1,97},{97,1},{33,65},{65,33},{2,98}... | collective-permute-start | bytes 688136 | tf_op jit(solution)/shard_map/ppermute | solution.py:25
  17.3 5.4 %collective-permute-done.10.nxt = bf16[128,896]{1,0:T(8,128)(2,1)S(1)} collective-permute-done((bf16[128,896]{1,0:T(8,128)(2,1)S(1)}, bf16[128,896]{1,0:T(8,128)(2,1)S(1)}, u32[]{:S(2)}, u32[]{:S(2)}) %collective-permute-start.10) | collective-permute-done | bytes 229408 | tf_op jit(solution)/shard_map/ppermute | solution.py:25
  22.7 1.3 collective-permute-start.11
  24.0 0.0 collective-permute-done.2.came_coup
  24.1 0.0 collective-permute-done.came_top
  24.1 7.4 %collective-permute-done.1.came_bot = bf16[448,512]{1,0:T(8,128)(2,1)S(1)} collective-permute-done((bf16[448,512]{1,0:T(8,128)(2,1)S(1)}, bf16[448,512]{1,0:T(8,128)(2,1)S(1)}, u32[]{:S(2)}, u32[]{:S(2)}) %collective-permute-start.1) | collective-permute-done | bytes 458784 | tf_op jit(solution)/shard_map/ppermute | solution.py:25
  31.5 1.4 shard_map.92
  32.9 4.1 %collective-permute-start.3 = (bf16[896,128]{1,0:T(8,128)(2,1)S(1)}, bf16[896,128]{1,0:T(8,128)(2,1)S(1)}, u32[]{:S(2)}, u32[]{:S(2)}) collective-permute-start(bf16[896,128]{1,0:T(8,128)(2,1)S(1)} %get-tuple-element.31), channel_id=1, source_target_pairs={{0,32},{32,0},{64,96},{96,64},{1,33},{33,1},{65,97},{97,65},{2,34}... | collective-permute-start | bytes 688136 | tf_op jit(solution)/shard_map/ppermute | solution.py:25
  37.0 1.9 %collective-permute-start.7 = (bf16[224,896]{1,0:T(8,128)(2,1)S(1)}, bf16[224,896]{1,0:T(8,128)(2,1)S(1)}, u32[]{:S(2)}, u32[]{:S(2)}) collective-permute-start(bf16[224,896]{1,0:T(8,128)(2,1)S(1)} %bitcast.19), channel_id=1, source_target_pairs={{0,32},{32,0},{64,96},{96,64},{1,33},{33,1},{65,97},{97,65},{2,34}... | collective-permute-start | bytes 1204232 | tf_op jit(solution)/shard_map/ppermute | solution.py:25
  39.0 7.4 %collective-permute-start.8 = (bf16[224,896]{1,0:T(8,128)(2,1)S(1)}, bf16[224,896]{1,0:T(8,128)(2,1)S(1)}, u32[]{:S(2)}, u32[]{:S(2)}) collective-permute-start(bf16[224,896]{1,0:T(8,128)(2,1)S(1)} %bitcast.20), channel_id=1, source_target_pairs={{0,96},{96,0},{32,64},{64,32},{1,97},{97,1},{33,65},{65,33},{2,98}... | collective-permute-start | bytes 1204232 | tf_op jit(solution)/shard_map/ppermute | solution.py:25
  46.4 0.0 collective-permute-done.3.near
  46.4 1.9 %collective-permute-start.4 = (bf16[448,1792]{1,0:T(8,128)(2,1)S(1)}, bf16[448,1792]{1,0:T(8,128)(2,1)S(1)}, u32[]{:S(2)}, u32[]{:S(2)}) collective-permute-start(bf16[448,1792]{1,0:T(8,128)(2,1)S(1)} %get-tuple-element.44.pack), channel_id=1, source_target_pairs={{0,32},{32,0},{64,96},{96,64},{1,33},{33,1},{65,97},{97,65},{2,34}... | collective-permute-start | bytes 4816904 | tf_op jit(solution)/shard_map/ppermute | solution.py:25
  48.3 0.0 collective-permute-done.11.up
  48.3 2.5 %collective-permute-start.12 = (bf16[256,896]{1,0:T(8,128)(2,1)S(1)}, bf16[256,896]{1,0:T(8,128)(2,1)S(1)}, u32[]{:S(2)}, u32[]{:S(2)}) collective-permute-start(bf16[256,896]{1,0:T(8,128)(2,1)S(1)} %collective-permute-done.11.up), channel_id=1, source_target_pairs={{0,96},{64,32},{1,97},{65,33},{2,98},{66,34},{3,99},{67,35},{4,100... | collective-permute-start | bytes 1376264 | tf_op jit(solution)/shard_map/ppermute | solution.py:25
  50.8 0.0 collective-permute-done.7.i1
  50.8 6.3 %collective-permute-start.9 = (bf16[224,896]{1,0:T(8,128)(2,1)S(1)}, bf16[224,896]{1,0:T(8,128)(2,1)S(1)}, u32[]{:S(2)}, u32[]{:S(2)}) collective-permute-start(bf16[224,896]{1,0:T(8,128)(2,1)S(1)} %collective-permute-done.7.i1), channel_id=1, source_target_pairs={{0,96},{96,0},{32,64},{64,32},{1,97},{97,1},{33,65},{65,33},{2,98}... | collective-permute-start | bytes 1204232 | tf_op jit(solution)/shard_map/ppermute | solution.py:25
  57.2 1.9 %collective-permute-start.5 = (bf16[896,128]{1,0:T(8,128)(2,1)S(1)}, bf16[896,128]{1,0:T(8,128)(2,1)S(1)}, u32[]{:S(2)}, u32[]{:S(2)}) collective-permute-start(bf16[896,128]{1,0:T(8,128)(2,1)S(1)} %get-tuple-element.35), channel_id=1, source_target_pairs={{0,96},{96,0},{32,64},{64,32},{1,97},{97,1},{33,65},{65,33},{2,98}... | collective-permute-start | bytes 688136 | tf_op jit(solution)/shard_map/ppermute | solution.py:25
  59.1 0.0 collective-permute-done.8.i2
  59.1 3.5 %collective-permute-start.6 = (bf16[896,128]{1,0:T(8,128)(2,1)S(1)}, bf16[896,128]{1,0:T(8,128)(2,1)S(1)}, u32[]{:S(2)}, u32[]{:S(2)}) collective-permute-start(bf16[896,128]{1,0:T(8,128)(2,1)S(1)} %get-tuple-element.36), channel_id=1, source_target_pairs={{0,64},{64,0},{32,96},{96,32},{1,65},{65,1},{33,97},{97,33},{2,66}... | collective-permute-start | bytes 688136 | tf_op jit(solution)/shard_map/ppermute | solution.py:25
  63.3 8.0 %collective-permute-done.9.i3 = bf16[224,896]{1,0:T(8,128)(2,1)S(1)} collective-permute-done((bf16[224,896]{1,0:T(8,128)(2,1)S(1)}, bf16[224,896]{1,0:T(8,128)(2,1)S(1)}, u32[]{:S(2)}, u32[]{:S(2)}) %collective-permute-start.9) | collective-permute-done | bytes 401440 | tf_op jit(solution)/shard_map/ppermute | solution.py:25
  71.3 0.0 collective-permute-done.12.down
  71.4 1.1 shard_map.93
  72.4 3.8 %collective-permute-done.5.nxt = bf16[896,128]{1,0:T(8,128)(2,1)S(1)} collective-permute-done((bf16[896,128]{1,0:T(8,128)(2,1)S(1)}, bf16[896,128]{1,0:T(8,128)(2,1)S(1)}, u32[]{:S(2)}, u32[]{:S(2)}) %collective-permute-start.5) | collective-permute-done | bytes 229408 | tf_op jit(solution)/shard_map/ppermute | solution.py:25
  76.3 18.1 %collective-permute-done.6.far = bf16[896,128]{1,0:T(8,128)(2,1)S(1)} collective-permute-done((bf16[896,128]{1,0:T(8,128)(2,1)S(1)}, bf16[896,128]{1,0:T(8,128)(2,1)S(1)}, u32[]{:S(2)}, u32[]{:S(2)}) %collective-permute-start.6) | collective-permute-done | bytes 229408 | tf_op jit(solution)/shard_map/ppermute | solution.py:25
  94.3 1.3 shard_map.94
  95.6 31.4 %all_to_all.10 = bf16[128,4,128]{2,1,0:T(4,128)(2,1)S(1)} all-to-all(bf16[128,4,128]{2,1,0:T(4,128)(2,1)S(1)} %bitcast.22), channel_id=1, replica_groups=mesh['zl'=4,'x'=4,'y'=8,'zh'=2,'c'=2] {'zl','y','zh','c'}, dimensions={0} | all-to-all | bytes 262144 | tf_op jit(solution)/shard_map/all_to_all | solution.py:29
  127.0 0.1 convert_reduce_fusion
  127.2 17.5 %all_to_all.11 = bf16[128,4,128]{2,1,0:T(4,128)(2,1)S(1)} all-to-all(bf16[128,4,128]{2,1,0:T(4,128)(2,1)S(1)} %broadcast_in_dim.10), channel_id=1, replica_groups=mesh['zl'=4,'x'=4,'y'=8,'zh'=2,'c'=2] {'zl','y','zh','c'}, dimensions={0} | all-to-all | bytes 262144 | tf_op jit(solution)/shard_map/all_to_all | solution.py:29
  144.7 1.9 %shard_map.95.own = bf16[896,128]{1,0:T(8,128)(2,1)S(1)} custom-call(s32[1]{0:T(128)S(6)} %copy.10.rows, bf16[512,128]{1,0:T(8,128)(2,1)S(1)} %bitcast.18, bf16[512,512]{1,0:T(8,128)(2,1)S(1)} %copy-done.1, bf16[512,512]{1,0:T(8,128)(2,1)S(1)} %get-tuple-element.40.inv_t, bf16[896,128]{1,0:T(8,128)(2,1)S(1)} %get-tuple-element.41.fwd, ...), custom_call_target="tpu_custom_call" | custom-call | flops 457179136 | bytes 3932164 | tf_op jit(solution)/shard_map/pallas_call | solution.py:43
  146.6 1.9 %collective-permute-start.13 = (bf16[896,128]{1,0:T(8,128)(2,1)S(1)}, bf16[896,128]{1,0:T(8,128)(2,1)S(1)}, u32[]{:S(2)}, u32[]{:S(2)}) collective-permute-start(bf16[896,128]{1,0:T(8,128)(2,1)S(1)} %shard_map.95.own), channel_id=1, source_target_pairs={{0,32},{32,0},{64,96},{96,64},{1,33},{33,1},{65,97},{97,65},{2,34}... | collective-permute-start | bytes 688136 | tf_op jit(solution)/shard_map/ppermute | solution.py:25
  148.5 2.7 %collective-permute-start.14 = (bf16[896,128]{1,0:T(8,128)(2,1)S(1)}, bf16[896,128]{1,0:T(8,128)(2,1)S(1)}, u32[]{:S(2)}, u32[]{:S(2)}) collective-permute-start(bf16[896,128]{1,0:T(8,128)(2,1)S(1)} %shard_map.95.own), channel_id=1, source_target_pairs={{0,96},{96,0},{32,64},{64,32},{1,97},{97,1},{33,65},{65,33},{2,98}... | collective-permute-start | bytes 688136 | tf_op jit(solution)/shard_map/ppermute | solution.py:25
  151.2 4.5 %collective-permute-start.15 = (bf16[896,128]{1,0:T(8,128)(2,1)S(1)}, bf16[896,128]{1,0:T(8,128)(2,1)S(1)}, u32[]{:S(2)}, u32[]{:S(2)}) collective-permute-start(bf16[896,128]{1,0:T(8,128)(2,1)S(1)} %shard_map.95.own), channel_id=1, source_target_pairs={{0,64},{64,0},{32,96},{96,32},{1,65},{65,1},{33,97},{97,33},{2,66}... | collective-permute-start | bytes 688136 | tf_op jit(solution)/shard_map/ppermute | solution.py:25
  155.8 0.0 collective-permute-done.4.came
  155.8 2.6 %shard_map.96 = (bf16[384,896]{1,0:T(8,128)(2,1)S(1)}, bf16[384,384]{1,0:T(8,128)(2,1)S(1)}, f32[384,512]{1,0:T(8,128)S(1)}) custom-call(s32[1]{0:T(128)} %bitcast.at, bf16[448,1792]{1,0:T(8,128)(2,1)S(1)} %get-tuple-element.44.pack, bf16[448,1792]{1,0:T(8,128)(2,1)S(1)} %collective-permute-done.4.came, bf16[448,896]{1,0:T(8,128)(2,1)S(1)} %bitcast.13, ...), custom_call_target="tpu_custom_call" | custom-call | flops 1585446912 | bytes 5849092 | tf_op jit(solution)/shard_map/pallas_call | solution.py:43
  158.5 0.0 collective-permute-done.13.near
  158.5 4.9 %collective-permute-done.14.nxt = bf16[896,128]{1,0:T(8,128)(2,1)S(1)} collective-permute-done((bf16[896,128]{1,0:T(8,128)(2,1)S(1)}, bf16[896,128]{1,0:T(8,128)(2,1)S(1)}, u32[]{:S(2)}, u32[]{:S(2)}) %collective-permute-start.14) | collective-permute-done | bytes 229408 | tf_op jit(solution)/shard_map/ppermute | solution.py:25
  163.4 1.8 %shard_map.97 = bf16[384,512]{1,0:T(8,128)(2,1)} custom-call(s32[1]{0:T(128)} %bitcast.at, bf16[384,896]{1,0:T(8,128)(2,1)S(1)} %get-tuple-element.47.fold_t, bf16[384,384]{1,0:T(8,128)(2,1)S(1)} %get-tuple-element.48.inv_t, f32[384,512]{1,0:T(8,128)S(1)} %get-tuple-element.49.rest, bf16[896,128]{1,0:T(8,128)(2,1)S(1)} %shard_map.95.own, ...), custom_call_target="tpu_custom_call" | custom-call | flops 503316480 | bytes 2686980 | tf_op jit(solution)/shard_map/pallas_call | solution.py:43
  (18 shorter events, 0.1 us)
Async XLA Ops:
  0.0 14.7 %copy-start.2 = (bf16[1,128,896]{2,1,0:T(8,128)(2,1)S(1)}, bf16[1,128,896]{2,1,0:T(8,128)(2,1)}, u32[]{:S(2)}) copy-start(bf16[1,128,896]{2,1,0:T(8,128)(2,1)} %param.15) | copy-start | bytes 688132
  1.3 30.2 %copy-start = (bf16[1,448,896]{2,1,0:T(8,128)(2,1)S(1)}, bf16[1,448,896]{2,1,0:T(8,128)(2,1)}, u32[]{:S(2)}) copy-start(bf16[1,448,896]{2,1,0:T(8,128)(2,1)} %param.13) | copy-start | bytes 2408452
  1.3 30.2 %copy-start.3 = (bf16[1,448,896]{2,1,0:T(8,128)(2,1)S(1)}, bf16[1,448,896]{2,1,0:T(8,128)(2,1)}, u32[]{:S(2)}) copy-start(bf16[1,448,896]{2,1,0:T(8,128)(2,1)} %param.12) | copy-start | bytes 2408452
  1.3 22.7 %collective-permute-start.2 = (bf16[448,512]{1,0:T(8,128)(2,1)S(1)}, bf16[448,512]{1,0:T(8,128)(2,1)S(1)}, u32[]{:S(2)}, u32[]{:S(2)}) collective-permute-start(bf16[448,512]{1,0:T(8,128)(2,1)S(1)} %slice_select_fusion), channel_id=1, source_target_pairs={{0,32},{32,0},{64,96},{96,64},{1,33},{33,1},{65,97},{97,65},{2,34}... | collective-permute-start | bytes 1376264 | tf_op jit(solution)/shard_map/ppermute | solution.py:25
  5.4 1.1 copy-start.5
  6.5 1.0 copy-start.7
  7.5 1.0 copy-start.8
  9.4 14.7 %collective-permute-start = (bf16[448,512]{1,0:T(8,128)(2,1)S(1)}, bf16[448,512]{1,0:T(8,128)(2,1)S(1)}, u32[]{:S(2)}, u32[]{:S(2)}) collective-permute-start(bf16[448,512]{1,0:T(8,128)(2,1)S(1)} %get-tuple-element.28.top), channel_id=1, source_target_pairs={{0,32},{32,0},{64,96},{96,64},{1,33},{33,1},{65,97},{97,65},{2,34}... | collective-permute-start | bytes 1376264 | tf_op jit(solution)/shard_map/ppermute | solution.py:25
  11.3 20.1 %collective-permute-start.1 = (bf16[448,512]{1,0:T(8,128)(2,1)S(1)}, bf16[448,512]{1,0:T(8,128)(2,1)S(1)}, u32[]{:S(2)}, u32[]{:S(2)}) collective-permute-start(bf16[448,512]{1,0:T(8,128)(2,1)S(1)} %get-tuple-element.29.bot), channel_id=1, source_target_pairs={{0,32},{64,96},{1,33},{65,97},{2,34},{66,98},{3,35},{67,99},{4,36}... | collective-permute-start | bytes 1376264 | tf_op jit(solution)/shard_map/ppermute | solution.py:25
  14.7 8.0 %collective-permute-start.10 = (bf16[128,896]{1,0:T(8,128)(2,1)S(1)}, bf16[128,896]{1,0:T(8,128)(2,1)S(1)}, u32[]{:S(2)}, u32[]{:S(2)}) collective-permute-start(bf16[128,896]{1,0:T(8,128)(2,1)S(1)} %bitcast.14), channel_id=1, source_target_pairs={{0,96},{96,0},{32,64},{64,32},{1,97},{97,1},{33,65},{65,33},{2,98}... | collective-permute-start | bytes 688136 | tf_op jit(solution)/shard_map/ppermute | solution.py:25
  22.7 25.6 %collective-permute-start.11 = (bf16[256,896]{1,0:T(8,128)(2,1)S(1)}, bf16[256,896]{1,0:T(8,128)(2,1)S(1)}, u32[]{:S(2)}, u32[]{:S(2)}) collective-permute-start(bf16[256,896]{1,0:T(8,128)(2,1)S(1)} %pad_maximum_fusion), channel_id=1, source_target_pairs={{32,0},{96,64},{33,1},{97,65},{34,2},{98,66},{35,3},{99,67},{36,4}... | collective-permute-start | bytes 1376264 | tf_op jit(solution)/shard_map/ppermute | solution.py:25
  31.5 5.6 %copy-start.4 = (bf16[1,224,896]{2,1,0:T(8,128)(2,1)S(1)}, bf16[1,224,896]{2,1,0:T(8,128)(2,1)}, u32[]{:S(2)}) copy-start(bf16[1,224,896]{2,1,0:T(8,128)(2,1)} %param.14) | copy-start | bytes 1204228
  31.5 39.9 %copy-start.1 = (bf16[512,512]{1,0:T(8,128)(2,1)S(1)}, bf16[512,512]{1,0:T(8,128)(2,1)}, u32[]{:S(2)}) copy-start(bf16[512,512]{1,0:T(8,128)(2,1)} %inv.1) | copy-start | bytes 1572868
  32.9 13.5 %collective-permute-start.3 = (bf16[896,128]{1,0:T(8,128)(2,1)S(1)}, bf16[896,128]{1,0:T(8,128)(2,1)S(1)}, u32[]{:S(2)}, u32[]{:S(2)}) collective-permute-start(bf16[896,128]{1,0:T(8,128)(2,1)S(1)} %get-tuple-element.31), channel_id=1, source_target_pairs={{0,32},{32,0},{64,96},{96,64},{1,33},{33,1},{65,97},{97,65},{2,34}... | collective-permute-start | bytes 688136 | tf_op jit(solution)/shard_map/ppermute | solution.py:25
  37.0 13.8 %collective-permute-start.7 = (bf16[224,896]{1,0:T(8,128)(2,1)S(1)}, bf16[224,896]{1,0:T(8,128)(2,1)S(1)}, u32[]{:S(2)}, u32[]{:S(2)}) collective-permute-start(bf16[224,896]{1,0:T(8,128)(2,1)S(1)} %bitcast.19), channel_id=1, source_target_pairs={{0,32},{32,0},{64,96},{96,64},{1,33},{33,1},{65,97},{97,65},{2,34}... | collective-permute-start | bytes 1204232 | tf_op jit(solution)/shard_map/ppermute | solution.py:25
  39.0 20.1 %collective-permute-start.8 = (bf16[224,896]{1,0:T(8,128)(2,1)S(1)}, bf16[224,896]{1,0:T(8,128)(2,1)S(1)}, u32[]{:S(2)}, u32[]{:S(2)}) collective-permute-start(bf16[224,896]{1,0:T(8,128)(2,1)S(1)} %bitcast.20), channel_id=1, source_target_pairs={{0,96},{96,0},{32,64},{64,32},{1,97},{97,1},{33,65},{65,33},{2,98}... | collective-permute-start | bytes 1204232 | tf_op jit(solution)/shard_map/ppermute | solution.py:25
  46.4 109.4 %collective-permute-start.4 = (bf16[448,1792]{1,0:T(8,128)(2,1)S(1)}, bf16[448,1792]{1,0:T(8,128)(2,1)S(1)}, u32[]{:S(2)}, u32[]{:S(2)}) collective-permute-start(bf16[448,1792]{1,0:T(8,128)(2,1)S(1)} %get-tuple-element.44.pack), channel_id=1, source_target_pairs={{0,32},{32,0},{64,96},{96,64},{1,33},{33,1},{65,97},{97,65},{2,34}... | collective-permute-start | bytes 4816904 | tf_op jit(solution)/shard_map/ppermute | solution.py:25
  48.3 23.0 %collective-permute-start.12 = (bf16[256,896]{1,0:T(8,128)(2,1)S(1)}, bf16[256,896]{1,0:T(8,128)(2,1)S(1)}, u32[]{:S(2)}, u32[]{:S(2)}) collective-permute-start(bf16[256,896]{1,0:T(8,128)(2,1)S(1)} %collective-permute-done.11.up), channel_id=1, source_target_pairs={{0,96},{64,32},{1,97},{65,33},{2,98},{66,34},{3,99},{67,35},{4,100... | collective-permute-start | bytes 1376264 | tf_op jit(solution)/shard_map/ppermute | solution.py:25
  50.8 20.5 %collective-permute-start.9 = (bf16[224,896]{1,0:T(8,128)(2,1)S(1)}, bf16[224,896]{1,0:T(8,128)(2,1)S(1)}, u32[]{:S(2)}, u32[]{:S(2)}) collective-permute-start(bf16[224,896]{1,0:T(8,128)(2,1)S(1)} %collective-permute-done.7.i1), channel_id=1, source_target_pairs={{0,96},{96,0},{32,64},{64,32},{1,97},{97,1},{33,65},{65,33},{2,98}... | collective-permute-start | bytes 1204232 | tf_op jit(solution)/shard_map/ppermute | solution.py:25
  57.2 19.1 %collective-permute-start.5 = (bf16[896,128]{1,0:T(8,128)(2,1)S(1)}, bf16[896,128]{1,0:T(8,128)(2,1)S(1)}, u32[]{:S(2)}, u32[]{:S(2)}) collective-permute-start(bf16[896,128]{1,0:T(8,128)(2,1)S(1)} %get-tuple-element.35), channel_id=1, source_target_pairs={{0,96},{96,0},{32,64},{64,32},{1,97},{97,1},{33,65},{65,33},{2,98}... | collective-permute-start | bytes 688136 | tf_op jit(solution)/shard_map/ppermute | solution.py:25
  59.1 35.2 %collective-permute-start.6 = (bf16[896,128]{1,0:T(8,128)(2,1)S(1)}, bf16[896,128]{1,0:T(8,128)(2,1)S(1)}, u32[]{:S(2)}, u32[]{:S(2)}) collective-permute-start(bf16[896,128]{1,0:T(8,128)(2,1)S(1)} %get-tuple-element.36), channel_id=1, source_target_pairs={{0,64},{64,0},{32,96},{96,32},{1,65},{65,1},{33,97},{97,33},{2,66}... | collective-permute-start | bytes 688136 | tf_op jit(solution)/shard_map/ppermute | solution.py:25
  144.7 11.1 %copy-start.6 = (bf16[1,1,896,384]{3,2,1,0:T(8,128)(2,1)S(1)}, bf16[1,1,896,384]{3,2,1,0:T(8,128)(2,1)}, u32[]{:S(2)}) copy-start(bf16[1,1,896,384]{3,2,1,0:T(8,128)(2,1)} %param.11) | copy-start | bytes 2064388
  144.7 11.1 %copy-start.9 = (bf16[1,1,384,384]{3,2,1,0:T(8,128)(2,1)S(1)}, bf16[1,1,384,384]{3,2,1,0:T(8,128)(2,1)}, u32[]{:S(2)}) copy-start(bf16[1,1,384,384]{3,2,1,0:T(8,128)(2,1)} %param.10) | copy-start | bytes 884740
  146.6 11.9 %collective-permute-start.13 = (bf16[896,128]{1,0:T(8,128)(2,1)S(1)}, bf16[896,128]{1,0:T(8,128)(2,1)S(1)}, u32[]{:S(2)}, u32[]{:S(2)}) collective-permute-start(bf16[896,128]{1,0:T(8,128)(2,1)S(1)} %shard_map.95.own), channel_id=1, source_target_pairs={{0,32},{32,0},{64,96},{96,64},{1,33},{33,1},{65,97},{97,65},{2,34}... | collective-permute-start | bytes 688136 | tf_op jit(solution)/shard_map/ppermute | solution.py:25
  148.5 14.8 %collective-permute-start.14 = (bf16[896,128]{1,0:T(8,128)(2,1)S(1)}, bf16[896,128]{1,0:T(8,128)(2,1)S(1)}, u32[]{:S(2)}, u32[]{:S(2)}) collective-permute-start(bf16[896,128]{1,0:T(8,128)(2,1)S(1)} %shard_map.95.own), channel_id=1, source_target_pairs={{0,96},{96,0},{32,64},{64,32},{1,97},{97,1},{33,65},{65,33},{2,98}... | collective-permute-start | bytes 688136 | tf_op jit(solution)/shard_map/ppermute | solution.py:25
  151.2 12.1 %collective-permute-start.15 = (bf16[896,128]{1,0:T(8,128)(2,1)S(1)}, bf16[896,128]{1,0:T(8,128)(2,1)S(1)}, u32[]{:S(2)}, u32[]{:S(2)}) collective-permute-start(bf16[896,128]{1,0:T(8,128)(2,1)S(1)} %shard_map.95.own), channel_id=1, source_target_pairs={{0,64},{64,0},{32,96},{96,32},{1,65},{65,1},{33,97},{97,33},{2,66}... | collective-permute-start | bytes 688136 | tf_op jit(solution)/shard_map/ppermute | solution.py:25

commit v5 on v4

--- a/solution.py
+++ b/solution.py
@@ -49,7 +49,7 @@
         ],
         out_specs=[space] * len(outs),
         scratch_shapes=[pltpu.VMEM(s, d) for s, d in scratch],
-        compiler_params=pltpu.CompilerParams(vmem_limit_bytes=24 << 20),
+        compiler_params=pltpu.CompilerParams(vmem_limit_bytes=16 << 20),
         cost_estimate=pl.CostEstimate(flops=flops, bytes_accessed=moved, transcendentals=0),
     )(*args)
 
@@ -58,11 +58,38 @@
     return x ^ 1, 3 - x, x ^ 2
 
 
-def leaf_kernel(loads, inv, coup, fwd, top, bot):
-    fwd[...] = mul(inv[...], loads[...]).astype(BF)
+def leaf_kernel(loads_hbm, inv_hbm, coup_hbm, top, bot, loads, inv, coup, sems):
+    copies = [
+        pltpu.make_async_copy(src, dst, sems.at[n])
+        for n, (src, dst) in enumerate(
+            ((loads_hbm, loads), (inv_hbm, inv), (coup_hbm, coup))
+        )
+    ]
+    for copy in copies:
+        copy.start()
+    copies[0].wait()
+    copies[1].wait()
+    fwd = mul(inv[...], loads[...]).astype(BF)
+    copies[2].wait()
     half = top.shape[0]
-    top[...] = mul(coup[:half], fwd[...]).astype(BF)
-    bot[...] = mul(coup[half:], fwd[...]).astype(BF)
+    bot[...] = mul(coup[half:], fwd).astype(BF)
+    top[...] = mul(coup[:half], fwd).astype(BF)
+
+
+def leaf_call(loads, inv, coup, half):
+    args = [pltpu.with_memory_space_constraint(a, pltpu.HBM) for a in (loads, inv, coup)]
+    ports = loads.shape[1]
+    shape = jax.ShapeDtypeStruct((half, ports), BF)
+    return pl.pallas_call(
+        leaf_kernel,
+        name="k_leaf",
+        out_shape=[shape, shape],
+        in_specs=[pl.BlockSpec(memory_space=pltpu.HBM)] * 3,
+        out_specs=[pl.BlockSpec(memory_space=pltpu.VMEM)] * 2,
+        scratch_shapes=[pltpu.VMEM(a.shape, a.dtype) for a in (loads, inv, coup)]
+        + [pltpu.SemaphoreType.DMA((3,))],
+        compiler_params=pltpu.CompilerParams(vmem_limit_bytes=8 << 20),
+    )(*args)
 
 
 def first_kernel(at, inv, top, bot, came_top, came_bot, coup, came_coup, pack, own, near, nxt, far, rhs, held, turned):
@@ -101,7 +128,7 @@
     return zip((x,) + others(x), refs)
 
 
-def join_kernel(at, i0, i1, i2, i3, b0, up, nxt, down, border_inv, inv, inv_t, coup, coup_t, border_t):
+def join_kernel(at, i0, i1, i2, i3, b0, up, nxt, down, inv, coup):
     x = at[0]
     each = i0.shape[0]
     for who, ref in pieces(x, (i0, i1, i2, i3)):
@@ -111,9 +138,6 @@
     far = up[count:] + down[:count]
     for who, block in pieces(x, (b0[...], near, nxt[...], far)):
         coup[pl.ds(pl.multiple_of(who * count, count), count)] = block
-    inv_t[...] = inv[...].T
-    coup_t[...] = coup[...].T
-    border_t[...] = border_inv[...].T
 
 
 def second_kernel(rows, own, near, nxt, far, inv, coup, fwd, tiles):
@@ -125,16 +149,16 @@
     tiles[...] = jnp.where(live, part, 0.0).astype(BF)
 
 
-def border_kernel(rows, rhs, inv, inv_t, fwd, second_t, coup_t, back):
+def border_kernel(rows, rhs, inv, fwd, second, coup, back):
     mid = mul(inv[...], rhs[...]).astype(BF)
-    end = mul(inv_t[...], mid)
+    end = mul_t(inv[...], mid)
     live = lax.broadcasted_iota(jnp.int32, end.shape, 0) < rows[0]
     sol = jnp.where(live, end, 0.0).astype(BF)
-    diff = (fwd[...].astype(F32) - mul(coup_t[...], sol)).astype(BF)
-    back[...] = mul(second_t[...], diff).astype(BF)
-
-
-def fold_kernel(at, pack, came, coup, came_coup, leaf_coup, fwd_leaf, leaf_inv, fold_t, inv_t, rest, full, fold):
+    diff = (fwd[...].astype(F32) - mul_t(coup[...], sol)).astype(BF)
+    back[...] = mul_t(second[...], diff).astype(BF)
+
+
+def fold_kernel(at, pack, came, coup, came_coup, leaf_coup, loads, leaf_inv, fold_t, inv_t, rest, full, fold):
     high = at[0] % 2
     half, sep = coup.shape
     width = came_coup.shape[1]
@@ -145,7 +169,7 @@
     full[pl.ds(mine_at, half)] = mine
     full[pl.ds(other_at, half)] = other
     rest[...] = (
-        fwd_leaf[...].astype(F32)
+        mul(leaf_inv[...], loads[...]).astype(BF).astype(F32)
         - mul_t(mine, pack[:, sep + sep - width :])
         - mul_t(other, came[:, sep + sep - width :])
     )
@@ -194,15 +218,7 @@
     inv_two, coup_border = second_inverse[0], border_coupling[0]
     i_near = send(inv_two, NEAR)
     b_next = send(coup_border, NEXT)
-    fwd_leaf, top, bot = call(
-        leaf_kernel,
-        [((leaf, ports), BF), ((half, ports), BF), ((half, ports), BF)],
-        [],
-        loads,
-        leaf_inv,
-        leaf_coup,
-        flops=2 * leaf * ports * (leaf + sep),
-    )
+    top, bot = leaf_call(loads, leaf_inv, leaf_coup, half)
     came_bot = send(bot, DOWN)
     b_up = send(jnp.concatenate([coup_border, b_next], 0), UP)
     window = jnp.where(low, coup_two[:, sep - width :], coup_two[:, :width])
@@ -231,15 +247,9 @@
     nxt = send(nxt, NEXT)
     late_pack, near = lax.optimization_barrier((pack, near))
     came_pack = send(late_pack, NEAR)
-    inv_full, inv_full_t, coup_full, coup_full_t, border_t = call(
+    inv_full, coup_full = call(
         join_kernel,
-        [
-            ((sep, sep), BF),
-            ((sep, sep), BF),
-            ((border, sep), BF),
-            ((sep, border), BF),
-            ((border, border), BF),
-        ],
+        [((sep, sep), BF), ((border, sep), BF)],
         [],
         at,
         inv_two,
@@ -250,7 +260,6 @@
         b_up,
         b_next,
         b_down,
-        border_inverse,
     )
     fwd_two, tiles = call(
         second_kernel,
@@ -276,10 +285,9 @@
         border_rows,
         rhs_border,
         border_inverse,
-        border_t,
         fwd_two,
-        inv_full_t,
-        coup_full_t,
+        inv_full,
+        coup_full,
         flops=2 * share * (2 * border * border + border * sep + sep * sep),
     )
     back_far = send(back_two, ACROSS)
@@ -296,7 +304,7 @@
         coup_two,
         came_coup,
         leaf_coup,
-        fwd_leaf,
+        loads,
         leaf_inv,
         flops=2 * sep * leaf * (2 * sep + ports),
     )

time: 166 us -> 165 us (level)
  local copies, waits for them, and re-layouts: 3.12 us -> 0.07 us
    unnamed x20 -> x16, local copies, waits for them, and re-layouts: 3.08 us -> 0.03 us
    pallas_call x0 -> x1, Pallas kernels: none -> 2.12 us  [leaf_call(): pl.pallas_call(leaf_kernel, name='k_leaf', out_shape=[shape, shape], in_s...]
    pallas_call x7 -> x6, Pallas kernels: 11.1 us -> 9.49 us  [call(): pl.pallas_call(kernel, out_shape=[jax.ShapeDtypeStruct(s, d) for s, d in...]
where the time goes in v5:
time: 165 us; the launch traced here: 164 us
  starting transfers between devices  52.4 us (32%)
  blocking collectives  48.9 us (30%)
  waiting for transfers between devices  48.8 us (30%)
  Pallas kernels  11.6 us (7%)
    ppermute x16, starting transfers between devices, send(): return lax.ppermute(x, 'x', pairs)  52.4 us
    all_to_all x2, blocking collectives, to_group(): return lax.all_to_all(tiles, GROUP, split_axis=0, concat_axis=0, tiled=True)  48.9 us
    ppermute x16, waiting for transfers between devices, send(): return lax.ppermute(x, 'x', pairs)  48.8 us
    pallas_call x6, Pallas kernels, call(): pl.pallas_call(kernel, out_shape=[jax.ShapeDtypeStruct(s, d) for s, d in...  9.49 us
  transfers between devices with their start and end apart: 16, of which 6 were waited for; matrix products, arithmetic and copies ran while one was open for 0% of the time, Pallas kernels for 6%

profile of v5, /device:TPU:1, one launch (start us, length us, event | category | flops | bytes accessed | tf_op | source)
XLA Modules:
  0.0 164.2 jit_solution(16798474983127048785)
XLA Ops:
  0.0 1.3 slice_select_fusion
  1.4 3.9 %collective-permute-start.2 = (bf16[448,512]{1,0:T(8,128)(2,1)S(1)}, bf16[448,512]{1,0:T(8,128)(2,1)S(1)}, u32[]{:S(2)}, u32[]{:S(2)}) collective-permute-start(bf16[448,512]{1,0:T(8,128)(2,1)S(1)} %slice_select_fusion), channel_id=1, source_target_pairs={{0,32},{32,0},{64,96},{96,64},{1,33},{33,1},{65,97},{97,65},{2,34}... | collective-permute-start | bytes 1376264 | tf_op jit(solution)/shard_map/ppermute | solution.py:25
  5.3 2.1 %k_leaf.1 = (bf16[448,512]{1,0:T(8,128)(2,1)S(1)}, bf16[448,512]{1,0:T(8,128)(2,1)S(1)}) custom-call(bf16[384,512]{1,0:T(8,128)(2,1)} %bitcast.24, bf16[384,384]{1,0:T(8,128)(2,1)} %bitcast.26, bf16[896,384]{1,0:T(8,128)(2,1)} %bitcast.18), custom_call_target="tpu_custom_call" | custom-call | tf_op jit(solution)/shard_map/k_leaf/pallas_call | solution.py:83
  7.4 1.9 %collective-permute-start = (bf16[448,512]{1,0:T(8,128)(2,1)S(1)}, bf16[448,512]{1,0:T(8,128)(2,1)S(1)}, u32[]{:S(2)}, u32[]{:S(2)}) collective-permute-start(bf16[448,512]{1,0:T(8,128)(2,1)S(1)} %get-tuple-element.24.top), channel_id=1, source_target_pairs={{0,32},{32,0},{64,96},{96,64},{1,33},{33,1},{65,97},{97,65},{2,34}... | collective-permute-start | bytes 1376264 | tf_op jit(solution)/shard_map/ppermute | solution.py:25
  9.4 3.4 %collective-permute-start.1 = (bf16[448,512]{1,0:T(8,128)(2,1)S(1)}, bf16[448,512]{1,0:T(8,128)(2,1)S(1)}, u32[]{:S(2)}, u32[]{:S(2)}) collective-permute-start(bf16[448,512]{1,0:T(8,128)(2,1)S(1)} %get-tuple-element.25.bot), channel_id=1, source_target_pairs={{0,32},{64,96},{1,33},{65,97},{2,34},{66,98},{3,35},{67,99},{4,36}... | collective-permute-start | bytes 1376264 | tf_op jit(solution)/shard_map/ppermute | solution.py:25
  12.7 0.0 copy-done.1
  12.8 2.5 %collective-permute-start.10 = (bf16[128,896]{1,0:T(8,128)(2,1)S(1)}, bf16[128,896]{1,0:T(8,128)(2,1)S(1)}, u32[]{:S(2)}, u32[]{:S(2)}) collective-permute-start(bf16[128,896]{1,0:T(8,128)(2,1)S(1)} %bitcast.14), channel_id=1, source_target_pairs={{0,96},{96,0},{32,64},{64,32},{1,97},{97,1},{33,65},{65,33},{2,98}... | collective-permute-start | bytes 688136 | tf_op jit(solution)/shard_map/ppermute | solution.py:25
  15.3 5.4 %collective-permute-done.10.nxt = bf16[128,896]{1,0:T(8,128)(2,1)S(1)} collective-permute-done((bf16[128,896]{1,0:T(8,128)(2,1)S(1)}, bf16[128,896]{1,0:T(8,128)(2,1)S(1)}, u32[]{:S(2)}, u32[]{:S(2)}) %collective-permute-start.10) | collective-permute-done | bytes 229408 | tf_op jit(solution)/shard_map/ppermute | solution.py:25
  20.8 1.3 collective-permute-start.11
  22.1 0.0 collective-permute-done.2.came_coup
  22.1 0.0 collective-permute-done.came_top
  22.1 8.2 %collective-permute-done.1.came_bot = bf16[448,512]{1,0:T(8,128)(2,1)S(1)} collective-permute-done((bf16[448,512]{1,0:T(8,128)(2,1)S(1)}, bf16[448,512]{1,0:T(8,128)(2,1)S(1)}, u32[]{:S(2)}, u32[]{:S(2)}) %collective-permute-start.1) | collective-permute-done | bytes 458784 | tf_op jit(solution)/shard_map/ppermute | solution.py:25
  30.3 0.0 copy-done
  30.3 1.4 shard_map.91
  31.7 4.1 %collective-permute-start.3 = (bf16[896,128]{1,0:T(8,128)(2,1)S(1)}, bf16[896,128]{1,0:T(8,128)(2,1)S(1)}, u32[]{:S(2)}, u32[]{:S(2)}) collective-permute-start(bf16[896,128]{1,0:T(8,128)(2,1)S(1)} %get-tuple-element.27), channel_id=1, source_target_pairs={{0,32},{32,0},{64,96},{96,64},{1,33},{33,1},{65,97},{97,65},{2,34}... | collective-permute-start | bytes 688136 | tf_op jit(solution)/shard_map/ppermute | solution.py:25
  35.9 1.9 %collective-permute-start.7 = (bf16[224,896]{1,0:T(8,128)(2,1)S(1)}, bf16[224,896]{1,0:T(8,128)(2,1)S(1)}, u32[]{:S(2)}, u32[]{:S(2)}) collective-permute-start(bf16[224,896]{1,0:T(8,128)(2,1)S(1)} %bitcast.21), channel_id=1, source_target_pairs={{0,32},{32,0},{64,96},{96,64},{1,33},{33,1},{65,97},{97,65},{2,34}... | collective-permute-start | bytes 1204232 | tf_op jit(solution)/shard_map/ppermute | solution.py:25
  37.8 8.5 %collective-permute-start.8 = (bf16[224,896]{1,0:T(8,128)(2,1)S(1)}, bf16[224,896]{1,0:T(8,128)(2,1)S(1)}, u32[]{:S(2)}, u32[]{:S(2)}) collective-permute-start(bf16[224,896]{1,0:T(8,128)(2,1)S(1)} %bitcast.22), channel_id=1, source_target_pairs={{0,96},{96,0},{32,64},{64,32},{1,97},{97,1},{33,65},{65,33},{2,98}... | collective-permute-start | bytes 1204232 | tf_op jit(solution)/shard_map/ppermute | solution.py:25
  46.3 0.0 collective-permute-done.3.near
  46.3 1.9 %collective-permute-start.4 = (bf16[448,1792]{1,0:T(8,128)(2,1)S(1)}, bf16[448,1792]{1,0:T(8,128)(2,1)S(1)}, u32[]{:S(2)}, u32[]{:S(2)}) collective-permute-start(bf16[448,1792]{1,0:T(8,128)(2,1)S(1)} %get-tuple-element.37.pack), channel_id=1, source_target_pairs={{0,32},{32,0},{64,96},{96,64},{1,33},{33,1},{65,97},{97,65},{2,34}... | collective-permute-start | bytes 4816904 | tf_op jit(solution)/shard_map/ppermute | solution.py:25
  48.2 0.0 collective-permute-done.11.up
  48.2 2.5 %collective-permute-start.12 = (bf16[256,896]{1,0:T(8,128)(2,1)S(1)}, bf16[256,896]{1,0:T(8,128)(2,1)S(1)}, u32[]{:S(2)}, u32[]{:S(2)}) collective-permute-start(bf16[256,896]{1,0:T(8,128)(2,1)S(1)} %collective-permute-done.11.up), channel_id=1, source_target_pairs={{0,96},{64,32},{1,97},{65,33},{2,98},{66,34},{3,99},{67,35},{4,100... | collective-permute-start | bytes 1376264 | tf_op jit(solution)/shard_map/ppermute | solution.py:25
  50.7 0.0 collective-permute-done.7.i1
  50.7 6.3 %collective-permute-start.9 = (bf16[224,896]{1,0:T(8,128)(2,1)S(1)}, bf16[224,896]{1,0:T(8,128)(2,1)S(1)}, u32[]{:S(2)}, u32[]{:S(2)}) collective-permute-start(bf16[224,896]{1,0:T(8,128)(2,1)S(1)} %collective-permute-done.7.i1), channel_id=1, source_target_pairs={{0,96},{96,0},{32,64},{64,32},{1,97},{97,1},{33,65},{65,33},{2,98}... | collective-permute-start | bytes 1204232 | tf_op jit(solution)/shard_map/ppermute | solution.py:25
  57.1 1.9 %collective-permute-start.5 = (bf16[896,128]{1,0:T(8,128)(2,1)S(1)}, bf16[896,128]{1,0:T(8,128)(2,1)S(1)}, u32[]{:S(2)}, u32[]{:S(2)}) collective-permute-start(bf16[896,128]{1,0:T(8,128)(2,1)S(1)} %get-tuple-element.31), channel_id=1, source_target_pairs={{0,96},{96,0},{32,64},{64,32},{1,97},{97,1},{33,65},{65,33},{2,98}... | collective-permute-start | bytes 688136 | tf_op jit(solution)/shard_map/ppermute | solution.py:25
  59.0 0.0 collective-permute-done.8.i2
  59.0 3.6 %collective-permute-start.6 = (bf16[896,128]{1,0:T(8,128)(2,1)S(1)}, bf16[896,128]{1,0:T(8,128)(2,1)S(1)}, u32[]{:S(2)}, u32[]{:S(2)}) collective-permute-start(bf16[896,128]{1,0:T(8,128)(2,1)S(1)} %get-tuple-element.32), channel_id=1, source_target_pairs={{0,64},{64,0},{32,96},{96,32},{1,65},{65,1},{33,97},{97,33},{2,66}... | collective-permute-start | bytes 688136 | tf_op jit(solution)/shard_map/ppermute | solution.py:25
  63.2 8.0 %collective-permute-done.9.i3 = bf16[224,896]{1,0:T(8,128)(2,1)S(1)} collective-permute-done((bf16[224,896]{1,0:T(8,128)(2,1)S(1)}, bf16[224,896]{1,0:T(8,128)(2,1)S(1)}, u32[]{:S(2)}, u32[]{:S(2)}) %collective-permute-start.9) | collective-permute-done | bytes 401440 | tf_op jit(solution)/shard_map/ppermute | solution.py:25
  71.2 0.0 collective-permute-done.12.down
  71.2 0.2 shard_map.92
  71.5 4.7 %collective-permute-done.5.nxt = bf16[896,128]{1,0:T(8,128)(2,1)S(1)} collective-permute-done((bf16[896,128]{1,0:T(8,128)(2,1)S(1)}, bf16[896,128]{1,0:T(8,128)(2,1)S(1)}, u32[]{:S(2)}, u32[]{:S(2)}) %collective-permute-start.5) | collective-permute-done | bytes 229408 | tf_op jit(solution)/shard_map/ppermute | solution.py:25
  76.2 18.1 %collective-permute-done.6.far = bf16[896,128]{1,0:T(8,128)(2,1)S(1)} collective-permute-done((bf16[896,128]{1,0:T(8,128)(2,1)S(1)}, bf16[896,128]{1,0:T(8,128)(2,1)S(1)}, u32[]{:S(2)}, u32[]{:S(2)}) %collective-permute-start.6) | collective-permute-done | bytes 229408 | tf_op jit(solution)/shard_map/ppermute | solution.py:25
  94.2 1.3 shard_map.93
  95.5 31.4 %all_to_all.10 = bf16[128,4,128]{2,1,0:T(4,128)(2,1)S(1)} all-to-all(bf16[128,4,128]{2,1,0:T(4,128)(2,1)S(1)} %bitcast.28), channel_id=1, replica_groups=mesh['zl'=4,'x'=4,'y'=8,'zh'=2,'c'=2] {'zl','y','zh','c'}, dimensions={0} | all-to-all | bytes 262144 | tf_op jit(solution)/shard_map/all_to_all | solution.py:29
  126.9 0.1 convert_reduce_fusion
  127.1 17.5 %all_to_all.11 = bf16[128,4,128]{2,1,0:T(4,128)(2,1)S(1)} all-to-all(bf16[128,4,128]{2,1,0:T(4,128)(2,1)S(1)} %broadcast_in_dim.10), channel_id=1, replica_groups=mesh['zl'=4,'x'=4,'y'=8,'zh'=2,'c'=2] {'zl','y','zh','c'}, dimensions={0} | all-to-all | bytes 262144 | tf_op jit(solution)/shard_map/all_to_all | solution.py:29
  144.6 1.9 %shard_map.94.own = bf16[896,128]{1,0:T(8,128)(2,1)S(1)} custom-call(s32[1]{0:T(128)S(6)} %copy.10.rows, bf16[512,128]{1,0:T(8,128)(2,1)S(1)} %bitcast.20, bf16[512,512]{1,0:T(8,128)(2,1)S(1)} %copy-done.4, bf16[896,128]{1,0:T(8,128)(2,1)S(1)} %get-tuple-element.36.fwd, bf16[896,896]{1,0:T(8,128)(2,1)S(1)} %get-tuple-element.33.inv.second, ...), custom_call_target="tpu_custom_call" | custom-call | flops 457179136 | bytes 3407876 | tf_op jit(solution)/shard_map/pallas_call | solution.py:43
  146.5 2.4 %collective-permute-start.15 = (bf16[896,128]{1,0:T(8,128)(2,1)S(1)}, bf16[896,128]{1,0:T(8,128)(2,1)S(1)}, u32[]{:S(2)}, u32[]{:S(2)}) collective-permute-start(bf16[896,128]{1,0:T(8,128)(2,1)S(1)} %shard_map.94.own), channel_id=1, source_target_pairs={{0,64},{64,0},{32,96},{96,32},{1,65},{65,1},{33,97},{97,33},{2,66}... | collective-permute-start | bytes 688136 | tf_op jit(solution)/shard_map/ppermute | solution.py:25
  149.0 3.2 %collective-permute-start.14 = (bf16[896,128]{1,0:T(8,128)(2,1)S(1)}, bf16[896,128]{1,0:T(8,128)(2,1)S(1)}, u32[]{:S(2)}, u32[]{:S(2)}) collective-permute-start(bf16[896,128]{1,0:T(8,128)(2,1)S(1)} %shard_map.94.own), channel_id=1, source_target_pairs={{0,96},{96,0},{32,64},{64,32},{1,97},{97,1},{33,65},{65,33},{2,98}... | collective-permute-start | bytes 688136 | tf_op jit(solution)/shard_map/ppermute | solution.py:25
  152.1 2.9 %collective-permute-start.13 = (bf16[896,128]{1,0:T(8,128)(2,1)S(1)}, bf16[896,128]{1,0:T(8,128)(2,1)S(1)}, u32[]{:S(2)}, u32[]{:S(2)}) collective-permute-start(bf16[896,128]{1,0:T(8,128)(2,1)S(1)} %shard_map.94.own), channel_id=1, source_target_pairs={{0,32},{32,0},{64,96},{96,64},{1,33},{33,1},{65,97},{97,65},{2,34}... | collective-permute-start | bytes 688136 | tf_op jit(solution)/shard_map/ppermute | solution.py:25
  155.1 0.0 collective-permute-done.4.came
  155.1 0.0 copy-done.3
  155.1 0.0 copy-done.6
  155.1 0.0 copy-done.7
  155.1 2.8 %shard_map.95 = (bf16[384,896]{1,0:T(8,128)(2,1)S(1)}, bf16[384,384]{1,0:T(8,128)(2,1)S(1)}, f32[384,512]{1,0:T(8,128)S(1)}) custom-call(s32[1]{0:T(128)} %bitcast.at, bf16[448,1792]{1,0:T(8,128)(2,1)S(1)} %get-tuple-element.37.pack, bf16[448,1792]{1,0:T(8,128)(2,1)S(1)} %collective-permute-done.4.came, bf16[448,896]{1,0:T(8,128)(2,1)S(1)} %bitcast.13, ...), custom_call_target="tpu_custom_call" | custom-call | flops 1585446912 | bytes 5849092 | tf_op jit(solution)/shard_map/pallas_call | solution.py:43
  158.0 0.0 collective-permute-done.15.far
  158.0 4.4 %collective-permute-done.14.nxt = bf16[896,128]{1,0:T(8,128)(2,1)S(1)} collective-permute-done((bf16[896,128]{1,0:T(8,128)(2,1)S(1)}, bf16[896,128]{1,0:T(8,128)(2,1)S(1)}, u32[]{:S(2)}, u32[]{:S(2)}) %collective-permute-start.14) | collective-permute-done | bytes 229408 | tf_op jit(solution)/shard_map/ppermute | solution.py:25
  162.4 0.0 collective-permute-done.13.near
  162.4 1.8 %shard_map.96 = bf16[384,512]{1,0:T(8,128)(2,1)} custom-call(s32[1]{0:T(128)} %bitcast.at, bf16[384,896]{1,0:T(8,128)(2,1)S(1)} %get-tuple-element.39.fold_t, bf16[384,384]{1,0:T(8,128)(2,1)S(1)} %get-tuple-element.40.inv_t, f32[384,512]{1,0:T(8,128)S(1)} %get-tuple-element.41.rest, bf16[896,128]{1,0:T(8,128)(2,1)S(1)} %shard_map.94.own, ...), custom_call_target="tpu_custom_call" | custom-call | flops 503316480 | bytes 2686980 | tf_op jit(solution)/shard_map/pallas_call | solution.py:43
  (14 shorter events, 0.1 us)
Async XLA Ops:
  0.0 12.7 %copy-start.1 = (bf16[1,128,896]{2,1,0:T(8,128)(2,1)S(1)}, bf16[1,128,896]{2,1,0:T(8,128)(2,1)}, u32[]{:S(2)}) copy-start(bf16[1,128,896]{2,1,0:T(8,128)(2,1)} %param.15) | copy-start | bytes 688132
  0.0 30.3 %copy-start = (bf16[1,448,896]{2,1,0:T(8,128)(2,1)S(1)}, bf16[1,448,896]{2,1,0:T(8,128)(2,1)}, u32[]{:S(2)}) copy-start(bf16[1,448,896]{2,1,0:T(8,128)(2,1)} %param.13) | copy-start | bytes 2408452
  0.0 30.3 %copy-start.2 = (bf16[1,448,896]{2,1,0:T(8,128)(2,1)S(1)}, bf16[1,448,896]{2,1,0:T(8,128)(2,1)}, u32[]{:S(2)}) copy-start(bf16[1,448,896]{2,1,0:T(8,128)(2,1)} %param.12) | copy-start | bytes 2408452
  1.4 20.7 %collective-permute-start.2 = (bf16[448,512]{1,0:T(8,128)(2,1)S(1)}, bf16[448,512]{1,0:T(8,128)(2,1)S(1)}, u32[]{:S(2)}, u32[]{:S(2)}) collective-permute-start(bf16[448,512]{1,0:T(8,128)(2,1)S(1)} %slice_select_fusion), channel_id=1, source_target_pairs={{0,32},{32,0},{64,96},{96,64},{1,33},{33,1},{65,97},{97,65},{2,34}... | collective-permute-start | bytes 1376264 | tf_op jit(solution)/shard_map/ppermute | solution.py:25
  7.4 14.7 %collective-permute-start = (bf16[448,512]{1,0:T(8,128)(2,1)S(1)}, bf16[448,512]{1,0:T(8,128)(2,1)S(1)}, u32[]{:S(2)}, u32[]{:S(2)}) collective-permute-start(bf16[448,512]{1,0:T(8,128)(2,1)S(1)} %get-tuple-element.24.top), channel_id=1, source_target_pairs={{0,32},{32,0},{64,96},{96,64},{1,33},{33,1},{65,97},{97,65},{2,34}... | collective-permute-start | bytes 1376264 | tf_op jit(solution)/shard_map/ppermute | solution.py:25
  9.4 20.9 %collective-permute-start.1 = (bf16[448,512]{1,0:T(8,128)(2,1)S(1)}, bf16[448,512]{1,0:T(8,128)(2,1)S(1)}, u32[]{:S(2)}, u32[]{:S(2)}) collective-permute-start(bf16[448,512]{1,0:T(8,128)(2,1)S(1)} %get-tuple-element.25.bot), channel_id=1, source_target_pairs={{0,32},{64,96},{1,33},{65,97},{2,34},{66,98},{3,35},{67,99},{4,36}... | collective-permute-start | bytes 1376264 | tf_op jit(solution)/shard_map/ppermute | solution.py:25
  12.8 8.0 %collective-permute-start.10 = (bf16[128,896]{1,0:T(8,128)(2,1)S(1)}, bf16[128,896]{1,0:T(8,128)(2,1)S(1)}, u32[]{:S(2)}, u32[]{:S(2)}) collective-permute-start(bf16[128,896]{1,0:T(8,128)(2,1)S(1)} %bitcast.14), channel_id=1, source_target_pairs={{0,96},{96,0},{32,64},{64,32},{1,97},{97,1},{33,65},{65,33},{2,98}... | collective-permute-start | bytes 688136 | tf_op jit(solution)/shard_map/ppermute | solution.py:25
  20.8 27.4 %collective-permute-start.11 = (bf16[256,896]{1,0:T(8,128)(2,1)S(1)}, bf16[256,896]{1,0:T(8,128)(2,1)S(1)}, u32[]{:S(2)}, u32[]{:S(2)}) collective-permute-start(bf16[256,896]{1,0:T(8,128)(2,1)S(1)} %pad_maximum_fusion), channel_id=1, source_target_pairs={{32,0},{96,64},{33,1},{97,65},{34,2},{98,66},{35,3},{99,67},{36,4}... | collective-permute-start | bytes 1376264 | tf_op jit(solution)/shard_map/ppermute | solution.py:25
  30.3 5.6 %copy-start.5 = (bf16[1,224,896]{2,1,0:T(8,128)(2,1)S(1)}, bf16[1,224,896]{2,1,0:T(8,128)(2,1)}, u32[]{:S(2)}) copy-start(bf16[1,224,896]{2,1,0:T(8,128)(2,1)} %param.14) | copy-start | bytes 1204228
  31.7 14.6 %collective-permute-start.3 = (bf16[896,128]{1,0:T(8,128)(2,1)S(1)}, bf16[896,128]{1,0:T(8,128)(2,1)S(1)}, u32[]{:S(2)}, u32[]{:S(2)}) collective-permute-start(bf16[896,128]{1,0:T(8,128)(2,1)S(1)} %get-tuple-element.27), channel_id=1, source_target_pairs={{0,32},{32,0},{64,96},{96,64},{1,33},{33,1},{65,97},{97,65},{2,34}... | collective-permute-start | bytes 688136 | tf_op jit(solution)/shard_map/ppermute | solution.py:25
  35.9 14.9 %collective-permute-start.7 = (bf16[224,896]{1,0:T(8,128)(2,1)S(1)}, bf16[224,896]{1,0:T(8,128)(2,1)S(1)}, u32[]{:S(2)}, u32[]{:S(2)}) collective-permute-start(bf16[224,896]{1,0:T(8,128)(2,1)S(1)} %bitcast.21), channel_id=1, source_target_pairs={{0,32},{32,0},{64,96},{96,64},{1,33},{33,1},{65,97},{97,65},{2,34}... | collective-permute-start | bytes 1204232 | tf_op jit(solution)/shard_map/ppermute | solution.py:25
  37.8 21.2 %collective-permute-start.8 = (bf16[224,896]{1,0:T(8,128)(2,1)S(1)}, bf16[224,896]{1,0:T(8,128)(2,1)S(1)}, u32[]{:S(2)}, u32[]{:S(2)}) collective-permute-start(bf16[224,896]{1,0:T(8,128)(2,1)S(1)} %bitcast.22), channel_id=1, source_target_pairs={{0,96},{96,0},{32,64},{64,32},{1,97},{97,1},{33,65},{65,33},{2,98}... | collective-permute-start | bytes 1204232 | tf_op jit(solution)/shard_map/ppermute | solution.py:25
  46.3 108.8 %collective-permute-start.4 = (bf16[448,1792]{1,0:T(8,128)(2,1)S(1)}, bf16[448,1792]{1,0:T(8,128)(2,1)S(1)}, u32[]{:S(2)}, u32[]{:S(2)}) collective-permute-start(bf16[448,1792]{1,0:T(8,128)(2,1)S(1)} %get-tuple-element.37.pack), channel_id=1, source_target_pairs={{0,32},{32,0},{64,96},{96,64},{1,33},{33,1},{65,97},{97,65},{2,34}... | collective-permute-start | bytes 4816904 | tf_op jit(solution)/shard_map/ppermute | solution.py:25
  48.2 23.0 %collective-permute-start.12 = (bf16[256,896]{1,0:T(8,128)(2,1)S(1)}, bf16[256,896]{1,0:T(8,128)(2,1)S(1)}, u32[]{:S(2)}, u32[]{:S(2)}) collective-permute-start(bf16[256,896]{1,0:T(8,128)(2,1)S(1)} %collective-permute-done.11.up), channel_id=1, source_target_pairs={{0,96},{64,32},{1,97},{65,33},{2,98},{66,34},{3,99},{67,35},{4,100... | collective-permute-start | bytes 1376264 | tf_op jit(solution)/shard_map/ppermute | solution.py:25
  50.7 20.5 %collective-permute-start.9 = (bf16[224,896]{1,0:T(8,128)(2,1)S(1)}, bf16[224,896]{1,0:T(8,128)(2,1)S(1)}, u32[]{:S(2)}, u32[]{:S(2)}) collective-permute-start(bf16[224,896]{1,0:T(8,128)(2,1)S(1)} %collective-permute-done.7.i1), channel_id=1, source_target_pairs={{0,96},{96,0},{32,64},{64,32},{1,97},{97,1},{33,65},{65,33},{2,98}... | collective-permute-start | bytes 1204232 | tf_op jit(solution)/shard_map/ppermute | solution.py:25
  57.1 19.1 %collective-permute-start.5 = (bf16[896,128]{1,0:T(8,128)(2,1)S(1)}, bf16[896,128]{1,0:T(8,128)(2,1)S(1)}, u32[]{:S(2)}, u32[]{:S(2)}) collective-permute-start(bf16[896,128]{1,0:T(8,128)(2,1)S(1)} %get-tuple-element.31), channel_id=1, source_target_pairs={{0,96},{96,0},{32,64},{64,32},{1,97},{97,1},{33,65},{65,33},{2,98}... | collective-permute-start | bytes 688136 | tf_op jit(solution)/shard_map/ppermute | solution.py:25
  59.0 35.2 %collective-permute-start.6 = (bf16[896,128]{1,0:T(8,128)(2,1)S(1)}, bf16[896,128]{1,0:T(8,128)(2,1)S(1)}, u32[]{:S(2)}, u32[]{:S(2)}) collective-permute-start(bf16[896,128]{1,0:T(8,128)(2,1)S(1)} %get-tuple-element.32), channel_id=1, source_target_pairs={{0,64},{64,0},{32,96},{96,32},{1,65},{65,1},{33,97},{97,33},{2,66}... | collective-permute-start | bytes 688136 | tf_op jit(solution)/shard_map/ppermute | solution.py:25
  94.2 50.4 %copy-start.4 = (bf16[512,512]{1,0:T(8,128)(2,1)S(1)}, bf16[512,512]{1,0:T(8,128)(2,1)}, u32[]{:S(2)}) copy-start(bf16[512,512]{1,0:T(8,128)(2,1)} %inv.1) | copy-start | bytes 1572868
  144.6 10.5 %copy-start.3 = (bf16[1,1,896,384]{3,2,1,0:T(8,128)(2,1)S(1)}, bf16[1,1,896,384]{3,2,1,0:T(8,128)(2,1)}, u32[]{:S(2)}) copy-start(bf16[1,1,896,384]{3,2,1,0:T(8,128)(2,1)} %param.11) | copy-start | bytes 2064388
  144.6 10.5 %copy-start.6 = (bf16[1,1,384,512]{3,2,1,0:T(8,128)(2,1)S(1)}, bf16[1,1,384,512]{3,2,1,0:T(8,128)(2,1)}, u32[]{:S(2)}) copy-start(bf16[1,1,384,512]{3,2,1,0:T(8,128)(2,1)} %param.9) | copy-start | bytes 1179652
  144.6 10.5 %copy-start.7 = (bf16[1,1,384,384]{3,2,1,0:T(8,128)(2,1)S(1)}, bf16[1,1,384,384]{3,2,1,0:T(8,128)(2,1)}, u32[]{:S(2)}) copy-start(bf16[1,1,384,384]{3,2,1,0:T(8,128)(2,1)} %param.10) | copy-start | bytes 884740
  146.5 11.5 %collective-permute-start.15 = (bf16[896,128]{1,0:T(8,128)(2,1)S(1)}, bf16[896,128]{1,0:T(8,128)(2,1)S(1)}, u32[]{:S(2)}, u32[]{:S(2)}) collective-permute-start(bf16[896,128]{1,0:T(8,128)(2,1)S(1)} %shard_map.94.own), channel_id=1, source_target_pairs={{0,64},{64,0},{32,96},{96,32},{1,65},{65,1},{33,97},{97,33},{2,66}... | collective-permute-start | bytes 688136 | tf_op jit(solution)/shard_map/ppermute | solution.py:25
  149.0 13.4 %collective-permute-start.14 = (bf16[896,128]{1,0:T(8,128)(2,1)S(1)}, bf16[896,128]{1,0:T(8,128)(2,1)S(1)}, u32[]{:S(2)}, u32[]{:S(2)}) collective-permute-start(bf16[896,128]{1,0:T(8,128)(2,1)S(1)} %shard_map.94.own), channel_id=1, source_target_pairs={{0,96},{96,0},{32,64},{64,32},{1,97},{97,1},{33,65},{65,33},{2,98}... | collective-permute-start | bytes 688136 | tf_op jit(solution)/shard_map/ppermute | solution.py:25
  152.1 10.2 %collective-permute-start.13 = (bf16[896,128]{1,0:T(8,128)(2,1)S(1)}, bf16[896,128]{1,0:T(8,128)(2,1)S(1)}, u32[]{:S(2)}, u32[]{:S(2)}) collective-permute-start(bf16[896,128]{1,0:T(8,128)(2,1)S(1)} %shard_map.94.own), channel_id=1, source_target_pairs={{0,32},{32,0},{64,96},{96,64},{1,33},{33,1},{65,97},{97,65},{2,34}... | collective-permute-start | bytes 688136 | tf_op jit(solution)/shard_map/ppermute | solution.py:25

commit v6 on v5

--- a/solution.py
+++ b/solution.py
@@ -19,6 +19,7 @@
 F32 = jnp.float32
 
 LANES = 128
+CHUNK = 256
 
 
 def send(x, pairs):
@@ -52,6 +53,20 @@
         compiler_params=pltpu.CompilerParams(vmem_limit_bytes=16 << 20),
         cost_estimate=pl.CostEstimate(flops=flops, bytes_accessed=moved, transcendentals=0),
     )(*args)
+
+
+def lower_mul(lower, vector, out):
+    size = vector.shape[0]
+    for first in range(0, size, CHUNK):
+        last = min(first + CHUNK, size)
+        out[first:last] = mul(lower[first:last, :last], vector[:last]).astype(out.dtype)
+
+
+def lower_mul_t(lower, vector, out):
+    size = vector.shape[0]
+    for first in range(0, size, CHUNK):
+        last = min(first + CHUNK, size)
+        out[first:last] = mul_t(lower[first:, first:last], vector[first:]).astype(out.dtype)
 
 
 def others(x):
@@ -140,22 +155,24 @@
         coup[pl.ds(pl.multiple_of(who * count, count), count)] = block
 
 
-def second_kernel(rows, own, near, nxt, far, inv, coup, fwd, tiles):
+def second_kernel(rows, own, near, nxt, far, inv, coup, fwd, tiles, rhs):
     total = own[...].astype(F32) + near[...].astype(F32)
     total = total + (nxt[...].astype(F32) + far[...].astype(F32))
-    fwd[...] = mul(inv[...], (-total).astype(BF)).astype(BF)
-    part = mul(coup[...], fwd[...])
-    live = lax.broadcasted_iota(jnp.int32, part.shape, 0) < rows[0]
-    tiles[...] = jnp.where(live, part, 0.0).astype(BF)
-
-
-def border_kernel(rows, rhs, inv, fwd, second, coup, back):
-    mid = mul(inv[...], rhs[...]).astype(BF)
-    end = mul_t(inv[...], mid)
-    live = lax.broadcasted_iota(jnp.int32, end.shape, 0) < rows[0]
-    sol = jnp.where(live, end, 0.0).astype(BF)
-    diff = (fwd[...].astype(F32) - mul_t(coup[...], sol)).astype(BF)
-    back[...] = mul_t(second[...], diff).astype(BF)
+    rhs[...] = (-total).astype(BF)
+    lower_mul(inv, rhs, fwd)
+    for first in range(0, tiles.shape[0], CHUNK):
+        part = mul(coup[first : first + CHUNK], fwd[...])
+        live = lax.broadcasted_iota(jnp.int32, part.shape, 0) + first < rows[0]
+        tiles[first : first + CHUNK] = jnp.where(live, part, 0.0).astype(BF)
+
+
+def border_kernel(rows, rhs, inv, fwd, second, coup, back, mid, sol, diff):
+    lower_mul(inv, rhs, mid)
+    lower_mul_t(inv, mid, sol)
+    live = lax.broadcasted_iota(jnp.int32, sol.shape, 0) < rows[0]
+    masked = jnp.where(live, sol[...], 0.0).astype(BF)
+    diff[...] = (fwd[...].astype(F32) - mul_t(coup[...], masked)).astype(BF)
+    lower_mul_t(second, diff, back)
 
 
 def fold_kernel(at, pack, came, coup, came_coup, leaf_coup, loads, leaf_inv, fold_t, inv_t, rest, full, fold):
@@ -264,7 +281,7 @@
     fwd_two, tiles = call(
         second_kernel,
         [quarter, ((border, share), BF)],
-        [],
+        [quarter],
         border_rows,
         own,
         near,
@@ -281,7 +298,7 @@
     (back_two,) = call(
         border_kernel,
         [quarter],
-        [],
+        [((border, share), BF), ((border, share), F32), quarter],
         border_rows,
         rhs_border,
         border_inverse,

time: 165 us -> 164 us (level)
  no operation moved by 1% of the time
where the time goes in v6:
time: 164 us; the launch traced here: 163 us
  starting transfers between devices  52.4 us (32%)
  blocking collectives  48.9 us (30%)
  waiting for transfers between devices  48.8 us (30%)
  Pallas kernels  10.9 us (7%)
    ppermute x16, starting transfers between devices, send(): return lax.ppermute(x, 'x', pairs)  52.4 us
    all_to_all x2, blocking collectives, to_group(): return lax.all_to_all(tiles, GROUP, split_axis=0, concat_axis=0, tiled=True)  48.9 us
    ppermute x16, waiting for transfers between devices, send(): return lax.ppermute(x, 'x', pairs)  48.8 us
    pallas_call x6, Pallas kernels, call(): pl.pallas_call(kernel, out_shape=[jax.ShapeDtypeStruct(s, d) for s, d in...  8.76 us
  transfers between devices with their start and end apart: 16, of which 6 were waited for; matrix products, arithmetic and copies ran while one was open for 0% of the time, Pallas kernels for 6%

profile of v6, /device:TPU:1, one launch (start us, length us, event | category | flops | bytes accessed | tf_op | source)
XLA Modules:
  0.0 163.5 jit_solution(10996002150661705781)
XLA Ops:
  0.0 1.3 slice_select_fusion
  1.4 3.9 %collective-permute-start.2 = (bf16[448,512]{1,0:T(8,128)(2,1)S(1)}, bf16[448,512]{1,0:T(8,128)(2,1)S(1)}, u32[]{:S(2)}, u32[]{:S(2)}) collective-permute-start(bf16[448,512]{1,0:T(8,128)(2,1)S(1)} %slice_select_fusion), channel_id=1, source_target_pairs={{0,32},{32,0},{64,96},{96,64},{1,33},{33,1},{65,97},{97,65},{2,34}... | collective-permute-start | bytes 1376264 | tf_op jit(solution)/shard_map/ppermute | solution.py:26
  5.3 2.1 %k_leaf.1 = (bf16[448,512]{1,0:T(8,128)(2,1)S(1)}, bf16[448,512]{1,0:T(8,128)(2,1)S(1)}) custom-call(bf16[384,512]{1,0:T(8,128)(2,1)} %bitcast.24, bf16[384,384]{1,0:T(8,128)(2,1)} %bitcast.26, bf16[896,384]{1,0:T(8,128)(2,1)} %bitcast.18), custom_call_target="tpu_custom_call" | custom-call | tf_op jit(solution)/shard_map/k_leaf/pallas_call | solution.py:98
  7.4 1.9 %collective-permute-start = (bf16[448,512]{1,0:T(8,128)(2,1)S(1)}, bf16[448,512]{1,0:T(8,128)(2,1)S(1)}, u32[]{:S(2)}, u32[]{:S(2)}) collective-permute-start(bf16[448,512]{1,0:T(8,128)(2,1)S(1)} %get-tuple-element.24.top), channel_id=1, source_target_pairs={{0,32},{32,0},{64,96},{96,64},{1,33},{33,1},{65,97},{97,65},{2,34}... | collective-permute-start | bytes 1376264 | tf_op jit(solution)/shard_map/ppermute | solution.py:26
  9.4 3.4 %collective-permute-start.1 = (bf16[448,512]{1,0:T(8,128)(2,1)S(1)}, bf16[448,512]{1,0:T(8,128)(2,1)S(1)}, u32[]{:S(2)}, u32[]{:S(2)}) collective-permute-start(bf16[448,512]{1,0:T(8,128)(2,1)S(1)} %get-tuple-element.25.bot), channel_id=1, source_target_pairs={{0,32},{64,96},{1,33},{65,97},{2,34},{66,98},{3,35},{67,99},{4,36}... | collective-permute-start | bytes 1376264 | tf_op jit(solution)/shard_map/ppermute | solution.py:26
  12.7 0.0 copy-done.1
  12.8 2.5 %collective-permute-start.10 = (bf16[128,896]{1,0:T(8,128)(2,1)S(1)}, bf16[128,896]{1,0:T(8,128)(2,1)S(1)}, u32[]{:S(2)}, u32[]{:S(2)}) collective-permute-start(bf16[128,896]{1,0:T(8,128)(2,1)S(1)} %bitcast.14), channel_id=1, source_target_pairs={{0,96},{96,0},{32,64},{64,32},{1,97},{97,1},{33,65},{65,33},{2,98}... | collective-permute-start | bytes 688136 | tf_op jit(solution)/shard_map/ppermute | solution.py:26
  15.3 5.4 %collective-permute-done.10.nxt = bf16[128,896]{1,0:T(8,128)(2,1)S(1)} collective-permute-done((bf16[128,896]{1,0:T(8,128)(2,1)S(1)}, bf16[128,896]{1,0:T(8,128)(2,1)S(1)}, u32[]{:S(2)}, u32[]{:S(2)}) %collective-permute-start.10) | collective-permute-done | bytes 229408 | tf_op jit(solution)/shard_map/ppermute | solution.py:26
  20.8 1.3 collective-permute-start.11
  22.1 0.0 collective-permute-done.2.came_coup
  22.1 0.0 collective-permute-done.came_top
  22.1 8.2 %collective-permute-done.1.came_bot = bf16[448,512]{1,0:T(8,128)(2,1)S(1)} collective-permute-done((bf16[448,512]{1,0:T(8,128)(2,1)S(1)}, bf16[448,512]{1,0:T(8,128)(2,1)S(1)}, u32[]{:S(2)}, u32[]{:S(2)}) %collective-permute-start.1) | collective-permute-done | bytes 458784 | tf_op jit(solution)/shard_map/ppermute | solution.py:26
  30.3 0.0 copy-done
  30.3 1.4 shard_map.91
  31.7 4.1 %collective-permute-start.3 = (bf16[896,128]{1,0:T(8,128)(2,1)S(1)}, bf16[896,128]{1,0:T(8,128)(2,1)S(1)}, u32[]{:S(2)}, u32[]{:S(2)}) collective-permute-start(bf16[896,128]{1,0:T(8,128)(2,1)S(1)} %get-tuple-element.27), channel_id=1, source_target_pairs={{0,32},{32,0},{64,96},{96,64},{1,33},{33,1},{65,97},{97,65},{2,34}... | collective-permute-start | bytes 688136 | tf_op jit(solution)/shard_map/ppermute | solution.py:26
  35.9 1.9 %collective-permute-start.7 = (bf16[224,896]{1,0:T(8,128)(2,1)S(1)}, bf16[224,896]{1,0:T(8,128)(2,1)S(1)}, u32[]{:S(2)}, u32[]{:S(2)}) collective-permute-start(bf16[224,896]{1,0:T(8,128)(2,1)S(1)} %bitcast.21), channel_id=1, source_target_pairs={{0,32},{32,0},{64,96},{96,64},{1,33},{33,1},{65,97},{97,65},{2,34}... | collective-permute-start | bytes 1204232 | tf_op jit(solution)/shard_map/ppermute | solution.py:26
  37.8 8.5 %collective-permute-start.8 = (bf16[224,896]{1,0:T(8,128)(2,1)S(1)}, bf16[224,896]{1,0:T(8,128)(2,1)S(1)}, u32[]{:S(2)}, u32[]{:S(2)}) collective-permute-start(bf16[224,896]{1,0:T(8,128)(2,1)S(1)} %bitcast.22), channel_id=1, source_target_pairs={{0,96},{96,0},{32,64},{64,32},{1,97},{97,1},{33,65},{65,33},{2,98}... | collective-permute-start | bytes 1204232 | tf_op jit(solution)/shard_map/ppermute | solution.py:26
  46.3 0.0 collective-permute-done.3.near
  46.3 1.9 %collective-permute-start.4 = (bf16[448,1792]{1,0:T(8,128)(2,1)S(1)}, bf16[448,1792]{1,0:T(8,128)(2,1)S(1)}, u32[]{:S(2)}, u32[]{:S(2)}) collective-permute-start(bf16[448,1792]{1,0:T(8,128)(2,1)S(1)} %get-tuple-element.37.pack), channel_id=1, source_target_pairs={{0,32},{32,0},{64,96},{96,64},{1,33},{33,1},{65,97},{97,65},{2,34}... | collective-permute-start | bytes 4816904 | tf_op jit(solution)/shard_map/ppermute | solution.py:26
  48.2 0.0 collective-permute-done.11.up
  48.2 2.5 %collective-permute-start.12 = (bf16[256,896]{1,0:T(8,128)(2,1)S(1)}, bf16[256,896]{1,0:T(8,128)(2,1)S(1)}, u32[]{:S(2)}, u32[]{:S(2)}) collective-permute-start(bf16[256,896]{1,0:T(8,128)(2,1)S(1)} %collective-permute-done.11.up), channel_id=1, source_target_pairs={{0,96},{64,32},{1,97},{65,33},{2,98},{66,34},{3,99},{67,35},{4,100... | collective-permute-start | bytes 1376264 | tf_op jit(solution)/shard_map/ppermute | solution.py:26
  50.7 0.0 collective-permute-done.7.i1
  50.7 6.3 %collective-permute-start.9 = (bf16[224,896]{1,0:T(8,128)(2,1)S(1)}, bf16[224,896]{1,0:T(8,128)(2,1)S(1)}, u32[]{:S(2)}, u32[]{:S(2)}) collective-permute-start(bf16[224,896]{1,0:T(8,128)(2,1)S(1)} %collective-permute-done.7.i1), channel_id=1, source_target_pairs={{0,96},{96,0},{32,64},{64,32},{1,97},{97,1},{33,65},{65,33},{2,98}... | collective-permute-start | bytes 1204232 | tf_op jit(solution)/shard_map/ppermute | solution.py:26
  57.1 1.9 %collective-permute-start.5 = (bf16[896,128]{1,0:T(8,128)(2,1)S(1)}, bf16[896,128]{1,0:T(8,128)(2,1)S(1)}, u32[]{:S(2)}, u32[]{:S(2)}) collective-permute-start(bf16[896,128]{1,0:T(8,128)(2,1)S(1)} %get-tuple-element.31), channel_id=1, source_target_pairs={{0,96},{96,0},{32,64},{64,32},{1,97},{97,1},{33,65},{65,33},{2,98}... | collective-permute-start | bytes 688136 | tf_op jit(solution)/shard_map/ppermute | solution.py:26
  59.0 0.0 collective-permute-done.8.i2
  59.0 3.6 %collective-permute-start.6 = (bf16[896,128]{1,0:T(8,128)(2,1)S(1)}, bf16[896,128]{1,0:T(8,128)(2,1)S(1)}, u32[]{:S(2)}, u32[]{:S(2)}) collective-permute-start(bf16[896,128]{1,0:T(8,128)(2,1)S(1)} %get-tuple-element.32), channel_id=1, source_target_pairs={{0,64},{64,0},{32,96},{96,32},{1,65},{65,1},{33,97},{97,33},{2,66}... | collective-permute-start | bytes 688136 | tf_op jit(solution)/shard_map/ppermute | solution.py:26
  63.2 8.0 %collective-permute-done.9.i3 = bf16[224,896]{1,0:T(8,128)(2,1)S(1)} collective-permute-done((bf16[224,896]{1,0:T(8,128)(2,1)S(1)}, bf16[224,896]{1,0:T(8,128)(2,1)S(1)}, u32[]{:S(2)}, u32[]{:S(2)}) %collective-permute-start.9) | collective-permute-done | bytes 401440 | tf_op jit(solution)/shard_map/ppermute | solution.py:26
  71.2 0.0 collective-permute-done.12.down
  71.2 0.2 shard_map.92
  71.5 4.7 %collective-permute-done.5.nxt = bf16[896,128]{1,0:T(8,128)(2,1)S(1)} collective-permute-done((bf16[896,128]{1,0:T(8,128)(2,1)S(1)}, bf16[896,128]{1,0:T(8,128)(2,1)S(1)}, u32[]{:S(2)}, u32[]{:S(2)}) %collective-permute-start.5) | collective-permute-done | bytes 229408 | tf_op jit(solution)/shard_map/ppermute | solution.py:26
  76.2 18.1 %collective-permute-done.6.far = bf16[896,128]{1,0:T(8,128)(2,1)S(1)} collective-permute-done((bf16[896,128]{1,0:T(8,128)(2,1)S(1)}, bf16[896,128]{1,0:T(8,128)(2,1)S(1)}, u32[]{:S(2)}, u32[]{:S(2)}) %collective-permute-start.6) | collective-permute-done | bytes 229408 | tf_op jit(solution)/shard_map/ppermute | solution.py:26
  94.2 0.8 shard_map.93
  95.1 31.4 %all_to_all.10 = bf16[128,4,128]{2,1,0:T(4,128)(2,1)S(1)} all-to-all(bf16[128,4,128]{2,1,0:T(4,128)(2,1)S(1)} %bitcast.28), channel_id=1, replica_groups=mesh['zl'=4,'x'=4,'y'=8,'zh'=2,'c'=2] {'zl','y','zh','c'}, dimensions={0} | all-to-all | bytes 262144 | tf_op jit(solution)/shard_map/all_to_all | solution.py:30
  126.5 0.1 convert_reduce_fusion
  126.6 17.5 %all_to_all.11 = bf16[128,4,128]{2,1,0:T(4,128)(2,1)S(1)} all-to-all(bf16[128,4,128]{2,1,0:T(4,128)(2,1)S(1)} %broadcast_in_dim.10), channel_id=1, replica_groups=mesh['zl'=4,'x'=4,'y'=8,'zh'=2,'c'=2] {'zl','y','zh','c'}, dimensions={0} | all-to-all | bytes 262144 | tf_op jit(solution)/shard_map/all_to_all | solution.py:30
  144.2 1.6 shard_map.94.own
  145.8 2.4 %collective-permute-start.15 = (bf16[896,128]{1,0:T(8,128)(2,1)S(1)}, bf16[896,128]{1,0:T(8,128)(2,1)S(1)}, u32[]{:S(2)}, u32[]{:S(2)}) collective-permute-start(bf16[896,128]{1,0:T(8,128)(2,1)S(1)} %shard_map.94.own), channel_id=1, source_target_pairs={{0,64},{64,0},{32,96},{96,32},{1,65},{65,1},{33,97},{97,33},{2,66}... | collective-permute-start | bytes 688136 | tf_op jit(solution)/shard_map/ppermute | solution.py:26
  148.2 3.2 %collective-permute-start.14 = (bf16[896,128]{1,0:T(8,128)(2,1)S(1)}, bf16[896,128]{1,0:T(8,128)(2,1)S(1)}, u32[]{:S(2)}, u32[]{:S(2)}) collective-permute-start(bf16[896,128]{1,0:T(8,128)(2,1)S(1)} %shard_map.94.own), channel_id=1, source_target_pairs={{0,96},{96,0},{32,64},{64,32},{1,97},{97,1},{33,65},{65,33},{2,98}... | collective-permute-start | bytes 688136 | tf_op jit(solution)/shard_map/ppermute | solution.py:26
  151.4 2.9 %collective-permute-start.13 = (bf16[896,128]{1,0:T(8,128)(2,1)S(1)}, bf16[896,128]{1,0:T(8,128)(2,1)S(1)}, u32[]{:S(2)}, u32[]{:S(2)}) collective-permute-start(bf16[896,128]{1,0:T(8,128)(2,1)S(1)} %shard_map.94.own), channel_id=1, source_target_pairs={{0,32},{32,0},{64,96},{96,64},{1,33},{33,1},{65,97},{97,65},{2,34}... | collective-permute-start | bytes 688136 | tf_op jit(solution)/shard_map/ppermute | solution.py:26
  154.4 0.0 collective-permute-done.4.came
  154.4 0.0 copy-done.3
  154.4 0.0 copy-done.6
  154.4 0.0 copy-done.7
  154.4 2.8 %shard_map.95 = (bf16[384,896]{1,0:T(8,128)(2,1)S(1)}, bf16[384,384]{1,0:T(8,128)(2,1)S(1)}, f32[384,512]{1,0:T(8,128)S(1)}) custom-call(s32[1]{0:T(128)} %bitcast.at, bf16[448,1792]{1,0:T(8,128)(2,1)S(1)} %get-tuple-element.37.pack, bf16[448,1792]{1,0:T(8,128)(2,1)S(1)} %collective-permute-done.4.came, bf16[448,896]{1,0:T(8,128)(2,1)S(1)} %bitcast.13, ...), custom_call_target="tpu_custom_call" | custom-call | flops 1585446912 | bytes 5849092 | tf_op jit(solution)/shard_map/pallas_call | solution.py:44
  157.2 0.0 collective-permute-done.15.far
  157.3 4.4 %collective-permute-done.14.nxt = bf16[896,128]{1,0:T(8,128)(2,1)S(1)} collective-permute-done((bf16[896,128]{1,0:T(8,128)(2,1)S(1)}, bf16[896,128]{1,0:T(8,128)(2,1)S(1)}, u32[]{:S(2)}, u32[]{:S(2)}) %collective-permute-start.14) | collective-permute-done | bytes 229408 | tf_op jit(solution)/shard_map/ppermute | solution.py:26
  161.6 0.0 collective-permute-done.13.near
  161.6 1.8 %shard_map.96 = bf16[384,512]{1,0:T(8,128)(2,1)} custom-call(s32[1]{0:T(128)} %bitcast.at, bf16[384,896]{1,0:T(8,128)(2,1)S(1)} %get-tuple-element.39.fold_t, bf16[384,384]{1,0:T(8,128)(2,1)S(1)} %get-tuple-element.40.inv_t, f32[384,512]{1,0:T(8,128)S(1)} %get-tuple-element.41.rest, bf16[896,128]{1,0:T(8,128)(2,1)S(1)} %shard_map.94.own, ...), custom_call_target="tpu_custom_call" | custom-call | flops 503316480 | bytes 2686980 | tf_op jit(solution)/shard_map/pallas_call | solution.py:44
  (14 shorter events, 0.1 us)
Async XLA Ops:
  0.0 12.7 %copy-start.1 = (bf16[1,128,896]{2,1,0:T(8,128)(2,1)S(1)}, bf16[1,128,896]{2,1,0:T(8,128)(2,1)}, u32[]{:S(2)}) copy-start(bf16[1,128,896]{2,1,0:T(8,128)(2,1)} %param.15) | copy-start | bytes 688132
  0.0 30.3 %copy-start = (bf16[1,448,896]{2,1,0:T(8,128)(2,1)S(1)}, bf16[1,448,896]{2,1,0:T(8,128)(2,1)}, u32[]{:S(2)}) copy-start(bf16[1,448,896]{2,1,0:T(8,128)(2,1)} %param.13) | copy-start | bytes 2408452
  0.0 30.3 %copy-start.2 = (bf16[1,448,896]{2,1,0:T(8,128)(2,1)S(1)}, bf16[1,448,896]{2,1,0:T(8,128)(2,1)}, u32[]{:S(2)}) copy-start(bf16[1,448,896]{2,1,0:T(8,128)(2,1)} %param.12) | copy-start | bytes 2408452
  1.4 20.7 %collective-permute-start.2 = (bf16[448,512]{1,0:T(8,128)(2,1)S(1)}, bf16[448,512]{1,0:T(8,128)(2,1)S(1)}, u32[]{:S(2)}, u32[]{:S(2)}) collective-permute-start(bf16[448,512]{1,0:T(8,128)(2,1)S(1)} %slice_select_fusion), channel_id=1, source_target_pairs={{0,32},{32,0},{64,96},{96,64},{1,33},{33,1},{65,97},{97,65},{2,34}... | collective-permute-start | bytes 1376264 | tf_op jit(solution)/shard_map/ppermute | solution.py:26
  7.4 14.7 %collective-permute-start = (bf16[448,512]{1,0:T(8,128)(2,1)S(1)}, bf16[448,512]{1,0:T(8,128)(2,1)S(1)}, u32[]{:S(2)}, u32[]{:S(2)}) collective-permute-start(bf16[448,512]{1,0:T(8,128)(2,1)S(1)} %get-tuple-element.24.top), channel_id=1, source_target_pairs={{0,32},{32,0},{64,96},{96,64},{1,33},{33,1},{65,97},{97,65},{2,34}... | collective-permute-start | bytes 1376264 | tf_op jit(solution)/shard_map/ppermute | solution.py:26
  9.4 20.9 %collective-permute-start.1 = (bf16[448,512]{1,0:T(8,128)(2,1)S(1)}, bf16[448,512]{1,0:T(8,128)(2,1)S(1)}, u32[]{:S(2)}, u32[]{:S(2)}) collective-permute-start(bf16[448,512]{1,0:T(8,128)(2,1)S(1)} %get-tuple-element.25.bot), channel_id=1, source_target_pairs={{0,32},{64,96},{1,33},{65,97},{2,34},{66,98},{3,35},{67,99},{4,36}... | collective-permute-start | bytes 1376264 | tf_op jit(solution)/shard_map/ppermute | solution.py:26
  12.8 8.0 %collective-permute-start.10 = (bf16[128,896]{1,0:T(8,128)(2,1)S(1)}, bf16[128,896]{1,0:T(8,128)(2,1)S(1)}, u32[]{:S(2)}, u32[]{:S(2)}) collective-permute-start(bf16[128,896]{1,0:T(8,128)(2,1)S(1)} %bitcast.14), channel_id=1, source_target_pairs={{0,96},{96,0},{32,64},{64,32},{1,97},{97,1},{33,65},{65,33},{2,98}... | collective-permute-start | bytes 688136 | tf_op jit(solution)/shard_map/ppermute | solution.py:26
  20.8 27.4 %collective-permute-start.11 = (bf16[256,896]{1,0:T(8,128)(2,1)S(1)}, bf16[256,896]{1,0:T(8,128)(2,1)S(1)}, u32[]{:S(2)}, u32[]{:S(2)}) collective-permute-start(bf16[256,896]{1,0:T(8,128)(2,1)S(1)} %pad_maximum_fusion), channel_id=1, source_target_pairs={{32,0},{96,64},{33,1},{97,65},{34,2},{98,66},{35,3},{99,67},{36,4}... | collective-permute-start | bytes 1376264 | tf_op jit(solution)/shard_map/ppermute | solution.py:26
  30.3 5.6 %copy-start.5 = (bf16[1,224,896]{2,1,0:T(8,128)(2,1)S(1)}, bf16[1,224,896]{2,1,0:T(8,128)(2,1)}, u32[]{:S(2)}) copy-start(bf16[1,224,896]{2,1,0:T(8,128)(2,1)} %param.14) | copy-start | bytes 1204228
  31.7 14.6 %collective-permute-start.3 = (bf16[896,128]{1,0:T(8,128)(2,1)S(1)}, bf16[896,128]{1,0:T(8,128)(2,1)S(1)}, u32[]{:S(2)}, u32[]{:S(2)}) collective-permute-start(bf16[896,128]{1,0:T(8,128)(2,1)S(1)} %get-tuple-element.27), channel_id=1, source_target_pairs={{0,32},{32,0},{64,96},{96,64},{1,33},{33,1},{65,97},{97,65},{2,34}... | collective-permute-start | bytes 688136 | tf_op jit(solution)/shard_map/ppermute | solution.py:26
  35.9 14.9 %collective-permute-start.7 = (bf16[224,896]{1,0:T(8,128)(2,1)S(1)}, bf16[224,896]{1,0:T(8,128)(2,1)S(1)}, u32[]{:S(2)}, u32[]{:S(2)}) collective-permute-start(bf16[224,896]{1,0:T(8,128)(2,1)S(1)} %bitcast.21), channel_id=1, source_target_pairs={{0,32},{32,0},{64,96},{96,64},{1,33},{33,1},{65,97},{97,65},{2,34}... | collective-permute-start | bytes 1204232 | tf_op jit(solution)/shard_map/ppermute | solution.py:26
  37.8 21.2 %collective-permute-start.8 = (bf16[224,896]{1,0:T(8,128)(2,1)S(1)}, bf16[224,896]{1,0:T(8,128)(2,1)S(1)}, u32[]{:S(2)}, u32[]{:S(2)}) collective-permute-start(bf16[224,896]{1,0:T(8,128)(2,1)S(1)} %bitcast.22), channel_id=1, source_target_pairs={{0,96},{96,0},{32,64},{64,32},{1,97},{97,1},{33,65},{65,33},{2,98}... | collective-permute-start | bytes 1204232 | tf_op jit(solution)/shard_map/ppermute | solution.py:26
  46.3 108.1 %collective-permute-start.4 = (bf16[448,1792]{1,0:T(8,128)(2,1)S(1)}, bf16[448,1792]{1,0:T(8,128)(2,1)S(1)}, u32[]{:S(2)}, u32[]{:S(2)}) collective-permute-start(bf16[448,1792]{1,0:T(8,128)(2,1)S(1)} %get-tuple-element.37.pack), channel_id=1, source_target_pairs={{0,32},{32,0},{64,96},{96,64},{1,33},{33,1},{65,97},{97,65},{2,34}... | collective-permute-start | bytes 4816904 | tf_op jit(solution)/shard_map/ppermute | solution.py:26
  48.2 23.0 %collective-permute-start.12 = (bf16[256,896]{1,0:T(8,128)(2,1)S(1)}, bf16[256,896]{1,0:T(8,128)(2,1)S(1)}, u32[]{:S(2)}, u32[]{:S(2)}) collective-permute-start(bf16[256,896]{1,0:T(8,128)(2,1)S(1)} %collective-permute-done.11.up), channel_id=1, source_target_pairs={{0,96},{64,32},{1,97},{65,33},{2,98},{66,34},{3,99},{67,35},{4,100... | collective-permute-start | bytes 1376264 | tf_op jit(solution)/shard_map/ppermute | solution.py:26
  50.7 20.5 %collective-permute-start.9 = (bf16[224,896]{1,0:T(8,128)(2,1)S(1)}, bf16[224,896]{1,0:T(8,128)(2,1)S(1)}, u32[]{:S(2)}, u32[]{:S(2)}) collective-permute-start(bf16[224,896]{1,0:T(8,128)(2,1)S(1)} %collective-permute-done.7.i1), channel_id=1, source_target_pairs={{0,96},{96,0},{32,64},{64,32},{1,97},{97,1},{33,65},{65,33},{2,98}... | collective-permute-start | bytes 1204232 | tf_op jit(solution)/shard_map/ppermute | solution.py:26
  57.1 19.1 %collective-permute-start.5 = (bf16[896,128]{1,0:T(8,128)(2,1)S(1)}, bf16[896,128]{1,0:T(8,128)(2,1)S(1)}, u32[]{:S(2)}, u32[]{:S(2)}) collective-permute-start(bf16[896,128]{1,0:T(8,128)(2,1)S(1)} %get-tuple-element.31), channel_id=1, source_target_pairs={{0,96},{96,0},{32,64},{64,32},{1,97},{97,1},{33,65},{65,33},{2,98}... | collective-permute-start | bytes 688136 | tf_op jit(solution)/shard_map/ppermute | solution.py:26
  59.0 35.2 %collective-permute-start.6 = (bf16[896,128]{1,0:T(8,128)(2,1)S(1)}, bf16[896,128]{1,0:T(8,128)(2,1)S(1)}, u32[]{:S(2)}, u32[]{:S(2)}) collective-permute-start(bf16[896,128]{1,0:T(8,128)(2,1)S(1)} %get-tuple-element.32), channel_id=1, source_target_pairs={{0,64},{64,0},{32,96},{96,32},{1,65},{65,1},{33,97},{97,33},{2,66}... | collective-permute-start | bytes 688136 | tf_op jit(solution)/shard_map/ppermute | solution.py:26
  94.2 49.9 %copy-start.4 = (bf16[512,512]{1,0:T(8,128)(2,1)S(1)}, bf16[512,512]{1,0:T(8,128)(2,1)}, u32[]{:S(2)}) copy-start(bf16[512,512]{1,0:T(8,128)(2,1)} %inv.1) | copy-start | bytes 1572868
  144.2 10.2 %copy-start.3 = (bf16[1,1,896,384]{3,2,1,0:T(8,128)(2,1)S(1)}, bf16[1,1,896,384]{3,2,1,0:T(8,128)(2,1)}, u32[]{:S(2)}) copy-start(bf16[1,1,896,384]{3,2,1,0:T(8,128)(2,1)} %param.11) | copy-start | bytes 2064388
  144.2 10.2 %copy-start.6 = (bf16[1,1,384,512]{3,2,1,0:T(8,128)(2,1)S(1)}, bf16[1,1,384,512]{3,2,1,0:T(8,128)(2,1)}, u32[]{:S(2)}) copy-start(bf16[1,1,384,512]{3,2,1,0:T(8,128)(2,1)} %param.9) | copy-start | bytes 1179652
  144.2 10.2 %copy-start.7 = (bf16[1,1,384,384]{3,2,1,0:T(8,128)(2,1)S(1)}, bf16[1,1,384,384]{3,2,1,0:T(8,128)(2,1)}, u32[]{:S(2)}) copy-start(bf16[1,1,384,384]{3,2,1,0:T(8,128)(2,1)} %param.10) | copy-start | bytes 884740
  145.8 11.5 %collective-permute-start.15 = (bf16[896,128]{1,0:T(8,128)(2,1)S(1)}, bf16[896,128]{1,0:T(8,128)(2,1)S(1)}, u32[]{:S(2)}, u32[]{:S(2)}) collective-permute-start(bf16[896,128]{1,0:T(8,128)(2,1)S(1)} %shard_map.94.own), channel_id=1, source_target_pairs={{0,64},{64,0},{32,96},{96,32},{1,65},{65,1},{33,97},{97,33},{2,66}... | collective-permute-start | bytes 688136 | tf_op jit(solution)/shard_map/ppermute | solution.py:26
  148.2 13.4 %collective-permute-start.14 = (bf16[896,128]{1,0:T(8,128)(2,1)S(1)}, bf16[896,128]{1,0:T(8,128)(2,1)S(1)}, u32[]{:S(2)}, u32[]{:S(2)}) collective-permute-start(bf16[896,128]{1,0:T(8,128)(2,1)S(1)} %shard_map.94.own), channel_id=1, source_target_pairs={{0,96},{96,0},{32,64},{64,32},{1,97},{97,1},{33,65},{65,33},{2,98}... | collective-permute-start | bytes 688136 | tf_op jit(solution)/shard_map/ppermute | solution.py:26
  151.4 10.2 %collective-permute-start.13 = (bf16[896,128]{1,0:T(8,128)(2,1)S(1)}, bf16[896,128]{1,0:T(8,128)(2,1)S(1)}, u32[]{:S(2)}, u32[]{:S(2)}) collective-permute-start(bf16[896,128]{1,0:T(8,128)(2,1)S(1)} %shard_map.94.own), channel_id=1, source_target_pairs={{0,32},{32,0},{64,96},{96,64},{1,33},{33,1},{65,97},{97,65},{2,34}... | collective-permute-start | bytes 688136 | tf_op jit(solution)/shard_map/ppermute | solution.py:26

commit v7 on v6

--- a/solution.py
+++ b/solution.py
@@ -73,7 +73,7 @@
     return x ^ 1, 3 - x, x ^ 2
 
 
-def leaf_kernel(loads_hbm, inv_hbm, coup_hbm, top, bot, loads, inv, coup, sems):
+def leaf_kernel(rows, loads_hbm, inv_hbm, coup_hbm, top, bot, loads, inv, coup, sems):
     copies = [
         pltpu.make_async_copy(src, dst, sems.at[n])
         for n, (src, dst) in enumerate(
@@ -91,7 +91,7 @@
     top[...] = mul(coup[:half], fwd).astype(BF)
 
 
-def leaf_call(loads, inv, coup, half):
+def leaf_call(rows, loads, inv, coup, half):
     args = [pltpu.with_memory_space_constraint(a, pltpu.HBM) for a in (loads, inv, coup)]
     ports = loads.shape[1]
     shape = jax.ShapeDtypeStruct((half, ports), BF)
@@ -99,15 +99,16 @@
         leaf_kernel,
         name="k_leaf",
         out_shape=[shape, shape],
-        in_specs=[pl.BlockSpec(memory_space=pltpu.HBM)] * 3,
+        in_specs=[pl.BlockSpec(memory_space=pltpu.SMEM)]
+        + [pl.BlockSpec(memory_space=pltpu.HBM)] * 3,
         out_specs=[pl.BlockSpec(memory_space=pltpu.VMEM)] * 2,
         scratch_shapes=[pltpu.VMEM(a.shape, a.dtype) for a in (loads, inv, coup)]
         + [pltpu.SemaphoreType.DMA((3,))],
         compiler_params=pltpu.CompilerParams(vmem_limit_bytes=8 << 20),
-    )(*args)
-
-
-def first_kernel(at, inv, top, bot, came_top, came_bot, coup, came_coup, pack, own, near, nxt, far, rhs, held, turned):
+    )(rows, *args)
+
+
+def first_kernel(at, inv, top, bot, came_top, came_bot, coup, came_coup, first, own, near, nxt, far, rhs, held, turned):
     x = at[0]
     high = x % 2
     half, sep = inv.shape
@@ -116,16 +117,13 @@
     rhs[:half] = (-(top[...].astype(F32) + came_top[...].astype(F32))).astype(BF)
     rhs[half:] = (-(bot[...].astype(F32) + came_bot[...].astype(F32))).astype(BF)
     fwd = mul(inv[...], rhs[...]).astype(BF)
-    pack[:, :sep] = inv[...]
-    pack[:, sep + sep - width :] = fwd
+    first[...] = fwd
     pad = width - half
     held[:pad] = jnp.zeros((pad, ports), BF)
     held[half:] = jnp.zeros((pad, ports), BF)
     start = pl.multiple_of(high * pad, pad)
     held[pl.ds(start, half)] = fwd
     lane = pl.multiple_of(high * (sep - width), LANES)
-    rest = pl.multiple_of(high * width, LANES)
-    pack[:, sep : sep + sep - width] = coup[:, pl.ds(rest, sep - width)]
     mine = coup[:, pl.ds(lane, width)]
     mine_at = pl.multiple_of(high * half, half)
     other_at = pl.multiple_of((1 - high) * half, half)
@@ -137,6 +135,15 @@
         part = mul(weights, turned[...]).astype(BF)
         for at_col, ref in enumerate((own, near, nxt, far)):
             ref[pl.ds(row, half)] = part[:, at_col * share : (at_col + 1) * share]
+
+
+def pack_kernel(at, inv, coup, fwd, pack):
+    sep = inv.shape[1]
+    rest = pack.shape[1] - sep - fwd.shape[1]
+    start = pl.multiple_of((at[0] % 2) * (sep - rest), LANES)
+    pack[:, :sep] = inv[...]
+    pack[:, sep : sep + rest] = coup[:, pl.ds(start, rest)]
+    pack[:, sep + rest :] = fwd[...]
 
 
 def pieces(x, refs):
@@ -201,12 +208,26 @@
     inv_t[...] = leaf_inv[...].T
 
 
-def last_kernel(at, fold_t, inv_t, rest, own, near, nxt, far, out, back):
+def most_kernel(at, fold_t, inv_t, rest, own, nxt, far, out, back, kept):
+    x = at[0]
     share = own.shape[1]
-    for who, ref in pieces(at[0], (own, near, nxt, far)):
-        back[:, pl.ds(pl.multiple_of(who * share, LANES), share)] = ref[...]
-    diff = (rest[...] + mul(fold_t[...], back[...])).astype(BF)
+    for place, (who, ref) in enumerate(zip((x, 3 - x, x ^ 2), (own, nxt, far))):
+        spot = slice(place * share, (place + 1) * share)
+        back[:, spot] = ref[...]
+        kept[:, spot] = rest[:, pl.ds(pl.multiple_of(who * share, LANES), share)]
+    diff = (kept[...] + mul(fold_t[...], back[...])).astype(BF)
     out[...] = mul(inv_t[...], diff).astype(BF)
+
+
+def last_kernel(at, fold_t, inv_t, rest, near, most, out):
+    x = at[0]
+    share = near.shape[1]
+    for place, who in enumerate((x, 3 - x, x ^ 2)):
+        spot = slice(place * share, (place + 1) * share)
+        out[:, pl.ds(pl.multiple_of(who * share, LANES), share)] = most[:, spot]
+    cols = pl.ds(pl.multiple_of((x ^ 1) * share, LANES), share)
+    diff = (rest[:, cols] + mul(fold_t[...], near[...])).astype(BF)
+    out[:, cols] = mul(inv_t[...], diff).astype(BF)
 
 
 def per_device(
@@ -235,7 +256,7 @@
     inv_two, coup_border = second_inverse[0], border_coupling[0]
     i_near = send(inv_two, NEAR)
     b_next = send(coup_border, NEXT)
-    top, bot = leaf_call(loads, leaf_inv, leaf_coup, half)
+    top, bot = leaf_call(border_rows, loads, leaf_inv, leaf_coup, half)
     came_bot = send(bot, DOWN)
     b_up = send(jnp.concatenate([coup_border, b_next], 0), UP)
     window = jnp.where(low, coup_two[:, sep - width :], coup_two[:, :width])
@@ -245,9 +266,9 @@
     i_far = send(i_near, NEXT)
     b_down = send(b_up, BACK)
     quarter = ((sep, share), BF)
-    pack, own, near, nxt, far = call(
+    fwd_one, own, near, nxt, far = call(
         first_kernel,
-        [((half, 2 * sep - width + ports), BF)] + [quarter] * 4,
+        [((half, ports), BF)] + [quarter] * 4,
         [((sep, ports), BF), ((width, ports), BF), ((width, ports), BF)],
         at,
         inv_one,
@@ -262,6 +283,15 @@
     near = send(near, NEAR)
     far = send(far, ACROSS)
     nxt = send(nxt, NEXT)
+    (pack,) = call(
+        pack_kernel,
+        [((half, 2 * sep - width + ports), BF)],
+        [],
+        at,
+        inv_one,
+        coup_two,
+        fwd_one,
+    )
     late_pack, near = lax.optimization_barrier((pack, near))
     came_pack = send(late_pack, NEAR)
     inv_full, coup_full = call(
@@ -325,19 +355,30 @@
         leaf_inv,
         flops=2 * sep * leaf * (2 * sep + ports),
     )
-    (out,) = call(
-        last_kernel,
-        [((leaf, ports), BF)],
-        [((sep, ports), BF)],
+    (most,) = call(
+        most_kernel,
+        [((leaf, ports - share), BF)],
+        [((sep, ports - share), BF), ((leaf, ports - share), F32)],
         at,
         fold_t,
         inv_t,
         rest,
         back_two,
-        back_near,
         back_next,
         back_far,
-        flops=2 * leaf * ports * (sep + leaf),
+        flops=2 * leaf * (ports - share) * (sep + leaf),
+    )
+    (out,) = call(
+        last_kernel,
+        [((leaf, ports), BF)],
+        [],
+        at,
+        fold_t,
+        inv_t,
+        rest,
+        back_near,
+        most,
+        flops=2 * leaf * share * (sep + leaf),
     )
     return out[None, None]
 

time: 164 us -> 165 us (level)
    pallas_call x6 -> x8, Pallas kernels: 8.76 us -> 9.37 us  [call(): pl.pallas_call(kernel, out_shape=[jax.ShapeDtypeStruct(s, d) for s, d in...]
where the time goes in v7:
time: 165 us; the launch traced here: 164 us
  starting transfers between devices  52.2 us (32%)
  blocking collectives  48.9 us (30%)
  waiting for transfers between devices  48.8 us (30%)
  Pallas kernels  11.5 us (7%)
    ppermute x16, starting transfers between devices, send(): return lax.ppermute(x, 'x', pairs)  52.2 us
    all_to_all x2, blocking collectives, to_group(): return lax.all_to_all(tiles, GROUP, split_axis=0, concat_axis=0, tiled=True)  48.9 us
    ppermute x16, waiting for transfers between devices, send(): return lax.ppermute(x, 'x', pairs)  48.8 us
    pallas_call x8, Pallas kernels, call(): pl.pallas_call(kernel, out_shape=[jax.ShapeDtypeStruct(s, d) for s, d in...  9.37 us
  transfers between devices with their start and end apart: 16, of which 6 were waited for; matrix products, arithmetic and copies ran while one was open for 0% of the time, Pallas kernels for 6%

profile of v7, /device:TPU:1, one launch (start us, length us, event | category | flops | bytes accessed | tf_op | source)
XLA Modules:
  0.0 164.0 jit_solution(11287821622577116453)
XLA Ops:
  0.0 1.3 slice_select_fusion
  1.4 3.9 %collective-permute-start.2 = (bf16[448,512]{1,0:T(8,128)(2,1)S(1)}, bf16[448,512]{1,0:T(8,128)(2,1)S(1)}, u32[]{:S(2)}, u32[]{:S(2)}) collective-permute-start(bf16[448,512]{1,0:T(8,128)(2,1)S(1)} %slice_select_fusion), channel_id=1, source_target_pairs={{0,32},{32,0},{64,96},{96,64},{1,33},{33,1},{65,97},{97,65},{2,34}... | collective-permute-start | bytes 1376264 | tf_op jit(solution)/shard_map/ppermute | solution.py:26
  5.9 2.1 %k_leaf.1 = (bf16[448,512]{1,0:T(8,128)(2,1)S(1)}, bf16[448,512]{1,0:T(8,128)(2,1)S(1)}) custom-call(s32[1]{0:T(128)S(6)} %copy.10.rows, bf16[384,512]{1,0:T(8,128)(2,1)} %bitcast.26, bf16[384,384]{1,0:T(8,128)(2,1)} %bitcast.28, bf16[896,384]{1,0:T(8,128)(2,1)} %bitcast.20), custom_call_target="tpu_custom_call" | custom-call | tf_op jit(solution)/shard_map/k_leaf/pallas_call | solution.py:98
  8.1 1.9 %collective-permute-start = (bf16[448,512]{1,0:T(8,128)(2,1)S(1)}, bf16[448,512]{1,0:T(8,128)(2,1)S(1)}, u32[]{:S(2)}, u32[]{:S(2)}) collective-permute-start(bf16[448,512]{1,0:T(8,128)(2,1)S(1)} %get-tuple-element.24.top), channel_id=1, source_target_pairs={{0,32},{32,0},{64,96},{96,64},{1,33},{33,1},{65,97},{97,65},{2,34}... | collective-permute-start | bytes 1376264 | tf_op jit(solution)/shard_map/ppermute | solution.py:26
  10.0 3.4 %collective-permute-start.1 = (bf16[448,512]{1,0:T(8,128)(2,1)S(1)}, bf16[448,512]{1,0:T(8,128)(2,1)S(1)}, u32[]{:S(2)}, u32[]{:S(2)}) collective-permute-start(bf16[448,512]{1,0:T(8,128)(2,1)S(1)} %get-tuple-element.25.bot), channel_id=1, source_target_pairs={{0,32},{64,96},{1,33},{65,97},{2,34},{66,98},{3,35},{67,99},{4,36}... | collective-permute-start | bytes 1376264 | tf_op jit(solution)/shard_map/ppermute | solution.py:26
  13.4 0.0 copy-done.2
  13.4 2.5 %collective-permute-start.10 = (bf16[128,896]{1,0:T(8,128)(2,1)S(1)}, bf16[128,896]{1,0:T(8,128)(2,1)S(1)}, u32[]{:S(2)}, u32[]{:S(2)}) collective-permute-start(bf16[128,896]{1,0:T(8,128)(2,1)S(1)} %bitcast.17), channel_id=1, source_target_pairs={{0,96},{96,0},{32,64},{64,32},{1,97},{97,1},{33,65},{65,33},{2,98}... | collective-permute-start | bytes 688136 | tf_op jit(solution)/shard_map/ppermute | solution.py:26
  15.9 5.4 %collective-permute-done.10.nxt = bf16[128,896]{1,0:T(8,128)(2,1)S(1)} collective-permute-done((bf16[128,896]{1,0:T(8,128)(2,1)S(1)}, bf16[128,896]{1,0:T(8,128)(2,1)S(1)}, u32[]{:S(2)}, u32[]{:S(2)}) %collective-permute-start.10) | collective-permute-done | bytes 229408 | tf_op jit(solution)/shard_map/ppermute | solution.py:26
  21.4 1.3 collective-permute-start.11
  22.7 0.0 collective-permute-done.2.came_coup
  22.7 0.0 collective-permute-done.came_top
  22.7 7.5 %collective-permute-done.1.came_bot = bf16[448,512]{1,0:T(8,128)(2,1)S(1)} collective-permute-done((bf16[448,512]{1,0:T(8,128)(2,1)S(1)}, bf16[448,512]{1,0:T(8,128)(2,1)S(1)}, u32[]{:S(2)}, u32[]{:S(2)}) %collective-permute-start.1) | collective-permute-done | bytes 458784 | tf_op jit(solution)/shard_map/ppermute | solution.py:26
  30.3 0.0 copy-done
  30.3 0.0 copy-done.1
  30.3 1.4 shard_map.91
  31.7 4.1 %collective-permute-start.3 = (bf16[896,128]{1,0:T(8,128)(2,1)S(1)}, bf16[896,128]{1,0:T(8,128)(2,1)S(1)}, u32[]{:S(2)}, u32[]{:S(2)}) collective-permute-start(bf16[896,128]{1,0:T(8,128)(2,1)S(1)} %get-tuple-element.27), channel_id=1, source_target_pairs={{0,32},{32,0},{64,96},{96,64},{1,33},{33,1},{65,97},{97,65},{2,34}... | collective-permute-start | bytes 688136 | tf_op jit(solution)/shard_map/ppermute | solution.py:26
  35.8 1.9 %collective-permute-start.7 = (bf16[224,896]{1,0:T(8,128)(2,1)S(1)}, bf16[224,896]{1,0:T(8,128)(2,1)S(1)}, u32[]{:S(2)}, u32[]{:S(2)}) collective-permute-start(bf16[224,896]{1,0:T(8,128)(2,1)S(1)} %bitcast.23), channel_id=1, source_target_pairs={{0,32},{32,0},{64,96},{96,64},{1,33},{33,1},{65,97},{97,65},{2,34}... | collective-permute-start | bytes 1204232 | tf_op jit(solution)/shard_map/ppermute | solution.py:26
  37.8 8.5 %collective-permute-start.8 = (bf16[224,896]{1,0:T(8,128)(2,1)S(1)}, bf16[224,896]{1,0:T(8,128)(2,1)S(1)}, u32[]{:S(2)}, u32[]{:S(2)}) collective-permute-start(bf16[224,896]{1,0:T(8,128)(2,1)S(1)} %bitcast.24), channel_id=1, source_target_pairs={{0,96},{96,0},{32,64},{64,32},{1,97},{97,1},{33,65},{65,33},{2,98}... | collective-permute-start | bytes 1204232 | tf_op jit(solution)/shard_map/ppermute | solution.py:26
  46.3 0.1 shard_map.92.pack
  46.4 0.0 collective-permute-done.3.near
  46.4 1.9 %collective-permute-start.4 = (bf16[448,1792]{1,0:T(8,128)(2,1)S(1)}, bf16[448,1792]{1,0:T(8,128)(2,1)S(1)}, u32[]{:S(2)}, u32[]{:S(2)}) collective-permute-start(bf16[448,1792]{1,0:T(8,128)(2,1)S(1)} %shard_map.92.pack), channel_id=1, source_target_pairs={{0,32},{32,0},{64,96},{96,64},{1,33},{33,1},{65,97},{97,65},{2,34}... | collective-permute-start | bytes 4816904 | tf_op jit(solution)/shard_map/ppermute | solution.py:26
  48.3 0.0 collective-permute-done.11.up
  48.3 2.4 %collective-permute-start.12 = (bf16[256,896]{1,0:T(8,128)(2,1)S(1)}, bf16[256,896]{1,0:T(8,128)(2,1)S(1)}, u32[]{:S(2)}, u32[]{:S(2)}) collective-permute-start(bf16[256,896]{1,0:T(8,128)(2,1)S(1)} %collective-permute-done.11.up), channel_id=1, source_target_pairs={{0,96},{64,32},{1,97},{65,33},{2,98},{66,34},{3,99},{67,35},{4,100... | collective-permute-start | bytes 1376264 | tf_op jit(solution)/shard_map/ppermute | solution.py:26
  50.7 0.0 collective-permute-done.7.i1
  50.7 6.3 %collective-permute-start.9 = (bf16[224,896]{1,0:T(8,128)(2,1)S(1)}, bf16[224,896]{1,0:T(8,128)(2,1)S(1)}, u32[]{:S(2)}, u32[]{:S(2)}) collective-permute-start(bf16[224,896]{1,0:T(8,128)(2,1)S(1)} %collective-permute-done.7.i1), channel_id=1, source_target_pairs={{0,96},{96,0},{32,64},{64,32},{1,97},{97,1},{33,65},{65,33},{2,98}... | collective-permute-start | bytes 1204232 | tf_op jit(solution)/shard_map/ppermute | solution.py:26
  57.1 1.9 %collective-permute-start.5 = (bf16[896,128]{1,0:T(8,128)(2,1)S(1)}, bf16[896,128]{1,0:T(8,128)(2,1)S(1)}, u32[]{:S(2)}, u32[]{:S(2)}) collective-permute-start(bf16[896,128]{1,0:T(8,128)(2,1)S(1)} %get-tuple-element.31), channel_id=1, source_target_pairs={{0,96},{96,0},{32,64},{64,32},{1,97},{97,1},{33,65},{65,33},{2,98}... | collective-permute-start | bytes 688136 | tf_op jit(solution)/shard_map/ppermute | solution.py:26
  59.0 0.0 collective-permute-done.8.i2
  59.0 3.5 %collective-permute-start.6 = (bf16[896,128]{1,0:T(8,128)(2,1)S(1)}, bf16[896,128]{1,0:T(8,128)(2,1)S(1)}, u32[]{:S(2)}, u32[]{:S(2)}) collective-permute-start(bf16[896,128]{1,0:T(8,128)(2,1)S(1)} %get-tuple-element.32), channel_id=1, source_target_pairs={{0,64},{64,0},{32,96},{96,32},{1,65},{65,1},{33,97},{97,33},{2,66}... | collective-permute-start | bytes 688136 | tf_op jit(solution)/shard_map/ppermute | solution.py:26
  62.6 8.7 %collective-permute-done.9.i3 = bf16[224,896]{1,0:T(8,128)(2,1)S(1)} collective-permute-done((bf16[224,896]{1,0:T(8,128)(2,1)S(1)}, bf16[224,896]{1,0:T(8,128)(2,1)S(1)}, u32[]{:S(2)}, u32[]{:S(2)}) %collective-permute-start.9) | collective-permute-done | bytes 401440 | tf_op jit(solution)/shard_map/ppermute | solution.py:26
  71.2 0.0 collective-permute-done.12.down
  71.2 0.2 shard_map.93
  71.5 4.7 %collective-permute-done.5.nxt = bf16[896,128]{1,0:T(8,128)(2,1)S(1)} collective-permute-done((bf16[896,128]{1,0:T(8,128)(2,1)S(1)}, bf16[896,128]{1,0:T(8,128)(2,1)S(1)}, u32[]{:S(2)}, u32[]{:S(2)}) %collective-permute-start.5) | collective-permute-done | bytes 229408 | tf_op jit(solution)/shard_map/ppermute | solution.py:26
  76.2 18.1 %collective-permute-done.6.far = bf16[896,128]{1,0:T(8,128)(2,1)S(1)} collective-permute-done((bf16[896,128]{1,0:T(8,128)(2,1)S(1)}, bf16[896,128]{1,0:T(8,128)(2,1)S(1)}, u32[]{:S(2)}, u32[]{:S(2)}) %collective-permute-start.6) | collective-permute-done | bytes 229408 | tf_op jit(solution)/shard_map/ppermute | solution.py:26
  94.2 0.9 shard_map.94
  95.1 31.4 %all_to_all.10 = bf16[128,4,128]{2,1,0:T(4,128)(2,1)S(1)} all-to-all(bf16[128,4,128]{2,1,0:T(4,128)(2,1)S(1)} %bitcast.30), channel_id=1, replica_groups=mesh['zl'=4,'x'=4,'y'=8,'zh'=2,'c'=2] {'zl','y','zh','c'}, dimensions={0} | all-to-all | bytes 262144 | tf_op jit(solution)/shard_map/all_to_all | solution.py:30
  126.4 0.1 convert_reduce_fusion
  126.6 17.5 %all_to_all.11 = bf16[128,4,128]{2,1,0:T(4,128)(2,1)S(1)} all-to-all(bf16[128,4,128]{2,1,0:T(4,128)(2,1)S(1)} %broadcast_in_dim.10), channel_id=1, replica_groups=mesh['zl'=4,'x'=4,'y'=8,'zh'=2,'c'=2] {'zl','y','zh','c'}, dimensions={0} | all-to-all | bytes 262144 | tf_op jit(solution)/shard_map/all_to_all | solution.py:30
  144.2 1.6 shard_map.95.own
  145.8 2.4 %collective-permute-start.15 = (bf16[896,128]{1,0:T(8,128)(2,1)S(1)}, bf16[896,128]{1,0:T(8,128)(2,1)S(1)}, u32[]{:S(2)}, u32[]{:S(2)}) collective-permute-start(bf16[896,128]{1,0:T(8,128)(2,1)S(1)} %shard_map.95.own), channel_id=1, source_target_pairs={{0,64},{64,0},{32,96},{96,32},{1,65},{65,1},{33,97},{97,33},{2,66}... | collective-permute-start | bytes 688136 | tf_op jit(solution)/shard_map/ppermute | solution.py:26
  148.2 3.2 %collective-permute-start.14 = (bf16[896,128]{1,0:T(8,128)(2,1)S(1)}, bf16[896,128]{1,0:T(8,128)(2,1)S(1)}, u32[]{:S(2)}, u32[]{:S(2)}) collective-permute-start(bf16[896,128]{1,0:T(8,128)(2,1)S(1)} %shard_map.95.own), channel_id=1, source_target_pairs={{0,96},{96,0},{32,64},{64,32},{1,97},{97,1},{33,65},{65,33},{2,98}... | collective-permute-start | bytes 688136 | tf_op jit(solution)/shard_map/ppermute | solution.py:26
  151.4 2.9 %collective-permute-start.13 = (bf16[896,128]{1,0:T(8,128)(2,1)S(1)}, bf16[896,128]{1,0:T(8,128)(2,1)S(1)}, u32[]{:S(2)}, u32[]{:S(2)}) collective-permute-start(bf16[896,128]{1,0:T(8,128)(2,1)S(1)} %shard_map.95.own), channel_id=1, source_target_pairs={{0,32},{32,0},{64,96},{96,64},{1,33},{33,1},{65,97},{97,65},{2,34}... | collective-permute-start | bytes 688136 | tf_op jit(solution)/shard_map/ppermute | solution.py:26
  154.3 0.0 collective-permute-done.4.came
  154.4 2.8 %shard_map.96 = (bf16[384,896]{1,0:T(8,128)(2,1)S(1)}, bf16[384,384]{1,0:T(8,128)(2,1)S(1)}, f32[384,512]{1,0:T(8,128)S(1)}) custom-call(s32[1]{0:T(128)} %bitcast.at, bf16[448,1792]{1,0:T(8,128)(2,1)S(1)} %shard_map.92.pack, bf16[448,1792]{1,0:T(8,128)(2,1)S(1)} %collective-permute-done.4.came, bf16[448,896]{1,0:T(8,128)(2,1)S(1)} %bitcast.14, ...), custom_call_target="tpu_custom_call" | custom-call | flops 1585446912 | bytes 5849092 | tf_op jit(solution)/shard_map/pallas_call | solution.py:44
  157.2 0.0 collective-permute-done.15.far
  157.2 4.4 %collective-permute-done.14.nxt = bf16[896,128]{1,0:T(8,128)(2,1)S(1)} collective-permute-done((bf16[896,128]{1,0:T(8,128)(2,1)S(1)}, bf16[896,128]{1,0:T(8,128)(2,1)S(1)}, u32[]{:S(2)}, u32[]{:S(2)}) %collective-permute-start.14) | collective-permute-done | bytes 229408 | tf_op jit(solution)/shard_map/ppermute | solution.py:26
  161.6 0.9 shard_map.97.most
  162.5 0.0 collective-permute-done.13.near
  162.6 1.4 shard_map.98
  (16 shorter events, 0.1 us)
Async XLA Ops:
  0.0 13.4 %copy-start.2 = (bf16[1,128,896]{2,1,0:T(8,128)(2,1)S(1)}, bf16[1,128,896]{2,1,0:T(8,128)(2,1)}, u32[]{:S(2)}) copy-start(bf16[1,128,896]{2,1,0:T(8,128)(2,1)} %param.15) | copy-start | bytes 688132
  0.0 30.3 %copy-start = (bf16[1,448,896]{2,1,0:T(8,128)(2,1)S(1)}, bf16[1,448,896]{2,1,0:T(8,128)(2,1)}, u32[]{:S(2)}) copy-start(bf16[1,448,896]{2,1,0:T(8,128)(2,1)} %param.13) | copy-start | bytes 2408452
  0.0 30.3 %copy-start.1 = (bf16[1,448,896]{2,1,0:T(8,128)(2,1)S(1)}, bf16[1,448,896]{2,1,0:T(8,128)(2,1)}, u32[]{:S(2)}) copy-start(bf16[1,448,896]{2,1,0:T(8,128)(2,1)} %param.12) | copy-start | bytes 2408452
  1.4 21.4 %collective-permute-start.2 = (bf16[448,512]{1,0:T(8,128)(2,1)S(1)}, bf16[448,512]{1,0:T(8,128)(2,1)S(1)}, u32[]{:S(2)}, u32[]{:S(2)}) collective-permute-start(bf16[448,512]{1,0:T(8,128)(2,1)S(1)} %slice_select_fusion), channel_id=1, source_target_pairs={{0,32},{32,0},{64,96},{96,64},{1,33},{33,1},{65,97},{97,65},{2,34}... | collective-permute-start | bytes 1376264 | tf_op jit(solution)/shard_map/ppermute | solution.py:26
  8.1 14.7 %collective-permute-start = (bf16[448,512]{1,0:T(8,128)(2,1)S(1)}, bf16[448,512]{1,0:T(8,128)(2,1)S(1)}, u32[]{:S(2)}, u32[]{:S(2)}) collective-permute-start(bf16[448,512]{1,0:T(8,128)(2,1)S(1)} %get-tuple-element.24.top), channel_id=1, source_target_pairs={{0,32},{32,0},{64,96},{96,64},{1,33},{33,1},{65,97},{97,65},{2,34}... | collective-permute-start | bytes 1376264 | tf_op jit(solution)/shard_map/ppermute | solution.py:26
  10.0 20.3 %collective-permute-start.1 = (bf16[448,512]{1,0:T(8,128)(2,1)S(1)}, bf16[448,512]{1,0:T(8,128)(2,1)S(1)}, u32[]{:S(2)}, u32[]{:S(2)}) collective-permute-start(bf16[448,512]{1,0:T(8,128)(2,1)S(1)} %get-tuple-element.25.bot), channel_id=1, source_target_pairs={{0,32},{64,96},{1,33},{65,97},{2,34},{66,98},{3,35},{67,99},{4,36}... | collective-permute-start | bytes 1376264 | tf_op jit(solution)/shard_map/ppermute | solution.py:26
  13.4 8.0 %collective-permute-start.10 = (bf16[128,896]{1,0:T(8,128)(2,1)S(1)}, bf16[128,896]{1,0:T(8,128)(2,1)S(1)}, u32[]{:S(2)}, u32[]{:S(2)}) collective-permute-start(bf16[128,896]{1,0:T(8,128)(2,1)S(1)} %bitcast.17), channel_id=1, source_target_pairs={{0,96},{96,0},{32,64},{64,32},{1,97},{97,1},{33,65},{65,33},{2,98}... | collective-permute-start | bytes 688136 | tf_op jit(solution)/shard_map/ppermute | solution.py:26
  21.4 26.9 %collective-permute-start.11 = (bf16[256,896]{1,0:T(8,128)(2,1)S(1)}, bf16[256,896]{1,0:T(8,128)(2,1)S(1)}, u32[]{:S(2)}, u32[]{:S(2)}) collective-permute-start(bf16[256,896]{1,0:T(8,128)(2,1)S(1)} %pad_maximum_fusion), channel_id=1, source_target_pairs={{32,0},{96,64},{33,1},{97,65},{34,2},{98,66},{35,3},{99,67},{36,4}... | collective-permute-start | bytes 1376264 | tf_op jit(solution)/shard_map/ppermute | solution.py:26
  30.3 5.5 %copy-start.5 = (bf16[1,224,896]{2,1,0:T(8,128)(2,1)S(1)}, bf16[1,224,896]{2,1,0:T(8,128)(2,1)}, u32[]{:S(2)}) copy-start(bf16[1,224,896]{2,1,0:T(8,128)(2,1)} %param.14) | copy-start | bytes 1204228
  31.7 14.7 %collective-permute-start.3 = (bf16[896,128]{1,0:T(8,128)(2,1)S(1)}, bf16[896,128]{1,0:T(8,128)(2,1)S(1)}, u32[]{:S(2)}, u32[]{:S(2)}) collective-permute-start(bf16[896,128]{1,0:T(8,128)(2,1)S(1)} %get-tuple-element.27), channel_id=1, source_target_pairs={{0,32},{32,0},{64,96},{96,64},{1,33},{33,1},{65,97},{97,65},{2,34}... | collective-permute-start | bytes 688136 | tf_op jit(solution)/shard_map/ppermute | solution.py:26
  35.8 14.9 %collective-permute-start.7 = (bf16[224,896]{1,0:T(8,128)(2,1)S(1)}, bf16[224,896]{1,0:T(8,128)(2,1)S(1)}, u32[]{:S(2)}, u32[]{:S(2)}) collective-permute-start(bf16[224,896]{1,0:T(8,128)(2,1)S(1)} %bitcast.23), channel_id=1, source_target_pairs={{0,32},{32,0},{64,96},{96,64},{1,33},{33,1},{65,97},{97,65},{2,34}... | collective-permute-start | bytes 1204232 | tf_op jit(solution)/shard_map/ppermute | solution.py:26
  37.8 21.2 %collective-permute-start.8 = (bf16[224,896]{1,0:T(8,128)(2,1)S(1)}, bf16[224,896]{1,0:T(8,128)(2,1)S(1)}, u32[]{:S(2)}, u32[]{:S(2)}) collective-permute-start(bf16[224,896]{1,0:T(8,128)(2,1)S(1)} %bitcast.24), channel_id=1, source_target_pairs={{0,96},{96,0},{32,64},{64,32},{1,97},{97,1},{33,65},{65,33},{2,98}... | collective-permute-start | bytes 1204232 | tf_op jit(solution)/shard_map/ppermute | solution.py:26
  46.4 107.9 %collective-permute-start.4 = (bf16[448,1792]{1,0:T(8,128)(2,1)S(1)}, bf16[448,1792]{1,0:T(8,128)(2,1)S(1)}, u32[]{:S(2)}, u32[]{:S(2)}) collective-permute-start(bf16[448,1792]{1,0:T(8,128)(2,1)S(1)} %shard_map.92.pack), channel_id=1, source_target_pairs={{0,32},{32,0},{64,96},{96,64},{1,33},{33,1},{65,97},{97,65},{2,34}... | collective-permute-start | bytes 4816904 | tf_op jit(solution)/shard_map/ppermute | solution.py:26
  48.3 22.9 %collective-permute-start.12 = (bf16[256,896]{1,0:T(8,128)(2,1)S(1)}, bf16[256,896]{1,0:T(8,128)(2,1)S(1)}, u32[]{:S(2)}, u32[]{:S(2)}) collective-permute-start(bf16[256,896]{1,0:T(8,128)(2,1)S(1)} %collective-permute-done.11.up), channel_id=1, source_target_pairs={{0,96},{64,32},{1,97},{65,33},{2,98},{66,34},{3,99},{67,35},{4,100... | collective-permute-start | bytes 1376264 | tf_op jit(solution)/shard_map/ppermute | solution.py:26
  50.7 20.5 %collective-permute-start.9 = (bf16[224,896]{1,0:T(8,128)(2,1)S(1)}, bf16[224,896]{1,0:T(8,128)(2,1)S(1)}, u32[]{:S(2)}, u32[]{:S(2)}) collective-permute-start(bf16[224,896]{1,0:T(8,128)(2,1)S(1)} %collective-permute-done.7.i1), channel_id=1, source_target_pairs={{0,96},{96,0},{32,64},{64,32},{1,97},{97,1},{33,65},{65,33},{2,98}... | collective-permute-start | bytes 1204232 | tf_op jit(solution)/shard_map/ppermute | solution.py:26
  57.1 19.1 %collective-permute-start.5 = (bf16[896,128]{1,0:T(8,128)(2,1)S(1)}, bf16[896,128]{1,0:T(8,128)(2,1)S(1)}, u32[]{:S(2)}, u32[]{:S(2)}) collective-permute-start(bf16[896,128]{1,0:T(8,128)(2,1)S(1)} %get-tuple-element.31), channel_id=1, source_target_pairs={{0,96},{96,0},{32,64},{64,32},{1,97},{97,1},{33,65},{65,33},{2,98}... | collective-permute-start | bytes 688136 | tf_op jit(solution)/shard_map/ppermute | solution.py:26
  59.0 35.2 %collective-permute-start.6 = (bf16[896,128]{1,0:T(8,128)(2,1)S(1)}, bf16[896,128]{1,0:T(8,128)(2,1)S(1)}, u32[]{:S(2)}, u32[]{:S(2)}) collective-permute-start(bf16[896,128]{1,0:T(8,128)(2,1)S(1)} %get-tuple-element.32), channel_id=1, source_target_pairs={{0,64},{64,0},{32,96},{96,32},{1,65},{65,1},{33,97},{97,33},{2,66}... | collective-permute-start | bytes 688136 | tf_op jit(solution)/shard_map/ppermute | solution.py:26
  94.2 49.9 %copy-start.4 = (bf16[512,512]{1,0:T(8,128)(2,1)S(1)}, bf16[512,512]{1,0:T(8,128)(2,1)}, u32[]{:S(2)}) copy-start(bf16[512,512]{1,0:T(8,128)(2,1)} %inv.1) | copy-start | bytes 1572868
  144.2 10.2 %copy-start.3 = (bf16[1,1,896,384]{3,2,1,0:T(8,128)(2,1)S(1)}, bf16[1,1,896,384]{3,2,1,0:T(8,128)(2,1)}, u32[]{:S(2)}) copy-start(bf16[1,1,896,384]{3,2,1,0:T(8,128)(2,1)} %param.11) | copy-start | bytes 2064388
  144.2 10.2 %copy-start.6 = (bf16[1,1,384,512]{3,2,1,0:T(8,128)(2,1)S(1)}, bf16[1,1,384,512]{3,2,1,0:T(8,128)(2,1)}, u32[]{:S(2)}) copy-start(bf16[1,1,384,512]{3,2,1,0:T(8,128)(2,1)} %param.9) | copy-start | bytes 1179652
  144.2 10.2 %copy-start.7 = (bf16[1,1,384,384]{3,2,1,0:T(8,128)(2,1)S(1)}, bf16[1,1,384,384]{3,2,1,0:T(8,128)(2,1)}, u32[]{:S(2)}) copy-start(bf16[1,1,384,384]{3,2,1,0:T(8,128)(2,1)} %param.10) | copy-start | bytes 884740
  145.8 11.5 %collective-permute-start.15 = (bf16[896,128]{1,0:T(8,128)(2,1)S(1)}, bf16[896,128]{1,0:T(8,128)(2,1)S(1)}, u32[]{:S(2)}, u32[]{:S(2)}) collective-permute-start(bf16[896,128]{1,0:T(8,128)(2,1)S(1)} %shard_map.95.own), channel_id=1, source_target_pairs={{0,64},{64,0},{32,96},{96,32},{1,65},{65,1},{33,97},{97,33},{2,66}... | collective-permute-start | bytes 688136 | tf_op jit(solution)/shard_map/ppermute | solution.py:26
  148.2 13.4 %collective-permute-start.14 = (bf16[896,128]{1,0:T(8,128)(2,1)S(1)}, bf16[896,128]{1,0:T(8,128)(2,1)S(1)}, u32[]{:S(2)}, u32[]{:S(2)}) collective-permute-start(bf16[896,128]{1,0:T(8,128)(2,1)S(1)} %shard_map.95.own), channel_id=1, source_target_pairs={{0,96},{96,0},{32,64},{64,32},{1,97},{97,1},{33,65},{65,33},{2,98}... | collective-permute-start | bytes 688136 | tf_op jit(solution)/shard_map/ppermute | solution.py:26
  151.4 11.1 %collective-permute-start.13 = (bf16[896,128]{1,0:T(8,128)(2,1)S(1)}, bf16[896,128]{1,0:T(8,128)(2,1)S(1)}, u32[]{:S(2)}, u32[]{:S(2)}) collective-permute-start(bf16[896,128]{1,0:T(8,128)(2,1)S(1)} %shard_map.95.own), channel_id=1, source_target_pairs={{0,32},{32,0},{64,96},{96,64},{1,33},{33,1},{65,97},{97,65},{2,34}... | collective-permute-start | bytes 688136 | tf_op jit(solution)/shard_map/ppermute | solution.py:26

commit v8 on v7

--- a/solution.py
+++ b/solution.py
@@ -60,13 +60,6 @@
     for first in range(0, size, CHUNK):
         last = min(first + CHUNK, size)
         out[first:last] = mul(lower[first:last, :last], vector[:last]).astype(out.dtype)
-
-
-def lower_mul_t(lower, vector, out):
-    size = vector.shape[0]
-    for first in range(0, size, CHUNK):
-        last = min(first + CHUNK, size)
-        out[first:last] = mul_t(lower[first:, first:last], vector[first:]).astype(out.dtype)
 
 
 def others(x):
@@ -108,15 +101,22 @@
     )(rows, *args)
 
 
-def first_kernel(at, inv, top, bot, came_top, came_bot, coup, came_coup, first, own, near, nxt, far, rhs, held, turned):
+def pre_kernel(inv, bot, came, part, rhs):
+    pad = rhs.shape[0] - bot.shape[0]
+    rhs[:pad] = jnp.zeros((pad, rhs.shape[1]), BF)
+    rhs[pad:] = (-(bot[...].astype(F32) + came[...].astype(F32))).astype(BF)
+    part[...] = mul(inv[:, inv.shape[1] - rhs.shape[0] :], rhs[...])
+
+
+def first_kernel(at, inv, part, top, came_top, coup, came_coup, first, own, near, nxt, far, rhs, held, turned):
     x = at[0]
     high = x % 2
     half, sep = inv.shape
     ports = top.shape[1]
     width = held.shape[0]
     rhs[:half] = (-(top[...].astype(F32) + came_top[...].astype(F32))).astype(BF)
-    rhs[half:] = (-(bot[...].astype(F32) + came_bot[...].astype(F32))).astype(BF)
-    fwd = mul(inv[...], rhs[...]).astype(BF)
+    rhs[half:] = jnp.zeros((width - half, ports), BF)
+    fwd = (part[...] + mul(inv[:, :width], rhs[...])).astype(BF)
     first[...] = fwd
     pad = width - half
     held[:pad] = jnp.zeros((pad, ports), BF)
@@ -150,7 +150,7 @@
     return zip((x,) + others(x), refs)
 
 
-def join_kernel(at, i0, i1, i2, i3, b0, up, nxt, down, inv, coup):
+def join_kernel(at, rows, i0, i1, i2, i3, b0, up, nxt, down, border, inv, coup, fold):
     x = at[0]
     each = i0.shape[0]
     for who, ref in pieces(x, (i0, i1, i2, i3)):
@@ -159,27 +159,29 @@
     near = up[:count] + down[count:]
     far = up[count:] + down[:count]
     for who, block in pieces(x, (b0[...], near, nxt[...], far)):
-        coup[pl.ds(pl.multiple_of(who * count, count), count)] = block
-
-
-def second_kernel(rows, own, near, nxt, far, inv, coup, fwd, tiles, rhs):
+        first = pl.multiple_of(who * count, count)
+        live = lax.broadcasted_iota(jnp.int32, block.shape, 0) + first < rows[0]
+        coup[pl.ds(first, count)] = jnp.where(live, block.astype(F32), 0.0).astype(BF)
+    both = mul_t(border[...], border[...]).astype(BF)
+    down_two = mul_t(coup[...], both).astype(BF)
+    fold[...] = mul_t(inv[...], down_two).astype(BF)
+
+
+def second_kernel(own, near, nxt, far, inv, coup, fwd, tiles, rhs):
     total = own[...].astype(F32) + near[...].astype(F32)
     total = total + (nxt[...].astype(F32) + far[...].astype(F32))
     rhs[...] = (-total).astype(BF)
     lower_mul(inv, rhs, fwd)
     for first in range(0, tiles.shape[0], CHUNK):
-        part = mul(coup[first : first + CHUNK], fwd[...])
-        live = lax.broadcasted_iota(jnp.int32, part.shape, 0) + first < rows[0]
-        tiles[first : first + CHUNK] = jnp.where(live, part, 0.0).astype(BF)
-
-
-def border_kernel(rows, rhs, inv, fwd, second, coup, back, mid, sol, diff):
-    lower_mul(inv, rhs, mid)
-    lower_mul_t(inv, mid, sol)
-    live = lax.broadcasted_iota(jnp.int32, sol.shape, 0) < rows[0]
-    masked = jnp.where(live, sol[...], 0.0).astype(BF)
-    diff[...] = (fwd[...].astype(F32) - mul_t(coup[...], masked)).astype(BF)
-    lower_mul_t(second, diff, back)
+        tiles[first : first + CHUNK] = mul(coup[first : first + CHUNK], fwd[...]).astype(BF)
+
+
+def border_kernel(rhs, fwd, second, fold, back):
+    size = fwd.shape[0]
+    for first in range(0, size, CHUNK):
+        last = min(first + CHUNK, size)
+        local = mul_t(second[first:, first:last], fwd[first:])
+        back[first:last] = (local - mul(fold[first:last], rhs[...])).astype(BF)
 
 
 def fold_kernel(at, pack, came, coup, came_coup, leaf_coup, loads, leaf_inv, fold_t, inv_t, rest, full, fold):
@@ -266,16 +268,24 @@
     i_far = send(i_near, NEXT)
     b_down = send(b_up, BACK)
     quarter = ((sep, share), BF)
+    (part_one,) = call(
+        pre_kernel,
+        [((half, ports), F32)],
+        [((width, ports), BF)],
+        inv_one,
+        bot,
+        came_bot,
+        flops=2 * half * ports * width,
+    )
     fwd_one, own, near, nxt, far = call(
         first_kernel,
         [((half, ports), BF)] + [quarter] * 4,
-        [((sep, ports), BF), ((width, ports), BF), ((width, ports), BF)],
+        [((width, ports), BF)] * 3,
         at,
         inv_one,
+        part_one,
         top,
-        bot,
         came_top,
-        came_bot,
         coup_two,
         came_coup,
         flops=2 * half * ports * sep + 2 * sep * ports * width,
@@ -294,11 +304,12 @@
     )
     late_pack, near = lax.optimization_barrier((pack, near))
     came_pack = send(late_pack, NEAR)
-    inv_full, coup_full = call(
+    inv_full, coup_full, border_fold = call(
         join_kernel,
-        [((sep, sep), BF), ((border, sep), BF)],
+        [((sep, sep), BF), ((border, sep), BF), ((sep, border), BF)],
         [],
         at,
+        border_rows,
         inv_two,
         i_near,
         i_next,
@@ -307,12 +318,12 @@
         b_up,
         b_next,
         b_down,
+        border_inverse,
     )
     fwd_two, tiles = call(
         second_kernel,
         [quarter, ((border, share), BF)],
         [quarter],
-        border_rows,
         own,
         near,
         nxt,
@@ -328,14 +339,12 @@
     (back_two,) = call(
         border_kernel,
         [quarter],
-        [((border, share), BF), ((border, share), F32), quarter],
-        border_rows,
+        [],
         rhs_border,
-        border_inverse,
         fwd_two,
         inv_full,
-        coup_full,
-        flops=2 * share * (2 * border * border + border * sep + sep * sep),
+        border_fold,
+        flops=2 * share * (border * sep + sep * sep),
     )
     back_far = send(back_two, ACROSS)
     back_next = send(back_two, NEXT)

time: 165 us -> 165 us (level)
    pallas_call x8 -> x9, Pallas kernels: 9.37 us -> 10.8 us  [call(): pl.pallas_call(kernel, out_shape=[jax.ShapeDtypeStruct(s, d) for s, d in...]
  transfers between devices with their start and end apart: 16 -> 16, of which waited for: 6 -> 7; matrix products, arithmetic and copies ran while one was open for 0% -> 0% of each run, Pallas kernels for 6% -> 6%
where the time goes in v8:
time: 165 us; the launch traced here: 164 us
  starting transfers between devices  52.2 us (32%)
  waiting for transfers between devices  48.9 us (30%)
  blocking collectives  48.9 us (30%)
  Pallas kernels  13 us (8%)
    ppermute x16, starting transfers between devices, send(): return lax.ppermute(x, 'x', pairs)  52.2 us
    all_to_all x2, blocking collectives, to_group(): return lax.all_to_all(tiles, GROUP, split_axis=0, concat_axis=0, tiled=True)  48.9 us
    ppermute x16, waiting for transfers between devices, send(): return lax.ppermute(x, 'x', pairs)  48.9 us
    pallas_call x9, Pallas kernels, call(): pl.pallas_call(kernel, out_shape=[jax.ShapeDtypeStruct(s, d) for s, d in...  10.8 us
  transfers between devices with their start and end apart: 16, of which 7 were waited for; matrix products, arithmetic and copies ran while one was open for 0% of the time, Pallas kernels for 6%

profile of v8, /device:TPU:1, one launch (start us, length us, event | category | flops | bytes accessed | tf_op | source)
XLA Modules:
  0.0 164.4 jit_solution(13830652294282787852)
XLA Ops:
  0.8 2.2 %k_leaf.1 = (bf16[448,512]{1,0:T(8,128)(2,1)S(1)}, bf16[448,512]{1,0:T(8,128)(2,1)S(1)}) custom-call(s32[1]{0:T(128)S(6)} %copy.10.rows, bf16[384,512]{1,0:T(8,128)(2,1)} %bitcast.27, bf16[384,384]{1,0:T(8,128)(2,1)} %bitcast.29, bf16[896,384]{1,0:T(8,128)(2,1)} %bitcast.21), custom_call_target="tpu_custom_call" | custom-call | tf_op jit(solution)/shard_map/k_leaf/pallas_call | solution.py:91
  2.9 4.0 %collective-permute-start = (bf16[448,512]{1,0:T(8,128)(2,1)S(1)}, bf16[448,512]{1,0:T(8,128)(2,1)S(1)}, u32[]{:S(2)}, u32[]{:S(2)}) collective-permute-start(bf16[448,512]{1,0:T(8,128)(2,1)S(1)} %get-tuple-element.25.bot), channel_id=1, source_target_pairs={{0,32},{64,96},{1,33},{65,97},{2,34},{66,98},{3,35},{67,99},{4,36}... | collective-permute-start | bytes 1376264 | tf_op jit(solution)/shard_map/ppermute | solution.py:26
  6.9 0.1 slice_select_fusion
  7.0 1.9 %collective-permute-start.2 = (bf16[448,512]{1,0:T(8,128)(2,1)S(1)}, bf16[448,512]{1,0:T(8,128)(2,1)S(1)}, u32[]{:S(2)}, u32[]{:S(2)}) collective-permute-start(bf16[448,512]{1,0:T(8,128)(2,1)S(1)} %slice_select_fusion), channel_id=1, source_target_pairs={{0,32},{32,0},{64,96},{96,64},{1,33},{33,1},{65,97},{97,65},{2,34}... | collective-permute-start | bytes 1376264 | tf_op jit(solution)/shard_map/ppermute | solution.py:26
  8.9 3.4 %collective-permute-start.1 = (bf16[448,512]{1,0:T(8,128)(2,1)S(1)}, bf16[448,512]{1,0:T(8,128)(2,1)S(1)}, u32[]{:S(2)}, u32[]{:S(2)}) collective-permute-start(bf16[448,512]{1,0:T(8,128)(2,1)S(1)} %get-tuple-element.26.top), channel_id=1, source_target_pairs={{0,32},{32,0},{64,96},{96,64},{1,33},{33,1},{65,97},{97,65},{2,34}... | collective-permute-start | bytes 1376264 | tf_op jit(solution)/shard_map/ppermute | solution.py:26
  12.3 3.2 %collective-permute-start.10 = (bf16[128,896]{1,0:T(8,128)(2,1)S(1)}, bf16[128,896]{1,0:T(8,128)(2,1)S(1)}, u32[]{:S(2)}, u32[]{:S(2)}) collective-permute-start(bf16[128,896]{1,0:T(8,128)(2,1)S(1)} %bitcast.18), channel_id=1, source_target_pairs={{0,96},{96,0},{32,64},{64,32},{1,97},{97,1},{33,65},{65,33},{2,98}... | collective-permute-start | bytes 688136 | tf_op jit(solution)/shard_map/ppermute | solution.py:26
  15.5 4.8 %collective-permute-done.10.nxt = bf16[128,896]{1,0:T(8,128)(2,1)S(1)} collective-permute-done((bf16[128,896]{1,0:T(8,128)(2,1)S(1)}, bf16[128,896]{1,0:T(8,128)(2,1)S(1)}, u32[]{:S(2)}, u32[]{:S(2)}) %collective-permute-start.10) | collective-permute-done | bytes 229408 | tf_op jit(solution)/shard_map/ppermute | solution.py:26
  20.3 1.3 collective-permute-start.11
  21.6 0.0 collective-permute-done.came
  21.7 0.4 shard_map.91.part
  22.1 0.6 collective-permute-done.2.came_coup
  22.7 9.8 %collective-permute-done.1.came_top = bf16[448,512]{1,0:T(8,128)(2,1)S(1)} collective-permute-done((bf16[448,512]{1,0:T(8,128)(2,1)S(1)}, bf16[448,512]{1,0:T(8,128)(2,1)S(1)}, u32[]{:S(2)}, u32[]{:S(2)}) %collective-permute-start.1) | collective-permute-done | bytes 458784 | tf_op jit(solution)/shard_map/ppermute | solution.py:26
  32.5 1.2 shard_map.92
  33.7 4.1 %collective-permute-start.3 = (bf16[896,128]{1,0:T(8,128)(2,1)S(1)}, bf16[896,128]{1,0:T(8,128)(2,1)S(1)}, u32[]{:S(2)}, u32[]{:S(2)}) collective-permute-start(bf16[896,128]{1,0:T(8,128)(2,1)S(1)} %get-tuple-element.28), channel_id=1, source_target_pairs={{0,32},{32,0},{64,96},{96,64},{1,33},{33,1},{65,97},{97,65},{2,34}... | collective-permute-start | bytes 688136 | tf_op jit(solution)/shard_map/ppermute | solution.py:26
  37.8 1.9 %collective-permute-start.7 = (bf16[224,896]{1,0:T(8,128)(2,1)S(1)}, bf16[224,896]{1,0:T(8,128)(2,1)S(1)}, u32[]{:S(2)}, u32[]{:S(2)}) collective-permute-start(bf16[224,896]{1,0:T(8,128)(2,1)S(1)} %bitcast.24), channel_id=1, source_target_pairs={{0,32},{32,0},{64,96},{96,64},{1,33},{33,1},{65,97},{97,65},{2,34}... | collective-permute-start | bytes 1204232 | tf_op jit(solution)/shard_map/ppermute | solution.py:26
  39.7 7.9 %collective-permute-start.8 = (bf16[224,896]{1,0:T(8,128)(2,1)S(1)}, bf16[224,896]{1,0:T(8,128)(2,1)S(1)}, u32[]{:S(2)}, u32[]{:S(2)}) collective-permute-start(bf16[224,896]{1,0:T(8,128)(2,1)S(1)} %bitcast.25), channel_id=1, source_target_pairs={{0,96},{96,0},{32,64},{64,32},{1,97},{97,1},{33,65},{65,33},{2,98}... | collective-permute-start | bytes 1204232 | tf_op jit(solution)/shard_map/ppermute | solution.py:26
  47.6 0.0 copy-start.4
  47.6 0.1 shard_map.93.pack
  47.7 0.0 collective-permute-done.3.near
  47.7 1.9 %collective-permute-start.4 = (bf16[448,1792]{1,0:T(8,128)(2,1)S(1)}, bf16[448,1792]{1,0:T(8,128)(2,1)S(1)}, u32[]{:S(2)}, u32[]{:S(2)}) collective-permute-start(bf16[448,1792]{1,0:T(8,128)(2,1)S(1)} %shard_map.93.pack), channel_id=1, source_target_pairs={{0,32},{32,0},{64,96},{96,64},{1,33},{33,1},{65,97},{97,65},{2,34}... | collective-permute-start | bytes 4816904 | tf_op jit(solution)/shard_map/ppermute | solution.py:26
  49.7 0.0 collective-permute-done.11.up
  49.7 2.3 %collective-permute-start.12 = (bf16[256,896]{1,0:T(8,128)(2,1)S(1)}, bf16[256,896]{1,0:T(8,128)(2,1)S(1)}, u32[]{:S(2)}, u32[]{:S(2)}) collective-permute-start(bf16[256,896]{1,0:T(8,128)(2,1)S(1)} %collective-permute-done.11.up), channel_id=1, source_target_pairs={{0,96},{64,32},{1,97},{65,33},{2,98},{66,34},{3,99},{67,35},{4,100... | collective-permute-start | bytes 1376264 | tf_op jit(solution)/shard_map/ppermute | solution.py:26
  52.0 0.0 collective-permute-done.7.i1
  52.0 6.3 %collective-permute-start.9 = (bf16[224,896]{1,0:T(8,128)(2,1)S(1)}, bf16[224,896]{1,0:T(8,128)(2,1)S(1)}, u32[]{:S(2)}, u32[]{:S(2)}) collective-permute-start(bf16[224,896]{1,0:T(8,128)(2,1)S(1)} %collective-permute-done.7.i1), channel_id=1, source_target_pairs={{0,96},{96,0},{32,64},{64,32},{1,97},{97,1},{33,65},{65,33},{2,98}... | collective-permute-start | bytes 1204232 | tf_op jit(solution)/shard_map/ppermute | solution.py:26
  58.4 1.9 %collective-permute-start.5 = (bf16[896,128]{1,0:T(8,128)(2,1)S(1)}, bf16[896,128]{1,0:T(8,128)(2,1)S(1)}, u32[]{:S(2)}, u32[]{:S(2)}) collective-permute-start(bf16[896,128]{1,0:T(8,128)(2,1)S(1)} %get-tuple-element.32), channel_id=1, source_target_pairs={{0,96},{96,0},{32,64},{64,32},{1,97},{97,1},{33,65},{65,33},{2,98}... | collective-permute-start | bytes 688136 | tf_op jit(solution)/shard_map/ppermute | solution.py:26
  60.3 0.0 collective-permute-done.8.i2
  60.3 3.6 %collective-permute-start.6 = (bf16[896,128]{1,0:T(8,128)(2,1)S(1)}, bf16[896,128]{1,0:T(8,128)(2,1)S(1)}, u32[]{:S(2)}, u32[]{:S(2)}) collective-permute-start(bf16[896,128]{1,0:T(8,128)(2,1)S(1)} %get-tuple-element.33), channel_id=1, source_target_pairs={{0,64},{64,0},{32,96},{96,32},{1,65},{65,1},{33,97},{97,33},{2,66}... | collective-permute-start | bytes 688136 | tf_op jit(solution)/shard_map/ppermute | solution.py:26
  63.9 8.7 %collective-permute-done.9.i3 = bf16[224,896]{1,0:T(8,128)(2,1)S(1)} collective-permute-done((bf16[224,896]{1,0:T(8,128)(2,1)S(1)}, bf16[224,896]{1,0:T(8,128)(2,1)S(1)}, u32[]{:S(2)}, u32[]{:S(2)}) %collective-permute-start.9) | collective-permute-done | bytes 401440 | tf_op jit(solution)/shard_map/ppermute | solution.py:26
  72.6 0.0 collective-permute-done.12.down
  72.6 0.0 copy-done.4
  72.6 2.3 %shard_map.94 = (bf16[896,896]{1,0:T(8,128)(2,1)S(1)}, bf16[512,896]{1,0:T(8,128)(2,1)S(1)}, bf16[896,512]{1,0:T(8,128)(2,1)S(1)}) custom-call(s32[1]{0:T(128)} %bitcast.at, s32[1]{0:T(128)S(6)} %copy.10.rows, bf16[224,896]{1,0:T(8,128)(2,1)S(1)} %bitcast.26, bf16[224,896]{1,0:T(8,128)(2,1)S(1)} %collective-permute-done.7.i1, ...), custom_call_target="tpu_custom_call" | custom-call | bytes 3506184 | tf_op jit(solution)/shard_map/pallas_call | solution.py:44
  74.9 2.6 %collective-permute-done.5.nxt = bf16[896,128]{1,0:T(8,128)(2,1)S(1)} collective-permute-done((bf16[896,128]{1,0:T(8,128)(2,1)S(1)}, bf16[896,128]{1,0:T(8,128)(2,1)S(1)}, u32[]{:S(2)}, u32[]{:S(2)}) %collective-permute-start.5) | collective-permute-done | bytes 229408 | tf_op jit(solution)/shard_map/ppermute | solution.py:26
  77.5 18.1 %collective-permute-done.6.far = bf16[896,128]{1,0:T(8,128)(2,1)S(1)} collective-permute-done((bf16[896,128]{1,0:T(8,128)(2,1)S(1)}, bf16[896,128]{1,0:T(8,128)(2,1)S(1)}, u32[]{:S(2)}, u32[]{:S(2)}) %collective-permute-start.6) | collective-permute-done | bytes 229408 | tf_op jit(solution)/shard_map/ppermute | solution.py:26
  95.5 0.8 shard_map.95
  96.4 31.4 %all_to_all.10 = bf16[128,4,128]{2,1,0:T(4,128)(2,1)S(1)} all-to-all(bf16[128,4,128]{2,1,0:T(4,128)(2,1)S(1)} %bitcast.31), channel_id=1, replica_groups=mesh['zl'=4,'x'=4,'y'=8,'zh'=2,'c'=2] {'zl','y','zh','c'}, dimensions={0} | all-to-all | bytes 262144 | tf_op jit(solution)/shard_map/all_to_all | solution.py:30
  127.8 0.1 convert_reduce_fusion
  128.0 17.5 %all_to_all.11 = bf16[128,4,128]{2,1,0:T(4,128)(2,1)S(1)} all-to-all(bf16[128,4,128]{2,1,0:T(4,128)(2,1)S(1)} %broadcast_in_dim.10), channel_id=1, replica_groups=mesh['zl'=4,'x'=4,'y'=8,'zh'=2,'c'=2] {'zl','y','zh','c'}, dimensions={0} | all-to-all | bytes 262144 | tf_op jit(solution)/shard_map/all_to_all | solution.py:30
  145.5 0.7 shard_map.96.own
  146.2 2.4 %collective-permute-start.15 = (bf16[896,128]{1,0:T(8,128)(2,1)S(1)}, bf16[896,128]{1,0:T(8,128)(2,1)S(1)}, u32[]{:S(2)}, u32[]{:S(2)}) collective-permute-start(bf16[896,128]{1,0:T(8,128)(2,1)S(1)} %shard_map.96.own), channel_id=1, source_target_pairs={{0,64},{64,0},{32,96},{96,32},{1,65},{65,1},{33,97},{97,33},{2,66}... | collective-permute-start | bytes 688136 | tf_op jit(solution)/shard_map/ppermute | solution.py:26
  148.7 3.2 %collective-permute-start.14 = (bf16[896,128]{1,0:T(8,128)(2,1)S(1)}, bf16[896,128]{1,0:T(8,128)(2,1)S(1)}, u32[]{:S(2)}, u32[]{:S(2)}) collective-permute-start(bf16[896,128]{1,0:T(8,128)(2,1)S(1)} %shard_map.96.own), channel_id=1, source_target_pairs={{0,96},{96,0},{32,64},{64,32},{1,97},{97,1},{33,65},{65,33},{2,98}... | collective-permute-start | bytes 688136 | tf_op jit(solution)/shard_map/ppermute | solution.py:26
  151.9 2.9 %collective-permute-start.13 = (bf16[896,128]{1,0:T(8,128)(2,1)S(1)}, bf16[896,128]{1,0:T(8,128)(2,1)S(1)}, u32[]{:S(2)}, u32[]{:S(2)}) collective-permute-start(bf16[896,128]{1,0:T(8,128)(2,1)S(1)} %shard_map.96.own), channel_id=1, source_target_pairs={{0,32},{32,0},{64,96},{96,64},{1,33},{33,1},{65,97},{97,65},{2,34}... | collective-permute-start | bytes 688136 | tf_op jit(solution)/shard_map/ppermute | solution.py:26
  154.8 0.0 collective-permute-done.4.came
  154.8 2.8 %shard_map.97 = (bf16[384,896]{1,0:T(8,128)(2,1)S(1)}, bf16[384,384]{1,0:T(8,128)(2,1)S(1)}, f32[384,512]{1,0:T(8,128)S(1)}) custom-call(s32[1]{0:T(128)} %bitcast.at, bf16[448,1792]{1,0:T(8,128)(2,1)S(1)} %shard_map.93.pack, bf16[448,1792]{1,0:T(8,128)(2,1)S(1)} %collective-permute-done.4.came, bf16[448,896]{1,0:T(8,128)(2,1)S(1)} %bitcast.14, ...), custom_call_target="tpu_custom_call" | custom-call | flops 1585446912 | bytes 5849092 | tf_op jit(solution)/shard_map/pallas_call | solution.py:44
  157.7 0.0 collective-permute-done.15.far
  157.7 4.4 %collective-permute-done.14.nxt = bf16[896,128]{1,0:T(8,128)(2,1)S(1)} collective-permute-done((bf16[896,128]{1,0:T(8,128)(2,1)S(1)}, bf16[896,128]{1,0:T(8,128)(2,1)S(1)}, u32[]{:S(2)}, u32[]{:S(2)}) %collective-permute-start.14) | collective-permute-done | bytes 229408 | tf_op jit(solution)/shard_map/ppermute | solution.py:26
  162.1 0.9 shard_map.98.most
  163.0 0.0 collective-permute-done.13.near
  163.0 1.4 shard_map.99
  (17 shorter events, 0.1 us)
Async XLA Ops:
  0.0 6.9 %copy-start = (bf16[1,448,896]{2,1,0:T(8,128)(2,1)S(1)}, bf16[1,448,896]{2,1,0:T(8,128)(2,1)}, u32[]{:S(2)}) copy-start(bf16[1,448,896]{2,1,0:T(8,128)(2,1)} %param.13) | copy-start | bytes 2408452
  0.0 12.3 %copy-start.2 = (bf16[1,128,896]{2,1,0:T(8,128)(2,1)S(1)}, bf16[1,128,896]{2,1,0:T(8,128)(2,1)}, u32[]{:S(2)}) copy-start(bf16[1,128,896]{2,1,0:T(8,128)(2,1)} %param.15) | copy-start | bytes 688132
  0.7 20.9 %copy-start.1 = (bf16[1,448,896]{2,1,0:T(8,128)(2,1)S(1)}, bf16[1,448,896]{2,1,0:T(8,128)(2,1)}, u32[]{:S(2)}) copy-start(bf16[1,448,896]{2,1,0:T(8,128)(2,1)} %param.12) | copy-start | bytes 2408452
  2.9 18.7 %collective-permute-start = (bf16[448,512]{1,0:T(8,128)(2,1)S(1)}, bf16[448,512]{1,0:T(8,128)(2,1)S(1)}, u32[]{:S(2)}, u32[]{:S(2)}) collective-permute-start(bf16[448,512]{1,0:T(8,128)(2,1)S(1)} %get-tuple-element.25.bot), channel_id=1, source_target_pairs={{0,32},{64,96},{1,33},{65,97},{2,34},{66,98},{3,35},{67,99},{4,36}... | collective-permute-start | bytes 1376264 | tf_op jit(solution)/shard_map/ppermute | solution.py:26
  7.0 15.7 %collective-permute-start.2 = (bf16[448,512]{1,0:T(8,128)(2,1)S(1)}, bf16[448,512]{1,0:T(8,128)(2,1)S(1)}, u32[]{:S(2)}, u32[]{:S(2)}) collective-permute-start(bf16[448,512]{1,0:T(8,128)(2,1)S(1)} %slice_select_fusion), channel_id=1, source_target_pairs={{0,32},{32,0},{64,96},{96,64},{1,33},{33,1},{65,97},{97,65},{2,34}... | collective-permute-start | bytes 1376264 | tf_op jit(solution)/shard_map/ppermute | solution.py:26
  8.9 23.6 %collective-permute-start.1 = (bf16[448,512]{1,0:T(8,128)(2,1)S(1)}, bf16[448,512]{1,0:T(8,128)(2,1)S(1)}, u32[]{:S(2)}, u32[]{:S(2)}) collective-permute-start(bf16[448,512]{1,0:T(8,128)(2,1)S(1)} %get-tuple-element.26.top), channel_id=1, source_target_pairs={{0,32},{32,0},{64,96},{96,64},{1,33},{33,1},{65,97},{97,65},{2,34}... | collective-permute-start | bytes 1376264 | tf_op jit(solution)/shard_map/ppermute | solution.py:26
  12.3 8.0 %collective-permute-start.10 = (bf16[128,896]{1,0:T(8,128)(2,1)S(1)}, bf16[128,896]{1,0:T(8,128)(2,1)S(1)}, u32[]{:S(2)}, u32[]{:S(2)}) collective-permute-start(bf16[128,896]{1,0:T(8,128)(2,1)S(1)} %bitcast.18), channel_id=1, source_target_pairs={{0,96},{96,0},{32,64},{64,32},{1,97},{97,1},{33,65},{65,33},{2,98}... | collective-permute-start | bytes 688136 | tf_op jit(solution)/shard_map/ppermute | solution.py:26
  20.3 29.3 %collective-permute-start.11 = (bf16[256,896]{1,0:T(8,128)(2,1)S(1)}, bf16[256,896]{1,0:T(8,128)(2,1)S(1)}, u32[]{:S(2)}, u32[]{:S(2)}) collective-permute-start(bf16[256,896]{1,0:T(8,128)(2,1)S(1)} %pad_maximum_fusion), channel_id=1, source_target_pairs={{32,0},{96,64},{33,1},{97,65},{34,2},{98,66},{35,3},{99,67},{36,4}... | collective-permute-start | bytes 1376264 | tf_op jit(solution)/shard_map/ppermute | solution.py:26
  32.5 5.3 %copy-start.5 = (bf16[1,224,896]{2,1,0:T(8,128)(2,1)S(1)}, bf16[1,224,896]{2,1,0:T(8,128)(2,1)}, u32[]{:S(2)}) copy-start(bf16[1,224,896]{2,1,0:T(8,128)(2,1)} %param.14) | copy-start | bytes 1204228
  33.7 14.1 %collective-permute-start.3 = (bf16[896,128]{1,0:T(8,128)(2,1)S(1)}, bf16[896,128]{1,0:T(8,128)(2,1)S(1)}, u32[]{:S(2)}, u32[]{:S(2)}) collective-permute-start(bf16[896,128]{1,0:T(8,128)(2,1)S(1)} %get-tuple-element.28), channel_id=1, source_target_pairs={{0,32},{32,0},{64,96},{96,64},{1,33},{33,1},{65,97},{97,65},{2,34}... | collective-permute-start | bytes 688136 | tf_op jit(solution)/shard_map/ppermute | solution.py:26
  37.8 14.2 %collective-permute-start.7 = (bf16[224,896]{1,0:T(8,128)(2,1)S(1)}, bf16[224,896]{1,0:T(8,128)(2,1)S(1)}, u32[]{:S(2)}, u32[]{:S(2)}) collective-permute-start(bf16[224,896]{1,0:T(8,128)(2,1)S(1)} %bitcast.24), channel_id=1, source_target_pairs={{0,32},{32,0},{64,96},{96,64},{1,33},{33,1},{65,97},{97,65},{2,34}... | collective-permute-start | bytes 1204232 | tf_op jit(solution)/shard_map/ppermute | solution.py:26
  39.7 20.6 %collective-permute-start.8 = (bf16[224,896]{1,0:T(8,128)(2,1)S(1)}, bf16[224,896]{1,0:T(8,128)(2,1)S(1)}, u32[]{:S(2)}, u32[]{:S(2)}) collective-permute-start(bf16[224,896]{1,0:T(8,128)(2,1)S(1)} %bitcast.25), channel_id=1, source_target_pairs={{0,96},{96,0},{32,64},{64,32},{1,97},{97,1},{33,65},{65,33},{2,98}... | collective-permute-start | bytes 1204232 | tf_op jit(solution)/shard_map/ppermute | solution.py:26
  47.6 25.0 %copy-start.4 = (bf16[512,512]{1,0:T(8,128)(2,1)S(1)}, bf16[512,512]{1,0:T(8,128)(2,1)}, u32[]{:S(2)}) copy-start(bf16[512,512]{1,0:T(8,128)(2,1)} %border.1) | copy-start | bytes 1572868
  47.7 107.1 %collective-permute-start.4 = (bf16[448,1792]{1,0:T(8,128)(2,1)S(1)}, bf16[448,1792]{1,0:T(8,128)(2,1)S(1)}, u32[]{:S(2)}, u32[]{:S(2)}) collective-permute-start(bf16[448,1792]{1,0:T(8,128)(2,1)S(1)} %shard_map.93.pack), channel_id=1, source_target_pairs={{0,32},{32,0},{64,96},{96,64},{1,33},{33,1},{65,97},{97,65},{2,34}... | collective-permute-start | bytes 4816904 | tf_op jit(solution)/shard_map/ppermute | solution.py:26
  49.7 22.9 %collective-permute-start.12 = (bf16[256,896]{1,0:T(8,128)(2,1)S(1)}, bf16[256,896]{1,0:T(8,128)(2,1)S(1)}, u32[]{:S(2)}, u32[]{:S(2)}) collective-permute-start(bf16[256,896]{1,0:T(8,128)(2,1)S(1)} %collective-permute-done.11.up), channel_id=1, source_target_pairs={{0,96},{64,32},{1,97},{65,33},{2,98},{66,34},{3,99},{67,35},{4,100... | collective-permute-start | bytes 1376264 | tf_op jit(solution)/shard_map/ppermute | solution.py:26
  52.0 20.5 %collective-permute-start.9 = (bf16[224,896]{1,0:T(8,128)(2,1)S(1)}, bf16[224,896]{1,0:T(8,128)(2,1)S(1)}, u32[]{:S(2)}, u32[]{:S(2)}) collective-permute-start(bf16[224,896]{1,0:T(8,128)(2,1)S(1)} %collective-permute-done.7.i1), channel_id=1, source_target_pairs={{0,96},{96,0},{32,64},{64,32},{1,97},{97,1},{33,65},{65,33},{2,98}... | collective-permute-start | bytes 1204232 | tf_op jit(solution)/shard_map/ppermute | solution.py:26
  58.4 19.1 %collective-permute-start.5 = (bf16[896,128]{1,0:T(8,128)(2,1)S(1)}, bf16[896,128]{1,0:T(8,128)(2,1)S(1)}, u32[]{:S(2)}, u32[]{:S(2)}) collective-permute-start(bf16[896,128]{1,0:T(8,128)(2,1)S(1)} %get-tuple-element.32), channel_id=1, source_target_pairs={{0,96},{96,0},{32,64},{64,32},{1,97},{97,1},{33,65},{65,33},{2,98}... | collective-permute-start | bytes 688136 | tf_op jit(solution)/shard_map/ppermute | solution.py:26
  60.3 35.2 %collective-permute-start.6 = (bf16[896,128]{1,0:T(8,128)(2,1)S(1)}, bf16[896,128]{1,0:T(8,128)(2,1)S(1)}, u32[]{:S(2)}, u32[]{:S(2)}) collective-permute-start(bf16[896,128]{1,0:T(8,128)(2,1)S(1)} %get-tuple-element.33), channel_id=1, source_target_pairs={{0,64},{64,0},{32,96},{96,32},{1,65},{65,1},{33,97},{97,33},{2,66}... | collective-permute-start | bytes 688136 | tf_op jit(solution)/shard_map/ppermute | solution.py:26
  145.5 9.3 %copy-start.3 = (bf16[1,1,896,384]{3,2,1,0:T(8,128)(2,1)S(1)}, bf16[1,1,896,384]{3,2,1,0:T(8,128)(2,1)}, u32[]{:S(2)}) copy-start(bf16[1,1,896,384]{3,2,1,0:T(8,128)(2,1)} %param.11) | copy-start | bytes 2064388
  145.5 9.3 %copy-start.6 = (bf16[1,1,384,512]{3,2,1,0:T(8,128)(2,1)S(1)}, bf16[1,1,384,512]{3,2,1,0:T(8,128)(2,1)}, u32[]{:S(2)}) copy-start(bf16[1,1,384,512]{3,2,1,0:T(8,128)(2,1)} %param.9) | copy-start | bytes 1179652
  145.5 9.3 %copy-start.7 = (bf16[1,1,384,384]{3,2,1,0:T(8,128)(2,1)S(1)}, bf16[1,1,384,384]{3,2,1,0:T(8,128)(2,1)}, u32[]{:S(2)}) copy-start(bf16[1,1,384,384]{3,2,1,0:T(8,128)(2,1)} %param.10) | copy-start | bytes 884740
  146.2 11.5 %collective-permute-start.15 = (bf16[896,128]{1,0:T(8,128)(2,1)S(1)}, bf16[896,128]{1,0:T(8,128)(2,1)S(1)}, u32[]{:S(2)}, u32[]{:S(2)}) collective-permute-start(bf16[896,128]{1,0:T(8,128)(2,1)S(1)} %shard_map.96.own), channel_id=1, source_target_pairs={{0,64},{64,0},{32,96},{96,32},{1,65},{65,1},{33,97},{97,33},{2,66}... | collective-permute-start | bytes 688136 | tf_op jit(solution)/shard_map/ppermute | solution.py:26
  148.7 13.4 %collective-permute-start.14 = (bf16[896,128]{1,0:T(8,128)(2,1)S(1)}, bf16[896,128]{1,0:T(8,128)(2,1)S(1)}, u32[]{:S(2)}, u32[]{:S(2)}) collective-permute-start(bf16[896,128]{1,0:T(8,128)(2,1)S(1)} %shard_map.96.own), channel_id=1, source_target_pairs={{0,96},{96,0},{32,64},{64,32},{1,97},{97,1},{33,65},{65,33},{2,98}... | collective-permute-start | bytes 688136 | tf_op jit(solution)/shard_map/ppermute | solution.py:26
  151.9 11.2 %collective-permute-start.13 = (bf16[896,128]{1,0:T(8,128)(2,1)S(1)}, bf16[896,128]{1,0:T(8,128)(2,1)S(1)}, u32[]{:S(2)}, u32[]{:S(2)}) collective-permute-start(bf16[896,128]{1,0:T(8,128)(2,1)S(1)} %shard_map.96.own), channel_id=1, source_target_pairs={{0,32},{32,0},{64,96},{96,64},{1,33},{33,1},{65,97},{97,65},{2,34}... | collective-permute-start | bytes 688136 | tf_op jit(solution)/shard_map/ppermute | solution.py:26

commit v9 on v8

--- a/solution.py
+++ b/solution.py
@@ -210,26 +210,54 @@
     inv_t[...] = leaf_inv[...].T
 
 
-def most_kernel(at, fold_t, inv_t, rest, own, nxt, far, out, back, kept):
+def most_kernel(at, fold_t, inv_t, rest, own, nxt, far, out, back, kept, done, sems):
     x = at[0]
     share = own.shape[1]
-    for place, (who, ref) in enumerate(zip((x, 3 - x, x ^ 2), (own, nxt, far))):
+    owners = (x, 3 - x, x ^ 2)
+    for place, (who, ref) in enumerate(zip(owners, (own, nxt, far))):
         spot = slice(place * share, (place + 1) * share)
         back[:, spot] = ref[...]
         kept[:, spot] = rest[:, pl.ds(pl.multiple_of(who * share, LANES), share)]
     diff = (kept[...] + mul(fold_t[...], back[...])).astype(BF)
-    out[...] = mul(inv_t[...], diff).astype(BF)
-
-
-def last_kernel(at, fold_t, inv_t, rest, near, most, out):
-    x = at[0]
+    done[...] = mul(inv_t[...], diff).astype(BF)
+    copies = [
+        pltpu.make_async_copy(
+            done.at[:, place * share : (place + 1) * share],
+            out.at[:, pl.ds(pl.multiple_of(who * share, LANES), share)],
+            sems.at[place],
+        )
+        for place, who in enumerate(owners)
+    ]
+    for copy in copies:
+        copy.start()
+    for copy in copies:
+        copy.wait()
+
+
+def last_kernel(at, fold_t, inv_t, rest, near, most, out, done, sem):
     share = near.shape[1]
-    for place, who in enumerate((x, 3 - x, x ^ 2)):
-        spot = slice(place * share, (place + 1) * share)
-        out[:, pl.ds(pl.multiple_of(who * share, LANES), share)] = most[:, spot]
-    cols = pl.ds(pl.multiple_of((x ^ 1) * share, LANES), share)
+    cols = pl.ds(pl.multiple_of((at[0] ^ 1) * share, LANES), share)
     diff = (rest[:, cols] + mul(fold_t[...], near[...])).astype(BF)
-    out[:, cols] = mul(inv_t[...], diff).astype(BF)
+    done[...] = mul(inv_t[...], diff).astype(BF)
+    copy = pltpu.make_async_copy(done, out.at[:, cols], sem)
+    copy.start()
+    copy.wait()
+
+
+def solve_call(kernel, shape, scratch, aliases, *args):
+    vmem, hbm = pl.BlockSpec(memory_space=pltpu.VMEM), pl.BlockSpec(memory_space=pltpu.HBM)
+    specs = [pl.BlockSpec(memory_space=pltpu.SMEM)] + [vmem] * (len(args) - 1)
+    for operand in aliases:
+        specs[operand] = hbm
+    return pl.pallas_call(
+        kernel,
+        out_shape=pltpu.HBM(shape, BF),
+        in_specs=specs,
+        out_specs=hbm,
+        scratch_shapes=scratch,
+        input_output_aliases=aliases,
+        compiler_params=pltpu.CompilerParams(vmem_limit_bytes=16 << 20),
+    )(*args)
 
 
 def per_device(
@@ -364,10 +392,17 @@
         leaf_inv,
         flops=2 * sep * leaf * (2 * sep + ports),
     )
-    (most,) = call(
+    kept = ports - share
+    most = solve_call(
         most_kernel,
-        [((leaf, ports - share), BF)],
-        [((sep, ports - share), BF), ((leaf, ports - share), F32)],
+        (leaf, ports),
+        [
+            pltpu.VMEM((sep, kept), BF),
+            pltpu.VMEM((leaf, kept), F32),
+            pltpu.VMEM((leaf, kept), BF),
+            pltpu.SemaphoreType.DMA((3,)),
+        ],
+        {},
         at,
         fold_t,
         inv_t,
@@ -375,19 +410,18 @@
         back_two,
         back_next,
         back_far,
-        flops=2 * leaf * (ports - share) * (sep + leaf),
-    )
-    (out,) = call(
+    )
+    out = solve_call(
         last_kernel,
-        [((leaf, ports), BF)],
-        [],
+        (leaf, ports),
+        [pltpu.VMEM((leaf, share), BF), pltpu.SemaphoreType.DMA(())],
+        {5: 0},
         at,
         fold_t,
         inv_t,
         rest,
         back_near,
         most,
-        flops=2 * leaf * share * (sep + leaf),
     )
     return out[None, None]
 

time: 165 us -> 166 us (level)
    pallas_call x0 -> x2, Pallas kernels: none -> 2.99 us  [solve_call(): pl.pallas_call(kernel, out_shape=pltpu.HBM(shape, BF), in_specs=specs, ou...]
    pallas_call x9 -> x7, Pallas kernels: 10.8 us -> 8.43 us  [call(): pl.pallas_call(kernel, out_shape=[jax.ShapeDtypeStruct(s, d) for s, d in...]
where the time goes in v9:
time: 166 us; the launch traced here: 165 us
  starting transfers between devices  52.2 us (31%)
  waiting for transfers between devices  48.9 us (29%)
  blocking collectives  48.9 us (29%)
  Pallas kernels  13.6 us (8%)
    ppermute x16, starting transfers between devices, send(): return lax.ppermute(x, 'x', pairs)  52.2 us
    all_to_all x2, blocking collectives, to_group(): return lax.all_to_all(tiles, GROUP, split_axis=0, concat_axis=0, tiled=True)  48.9 us
    ppermute x16, waiting for transfers between devices, send(): return lax.ppermute(x, 'x', pairs)  48.9 us
    pallas_call x7, Pallas kernels, call(): pl.pallas_call(kernel, out_shape=[jax.ShapeDtypeStruct(s, d) for s, d in...  8.43 us
  transfers between devices with their start and end apart: 16, of which 7 were waited for; matrix products, arithmetic and copies ran while one was open for 0% of the time, Pallas kernels for 6%

profile of v9, /device:TPU:1, one launch (start us, length us, event | category | flops | bytes accessed | tf_op | source)
XLA Modules:
  0.0 165.2 jit_solution(4602215114309086188)
XLA Ops:
  0.8 2.2 %k_leaf.1 = (bf16[448,512]{1,0:T(8,128)(2,1)S(1)}, bf16[448,512]{1,0:T(8,128)(2,1)S(1)}) custom-call(s32[1]{0:T(128)S(6)} %copy.12.rows, bf16[384,512]{1,0:T(8,128)(2,1)} %bitcast.27, bf16[384,384]{1,0:T(8,128)(2,1)} %bitcast.29, bf16[896,384]{1,0:T(8,128)(2,1)} %bitcast.21), custom_call_target="tpu_custom_call" | custom-call | tf_op jit(solution)/shard_map/k_leaf/pallas_call | solution.py:91
  2.9 4.0 %collective-permute-start = (bf16[448,512]{1,0:T(8,128)(2,1)S(1)}, bf16[448,512]{1,0:T(8,128)(2,1)S(1)}, u32[]{:S(2)}, u32[]{:S(2)}) collective-permute-start(bf16[448,512]{1,0:T(8,128)(2,1)S(1)} %get-tuple-element.25.bot), channel_id=1, source_target_pairs={{0,32},{64,96},{1,33},{65,97},{2,34},{66,98},{3,35},{67,99},{4,36}... | collective-permute-start | bytes 1376264 | tf_op jit(solution)/shard_map/ppermute | solution.py:26
  6.9 0.1 slice_select_fusion
  7.0 1.9 %collective-permute-start.2 = (bf16[448,512]{1,0:T(8,128)(2,1)S(1)}, bf16[448,512]{1,0:T(8,128)(2,1)S(1)}, u32[]{:S(2)}, u32[]{:S(2)}) collective-permute-start(bf16[448,512]{1,0:T(8,128)(2,1)S(1)} %slice_select_fusion), channel_id=1, source_target_pairs={{0,32},{32,0},{64,96},{96,64},{1,33},{33,1},{65,97},{97,65},{2,34}... | collective-permute-start | bytes 1376264 | tf_op jit(solution)/shard_map/ppermute | solution.py:26
  8.9 3.4 %collective-permute-start.1 = (bf16[448,512]{1,0:T(8,128)(2,1)S(1)}, bf16[448,512]{1,0:T(8,128)(2,1)S(1)}, u32[]{:S(2)}, u32[]{:S(2)}) collective-permute-start(bf16[448,512]{1,0:T(8,128)(2,1)S(1)} %get-tuple-element.26.top), channel_id=1, source_target_pairs={{0,32},{32,0},{64,96},{96,64},{1,33},{33,1},{65,97},{97,65},{2,34}... | collective-permute-start | bytes 1376264 | tf_op jit(solution)/shard_map/ppermute | solution.py:26
  12.3 3.2 %collective-permute-start.10 = (bf16[128,896]{1,0:T(8,128)(2,1)S(1)}, bf16[128,896]{1,0:T(8,128)(2,1)S(1)}, u32[]{:S(2)}, u32[]{:S(2)}) collective-permute-start(bf16[128,896]{1,0:T(8,128)(2,1)S(1)} %bitcast.18), channel_id=1, source_target_pairs={{0,96},{96,0},{32,64},{64,32},{1,97},{97,1},{33,65},{65,33},{2,98}... | collective-permute-start | bytes 688136 | tf_op jit(solution)/shard_map/ppermute | solution.py:26
  15.5 4.8 %collective-permute-done.10.nxt = bf16[128,896]{1,0:T(8,128)(2,1)S(1)} collective-permute-done((bf16[128,896]{1,0:T(8,128)(2,1)S(1)}, bf16[128,896]{1,0:T(8,128)(2,1)S(1)}, u32[]{:S(2)}, u32[]{:S(2)}) %collective-permute-start.10) | collective-permute-done | bytes 229408 | tf_op jit(solution)/shard_map/ppermute | solution.py:26
  20.3 1.3 collective-permute-start.11
  21.6 0.0 collective-permute-done.came
  21.7 0.4 shard_map.91.part
  22.1 0.6 collective-permute-done.2.came_coup
  22.7 9.8 %collective-permute-done.1.came_top = bf16[448,512]{1,0:T(8,128)(2,1)S(1)} collective-permute-done((bf16[448,512]{1,0:T(8,128)(2,1)S(1)}, bf16[448,512]{1,0:T(8,128)(2,1)S(1)}, u32[]{:S(2)}, u32[]{:S(2)}) %collective-permute-start.1) | collective-permute-done | bytes 458784 | tf_op jit(solution)/shard_map/ppermute | solution.py:26
  32.5 1.2 shard_map.92
  33.7 4.1 %collective-permute-start.3 = (bf16[896,128]{1,0:T(8,128)(2,1)S(1)}, bf16[896,128]{1,0:T(8,128)(2,1)S(1)}, u32[]{:S(2)}, u32[]{:S(2)}) collective-permute-start(bf16[896,128]{1,0:T(8,128)(2,1)S(1)} %get-tuple-element.28), channel_id=1, source_target_pairs={{0,32},{32,0},{64,96},{96,64},{1,33},{33,1},{65,97},{97,65},{2,34}... | collective-permute-start | bytes 688136 | tf_op jit(solution)/shard_map/ppermute | solution.py:26
  37.8 1.9 %collective-permute-start.7 = (bf16[224,896]{1,0:T(8,128)(2,1)S(1)}, bf16[224,896]{1,0:T(8,128)(2,1)S(1)}, u32[]{:S(2)}, u32[]{:S(2)}) collective-permute-start(bf16[224,896]{1,0:T(8,128)(2,1)S(1)} %bitcast.24), channel_id=1, source_target_pairs={{0,32},{32,0},{64,96},{96,64},{1,33},{33,1},{65,97},{97,65},{2,34}... | collective-permute-start | bytes 1204232 | tf_op jit(solution)/shard_map/ppermute | solution.py:26
  39.7 7.9 %collective-permute-start.8 = (bf16[224,896]{1,0:T(8,128)(2,1)S(1)}, bf16[224,896]{1,0:T(8,128)(2,1)S(1)}, u32[]{:S(2)}, u32[]{:S(2)}) collective-permute-start(bf16[224,896]{1,0:T(8,128)(2,1)S(1)} %bitcast.25), channel_id=1, source_target_pairs={{0,96},{96,0},{32,64},{64,32},{1,97},{97,1},{33,65},{65,33},{2,98}... | collective-permute-start | bytes 1204232 | tf_op jit(solution)/shard_map/ppermute | solution.py:26
  47.6 0.0 copy-start.4
  47.6 0.1 shard_map.93.pack
  47.7 0.0 collective-permute-done.3.near
  47.7 1.9 %collective-permute-start.4 = (bf16[448,1792]{1,0:T(8,128)(2,1)S(1)}, bf16[448,1792]{1,0:T(8,128)(2,1)S(1)}, u32[]{:S(2)}, u32[]{:S(2)}) collective-permute-start(bf16[448,1792]{1,0:T(8,128)(2,1)S(1)} %shard_map.93.pack), channel_id=1, source_target_pairs={{0,32},{32,0},{64,96},{96,64},{1,33},{33,1},{65,97},{97,65},{2,34}... | collective-permute-start | bytes 4816904 | tf_op jit(solution)/shard_map/ppermute | solution.py:26
  49.7 0.0 collective-permute-done.11.up
  49.7 2.3 %collective-permute-start.12 = (bf16[256,896]{1,0:T(8,128)(2,1)S(1)}, bf16[256,896]{1,0:T(8,128)(2,1)S(1)}, u32[]{:S(2)}, u32[]{:S(2)}) collective-permute-start(bf16[256,896]{1,0:T(8,128)(2,1)S(1)} %collective-permute-done.11.up), channel_id=1, source_target_pairs={{0,96},{64,32},{1,97},{65,33},{2,98},{66,34},{3,99},{67,35},{4,100... | collective-permute-start | bytes 1376264 | tf_op jit(solution)/shard_map/ppermute | solution.py:26
  52.0 0.0 collective-permute-done.7.i1
  52.0 6.3 %collective-permute-start.9 = (bf16[224,896]{1,0:T(8,128)(2,1)S(1)}, bf16[224,896]{1,0:T(8,128)(2,1)S(1)}, u32[]{:S(2)}, u32[]{:S(2)}) collective-permute-start(bf16[224,896]{1,0:T(8,128)(2,1)S(1)} %collective-permute-done.7.i1), channel_id=1, source_target_pairs={{0,96},{96,0},{32,64},{64,32},{1,97},{97,1},{33,65},{65,33},{2,98}... | collective-permute-start | bytes 1204232 | tf_op jit(solution)/shard_map/ppermute | solution.py:26
  58.4 1.9 %collective-permute-start.5 = (bf16[896,128]{1,0:T(8,128)(2,1)S(1)}, bf16[896,128]{1,0:T(8,128)(2,1)S(1)}, u32[]{:S(2)}, u32[]{:S(2)}) collective-permute-start(bf16[896,128]{1,0:T(8,128)(2,1)S(1)} %get-tuple-element.32), channel_id=1, source_target_pairs={{0,96},{96,0},{32,64},{64,32},{1,97},{97,1},{33,65},{65,33},{2,98}... | collective-permute-start | bytes 688136 | tf_op jit(solution)/shard_map/ppermute | solution.py:26
  60.3 0.0 collective-permute-done.8.i2
  60.3 3.6 %collective-permute-start.6 = (bf16[896,128]{1,0:T(8,128)(2,1)S(1)}, bf16[896,128]{1,0:T(8,128)(2,1)S(1)}, u32[]{:S(2)}, u32[]{:S(2)}) collective-permute-start(bf16[896,128]{1,0:T(8,128)(2,1)S(1)} %get-tuple-element.33), channel_id=1, source_target_pairs={{0,64},{64,0},{32,96},{96,32},{1,65},{65,1},{33,97},{97,33},{2,66}... | collective-permute-start | bytes 688136 | tf_op jit(solution)/shard_map/ppermute | solution.py:26
  63.9 8.7 %collective-permute-done.9.i3 = bf16[224,896]{1,0:T(8,128)(2,1)S(1)} collective-permute-done((bf16[224,896]{1,0:T(8,128)(2,1)S(1)}, bf16[224,896]{1,0:T(8,128)(2,1)S(1)}, u32[]{:S(2)}, u32[]{:S(2)}) %collective-permute-start.9) | collective-permute-done | bytes 401440 | tf_op jit(solution)/shard_map/ppermute | solution.py:26
  72.6 0.0 collective-permute-done.12.down
  72.6 0.0 copy-done.4
  72.6 2.3 %shard_map.94 = (bf16[896,896]{1,0:T(8,128)(2,1)S(1)}, bf16[512,896]{1,0:T(8,128)(2,1)S(1)}, bf16[896,512]{1,0:T(8,128)(2,1)S(1)}) custom-call(s32[1]{0:T(128)} %bitcast.at, s32[1]{0:T(128)S(6)} %copy.12.rows, bf16[224,896]{1,0:T(8,128)(2,1)S(1)} %bitcast.26, bf16[224,896]{1,0:T(8,128)(2,1)S(1)} %collective-permute-done.7.i1, ...), custom_call_target="tpu_custom_call" | custom-call | bytes 3506184 | tf_op jit(solution)/shard_map/pallas_call | solution.py:44
  74.9 2.6 %collective-permute-done.5.nxt = bf16[896,128]{1,0:T(8,128)(2,1)S(1)} collective-permute-done((bf16[896,128]{1,0:T(8,128)(2,1)S(1)}, bf16[896,128]{1,0:T(8,128)(2,1)S(1)}, u32[]{:S(2)}, u32[]{:S(2)}) %collective-permute-start.5) | collective-permute-done | bytes 229408 | tf_op jit(solution)/shard_map/ppermute | solution.py:26
  77.5 18.1 %collective-permute-done.6.far = bf16[896,128]{1,0:T(8,128)(2,1)S(1)} collective-permute-done((bf16[896,128]{1,0:T(8,128)(2,1)S(1)}, bf16[896,128]{1,0:T(8,128)(2,1)S(1)}, u32[]{:S(2)}, u32[]{:S(2)}) %collective-permute-start.6) | collective-permute-done | bytes 229408 | tf_op jit(solution)/shard_map/ppermute | solution.py:26
  95.5 0.8 shard_map.95
  96.4 31.4 %all_to_all.10 = bf16[128,4,128]{2,1,0:T(4,128)(2,1)S(1)} all-to-all(bf16[128,4,128]{2,1,0:T(4,128)(2,1)S(1)} %bitcast.31), channel_id=1, replica_groups=mesh['zl'=4,'x'=4,'y'=8,'zh'=2,'c'=2] {'zl','y','zh','c'}, dimensions={0} | all-to-all | bytes 262144 | tf_op jit(solution)/shard_map/all_to_all | solution.py:30
  127.8 0.1 convert_reduce_fusion
  128.0 17.5 %all_to_all.11 = bf16[128,4,128]{2,1,0:T(4,128)(2,1)S(1)} all-to-all(bf16[128,4,128]{2,1,0:T(4,128)(2,1)S(1)} %broadcast_in_dim.10), channel_id=1, replica_groups=mesh['zl'=4,'x'=4,'y'=8,'zh'=2,'c'=2] {'zl','y','zh','c'}, dimensions={0} | all-to-all | bytes 262144 | tf_op jit(solution)/shard_map/all_to_all | solution.py:30
  145.5 0.7 shard_map.96.own
  146.2 2.4 %collective-permute-start.15 = (bf16[896,128]{1,0:T(8,128)(2,1)S(1)}, bf16[896,128]{1,0:T(8,128)(2,1)S(1)}, u32[]{:S(2)}, u32[]{:S(2)}) collective-permute-start(bf16[896,128]{1,0:T(8,128)(2,1)S(1)} %shard_map.96.own), channel_id=1, source_target_pairs={{0,64},{64,0},{32,96},{96,32},{1,65},{65,1},{33,97},{97,33},{2,66}... | collective-permute-start | bytes 688136 | tf_op jit(solution)/shard_map/ppermute | solution.py:26
  148.7 3.2 %collective-permute-start.14 = (bf16[896,128]{1,0:T(8,128)(2,1)S(1)}, bf16[896,128]{1,0:T(8,128)(2,1)S(1)}, u32[]{:S(2)}, u32[]{:S(2)}) collective-permute-start(bf16[896,128]{1,0:T(8,128)(2,1)S(1)} %shard_map.96.own), channel_id=1, source_target_pairs={{0,96},{96,0},{32,64},{64,32},{1,97},{97,1},{33,65},{65,33},{2,98}... | collective-permute-start | bytes 688136 | tf_op jit(solution)/shard_map/ppermute | solution.py:26
  151.9 2.9 %collective-permute-start.13 = (bf16[896,128]{1,0:T(8,128)(2,1)S(1)}, bf16[896,128]{1,0:T(8,128)(2,1)S(1)}, u32[]{:S(2)}, u32[]{:S(2)}) collective-permute-start(bf16[896,128]{1,0:T(8,128)(2,1)S(1)} %shard_map.96.own), channel_id=1, source_target_pairs={{0,32},{32,0},{64,96},{96,64},{1,33},{33,1},{65,97},{97,65},{2,34}... | collective-permute-start | bytes 688136 | tf_op jit(solution)/shard_map/ppermute | solution.py:26
  154.8 0.0 collective-permute-done.4.came
  154.8 2.8 %shard_map.97 = (bf16[384,896]{1,0:T(8,128)(2,1)S(1)}, bf16[384,384]{1,0:T(8,128)(2,1)S(1)}, f32[384,512]{1,0:T(8,128)S(1)}) custom-call(s32[1]{0:T(128)} %bitcast.at, bf16[448,1792]{1,0:T(8,128)(2,1)S(1)} %shard_map.93.pack, bf16[448,1792]{1,0:T(8,128)(2,1)S(1)} %collective-permute-done.4.came, bf16[448,896]{1,0:T(8,128)(2,1)S(1)} %bitcast.14, ...), custom_call_target="tpu_custom_call" | custom-call | flops 1585446912 | bytes 5849092 | tf_op jit(solution)/shard_map/pallas_call | solution.py:44
  157.7 0.0 collective-permute-done.15.far
  157.7 4.4 %collective-permute-done.14.nxt = bf16[896,128]{1,0:T(8,128)(2,1)S(1)} collective-permute-done((bf16[896,128]{1,0:T(8,128)(2,1)S(1)}, bf16[896,128]{1,0:T(8,128)(2,1)S(1)}, u32[]{:S(2)}, u32[]{:S(2)}) %collective-permute-start.14) | collective-permute-done | bytes 229408 | tf_op jit(solution)/shard_map/ppermute | solution.py:26
  162.1 1.7 %shard_map.98.most = bf16[384,512]{1,0:T(8,128)(2,1)} custom-call(s32[1]{0:T(128)} %bitcast.at, bf16[384,896]{1,0:T(8,128)(2,1)S(1)} %get-tuple-element.41.fold_t, bf16[384,384]{1,0:T(8,128)(2,1)S(1)} %get-tuple-element.42.inv_t, f32[384,512]{1,0:T(8,128)S(1)} %get-tuple-element.43.rest, bf16[896,128]{1,0:T(8,128)(2,1)S(1)} %shard_map.96.own, ...), custom_call_target="tpu_custom_call" | custom-call | tf_op jit(solution)/shard_map/pallas_call | solution.py:252
  163.7 0.0 collective-permute-done.13.near
  163.8 1.3 shard_map.99
  (17 shorter events, 0.1 us)
Async XLA Ops:
  0.0 6.9 %copy-start = (bf16[1,448,896]{2,1,0:T(8,128)(2,1)S(1)}, bf16[1,448,896]{2,1,0:T(8,128)(2,1)}, u32[]{:S(2)}) copy-start(bf16[1,448,896]{2,1,0:T(8,128)(2,1)} %param.13) | copy-start | bytes 2408452
  0.0 12.3 %copy-start.2 = (bf16[1,128,896]{2,1,0:T(8,128)(2,1)S(1)}, bf16[1,128,896]{2,1,0:T(8,128)(2,1)}, u32[]{:S(2)}) copy-start(bf16[1,128,896]{2,1,0:T(8,128)(2,1)} %param.15) | copy-start | bytes 688132
  0.7 20.9 %copy-start.1 = (bf16[1,448,896]{2,1,0:T(8,128)(2,1)S(1)}, bf16[1,448,896]{2,1,0:T(8,128)(2,1)}, u32[]{:S(2)}) copy-start(bf16[1,448,896]{2,1,0:T(8,128)(2,1)} %param.12) | copy-start | bytes 2408452
  2.9 18.7 %collective-permute-start = (bf16[448,512]{1,0:T(8,128)(2,1)S(1)}, bf16[448,512]{1,0:T(8,128)(2,1)S(1)}, u32[]{:S(2)}, u32[]{:S(2)}) collective-permute-start(bf16[448,512]{1,0:T(8,128)(2,1)S(1)} %get-tuple-element.25.bot), channel_id=1, source_target_pairs={{0,32},{64,96},{1,33},{65,97},{2,34},{66,98},{3,35},{67,99},{4,36}... | collective-permute-start | bytes 1376264 | tf_op jit(solution)/shard_map/ppermute | solution.py:26
  7.0 15.7 %collective-permute-start.2 = (bf16[448,512]{1,0:T(8,128)(2,1)S(1)}, bf16[448,512]{1,0:T(8,128)(2,1)S(1)}, u32[]{:S(2)}, u32[]{:S(2)}) collective-permute-start(bf16[448,512]{1,0:T(8,128)(2,1)S(1)} %slice_select_fusion), channel_id=1, source_target_pairs={{0,32},{32,0},{64,96},{96,64},{1,33},{33,1},{65,97},{97,65},{2,34}... | collective-permute-start | bytes 1376264 | tf_op jit(solution)/shard_map/ppermute | solution.py:26
  8.9 23.6 %collective-permute-start.1 = (bf16[448,512]{1,0:T(8,128)(2,1)S(1)}, bf16[448,512]{1,0:T(8,128)(2,1)S(1)}, u32[]{:S(2)}, u32[]{:S(2)}) collective-permute-start(bf16[448,512]{1,0:T(8,128)(2,1)S(1)} %get-tuple-element.26.top), channel_id=1, source_target_pairs={{0,32},{32,0},{64,96},{96,64},{1,33},{33,1},{65,97},{97,65},{2,34}... | collective-permute-start | bytes 1376264 | tf_op jit(solution)/shard_map/ppermute | solution.py:26
  12.3 8.0 %collective-permute-start.10 = (bf16[128,896]{1,0:T(8,128)(2,1)S(1)}, bf16[128,896]{1,0:T(8,128)(2,1)S(1)}, u32[]{:S(2)}, u32[]{:S(2)}) collective-permute-start(bf16[128,896]{1,0:T(8,128)(2,1)S(1)} %bitcast.18), channel_id=1, source_target_pairs={{0,96},{96,0},{32,64},{64,32},{1,97},{97,1},{33,65},{65,33},{2,98}... | collective-permute-start | bytes 688136 | tf_op jit(solution)/shard_map/ppermute | solution.py:26
  20.3 29.3 %collective-permute-start.11 = (bf16[256,896]{1,0:T(8,128)(2,1)S(1)}, bf16[256,896]{1,0:T(8,128)(2,1)S(1)}, u32[]{:S(2)}, u32[]{:S(2)}) collective-permute-start(bf16[256,896]{1,0:T(8,128)(2,1)S(1)} %pad_maximum_fusion), channel_id=1, source_target_pairs={{32,0},{96,64},{33,1},{97,65},{34,2},{98,66},{35,3},{99,67},{36,4}... | collective-permute-start | bytes 1376264 | tf_op jit(solution)/shard_map/ppermute | solution.py:26
  32.5 5.3 %copy-start.5 = (bf16[1,224,896]{2,1,0:T(8,128)(2,1)S(1)}, bf16[1,224,896]{2,1,0:T(8,128)(2,1)}, u32[]{:S(2)}) copy-start(bf16[1,224,896]{2,1,0:T(8,128)(2,1)} %param.14) | copy-start | bytes 1204228
  33.7 14.1 %collective-permute-start.3 = (bf16[896,128]{1,0:T(8,128)(2,1)S(1)}, bf16[896,128]{1,0:T(8,128)(2,1)S(1)}, u32[]{:S(2)}, u32[]{:S(2)}) collective-permute-start(bf16[896,128]{1,0:T(8,128)(2,1)S(1)} %get-tuple-element.28), channel_id=1, source_target_pairs={{0,32},{32,0},{64,96},{96,64},{1,33},{33,1},{65,97},{97,65},{2,34}... | collective-permute-start | bytes 688136 | tf_op jit(solution)/shard_map/ppermute | solution.py:26
  37.8 14.2 %collective-permute-start.7 = (bf16[224,896]{1,0:T(8,128)(2,1)S(1)}, bf16[224,896]{1,0:T(8,128)(2,1)S(1)}, u32[]{:S(2)}, u32[]{:S(2)}) collective-permute-start(bf16[224,896]{1,0:T(8,128)(2,1)S(1)} %bitcast.24), channel_id=1, source_target_pairs={{0,32},{32,0},{64,96},{96,64},{1,33},{33,1},{65,97},{97,65},{2,34}... | collective-permute-start | bytes 1204232 | tf_op jit(solution)/shard_map/ppermute | solution.py:26
  39.7 20.6 %collective-permute-start.8 = (bf16[224,896]{1,0:T(8,128)(2,1)S(1)}, bf16[224,896]{1,0:T(8,128)(2,1)S(1)}, u32[]{:S(2)}, u32[]{:S(2)}) collective-permute-start(bf16[224,896]{1,0:T(8,128)(2,1)S(1)} %bitcast.25), channel_id=1, source_target_pairs={{0,96},{96,0},{32,64},{64,32},{1,97},{97,1},{33,65},{65,33},{2,98}... | collective-permute-start | bytes 1204232 | tf_op jit(solution)/shard_map/ppermute | solution.py:26
  47.6 25.0 %copy-start.4 = (bf16[512,512]{1,0:T(8,128)(2,1)S(1)}, bf16[512,512]{1,0:T(8,128)(2,1)}, u32[]{:S(2)}) copy-start(bf16[512,512]{1,0:T(8,128)(2,1)} %border.1) | copy-start | bytes 1572868
  47.7 107.1 %collective-permute-start.4 = (bf16[448,1792]{1,0:T(8,128)(2,1)S(1)}, bf16[448,1792]{1,0:T(8,128)(2,1)S(1)}, u32[]{:S(2)}, u32[]{:S(2)}) collective-permute-start(bf16[448,1792]{1,0:T(8,128)(2,1)S(1)} %shard_map.93.pack), channel_id=1, source_target_pairs={{0,32},{32,0},{64,96},{96,64},{1,33},{33,1},{65,97},{97,65},{2,34}... | collective-permute-start | bytes 4816904 | tf_op jit(solution)/shard_map/ppermute | solution.py:26
  49.7 22.9 %collective-permute-start.12 = (bf16[256,896]{1,0:T(8,128)(2,1)S(1)}, bf16[256,896]{1,0:T(8,128)(2,1)S(1)}, u32[]{:S(2)}, u32[]{:S(2)}) collective-permute-start(bf16[256,896]{1,0:T(8,128)(2,1)S(1)} %collective-permute-done.11.up), channel_id=1, source_target_pairs={{0,96},{64,32},{1,97},{65,33},{2,98},{66,34},{3,99},{67,35},{4,100... | collective-permute-start | bytes 1376264 | tf_op jit(solution)/shard_map/ppermute | solution.py:26
  52.0 20.5 %collective-permute-start.9 = (bf16[224,896]{1,0:T(8,128)(2,1)S(1)}, bf16[224,896]{1,0:T(8,128)(2,1)S(1)}, u32[]{:S(2)}, u32[]{:S(2)}) collective-permute-start(bf16[224,896]{1,0:T(8,128)(2,1)S(1)} %collective-permute-done.7.i1), channel_id=1, source_target_pairs={{0,96},{96,0},{32,64},{64,32},{1,97},{97,1},{33,65},{65,33},{2,98}... | collective-permute-start | bytes 1204232 | tf_op jit(solution)/shard_map/ppermute | solution.py:26
  58.4 19.1 %collective-permute-start.5 = (bf16[896,128]{1,0:T(8,128)(2,1)S(1)}, bf16[896,128]{1,0:T(8,128)(2,1)S(1)}, u32[]{:S(2)}, u32[]{:S(2)}) collective-permute-start(bf16[896,128]{1,0:T(8,128)(2,1)S(1)} %get-tuple-element.32), channel_id=1, source_target_pairs={{0,96},{96,0},{32,64},{64,32},{1,97},{97,1},{33,65},{65,33},{2,98}... | collective-permute-start | bytes 688136 | tf_op jit(solution)/shard_map/ppermute | solution.py:26
  60.3 35.2 %collective-permute-start.6 = (bf16[896,128]{1,0:T(8,128)(2,1)S(1)}, bf16[896,128]{1,0:T(8,128)(2,1)S(1)}, u32[]{:S(2)}, u32[]{:S(2)}) collective-permute-start(bf16[896,128]{1,0:T(8,128)(2,1)S(1)} %get-tuple-element.33), channel_id=1, source_target_pairs={{0,64},{64,0},{32,96},{96,32},{1,65},{65,1},{33,97},{97,33},{2,66}... | collective-permute-start | bytes 688136 | tf_op jit(solution)/shard_map/ppermute | solution.py:26
  145.5 9.3 %copy-start.3 = (bf16[1,1,896,384]{3,2,1,0:T(8,128)(2,1)S(1)}, bf16[1,1,896,384]{3,2,1,0:T(8,128)(2,1)}, u32[]{:S(2)}) copy-start(bf16[1,1,896,384]{3,2,1,0:T(8,128)(2,1)} %param.11) | copy-start | bytes 2064388
  145.5 9.3 %copy-start.6 = (bf16[1,1,384,512]{3,2,1,0:T(8,128)(2,1)S(1)}, bf16[1,1,384,512]{3,2,1,0:T(8,128)(2,1)}, u32[]{:S(2)}) copy-start(bf16[1,1,384,512]{3,2,1,0:T(8,128)(2,1)} %param.9) | copy-start | bytes 1179652
  145.5 9.3 %copy-start.7 = (bf16[1,1,384,384]{3,2,1,0:T(8,128)(2,1)S(1)}, bf16[1,1,384,384]{3,2,1,0:T(8,128)(2,1)}, u32[]{:S(2)}) copy-start(bf16[1,1,384,384]{3,2,1,0:T(8,128)(2,1)} %param.10) | copy-start | bytes 884740
  146.2 11.5 %collective-permute-start.15 = (bf16[896,128]{1,0:T(8,128)(2,1)S(1)}, bf16[896,128]{1,0:T(8,128)(2,1)S(1)}, u32[]{:S(2)}, u32[]{:S(2)}) collective-permute-start(bf16[896,128]{1,0:T(8,128)(2,1)S(1)} %shard_map.96.own), channel_id=1, source_target_pairs={{0,64},{64,0},{32,96},{96,32},{1,65},{65,1},{33,97},{97,33},{2,66}... | collective-permute-start | bytes 688136 | tf_op jit(solution)/shard_map/ppermute | solution.py:26
  148.7 13.4 %collective-permute-start.14 = (bf16[896,128]{1,0:T(8,128)(2,1)S(1)}, bf16[896,128]{1,0:T(8,128)(2,1)S(1)}, u32[]{:S(2)}, u32[]{:S(2)}) collective-permute-start(bf16[896,128]{1,0:T(8,128)(2,1)S(1)} %shard_map.96.own), channel_id=1, source_target_pairs={{0,96},{96,0},{32,64},{64,32},{1,97},{97,1},{33,65},{65,33},{2,98}... | collective-permute-start | bytes 688136 | tf_op jit(solution)/shard_map/ppermute | solution.py:26
  151.9 11.9 %collective-permute-start.13 = (bf16[896,128]{1,0:T(8,128)(2,1)S(1)}, bf16[896,128]{1,0:T(8,128)(2,1)S(1)}, u32[]{:S(2)}, u32[]{:S(2)}) collective-permute-start(bf16[896,128]{1,0:T(8,128)(2,1)S(1)} %shard_map.96.own), channel_id=1, source_target_pairs={{0,32},{32,0},{64,96},{96,64},{1,33},{33,1},{65,97},{97,65},{2,34}... | collective-permute-start | bytes 688136 | tf_op jit(solution)/shard_map/ppermute | solution.py:26
